TPU v7x, 128 devices: a whole 4x4x4 slice. The times are simulated.
128 devices in a mesh: row: 16 (over y, z), col: 8 (over x, core).
Axes of the slice: x: 4, y: 4, z: 4, core: 2. Of those that a mesh axis runs over, the one named last changes fastest.
Arguments:
- current_image: float32 [16, 2048, 2048], P(None, 'row', 'col'), may hold values from -6 to 6
- measured: float32 [16, 16, 16, 128], P('col', 'row'), may hold values from -6 to 6
- ray_weight: float32 [16, 16, 128], P('col', 'row'), may hold values from 0.25 to 4
- angle_ids: int32 [16], replicated, may hold values from 0 to 255, as said below
- shadow_start: int32 [16, 16, 16], replicated, may hold values from 0 to 1920, as said below
Outputs:
- smoothed_image: float32 [16, 2048, 2048], P(None, 'row', 'col')
Inputs may be any that keep to these rules, and one draw needn't show every extreme that they name: `angle_ids`: distinct angle numbers. `shadow_start`: the shadow of a tile covers the 128 detector bins from this bin on, so it touches one or two detector blocks.
All inputs are finite; a program needn't handle non-finite values.
Results may differ from a plain program's by a relative error of at most 0.0033.
Values may be sent and summed in bfloat16 or wider, within the bound.
No kernel may reach another device: no remote copies, remote signals or barrier semaphores. Data moves between devices by JAX's collectives and lax.ppermute only.
A program may use at most 64 MiB of HBM per device.

v0:
```python
import math

import jax
import jax.numpy as jnp
from jax import lax
from jax.sharding import PartitionSpec as P

TILE = 128
ANGLES = 16
ALL_ANGLES = 256
TV_STEPS = 4


inverse_root = 0.7071067811865476
proj_scale = 0.03125
relaxation = 8.0
smoothing = 0.25
descent_step = 0.05


def with_halo(value, sides, width):
    for axis, dim in sides:
        peers, length = (lax.axis_size(axis), value.shape[dim])
        up = [(i, (i + 1) % peers) for i in range(peers - 1)]
        down = [(j, i) for i, j in up]
        last = lax.slice_in_dim(value, length - width, length, axis=dim)
        initial = lax.slice_in_dim(value, 0, width, axis=dim)
        before = lax.ppermute(last, axis, up)
        after = lax.ppermute(initial, axis, down)
        value = jnp.concatenate([before, value, after], axis=dim)
    return value


def cut_along(value, dim, peers):
    before, after = (value.shape[:dim], value.shape[dim + 1 :])
    return jnp.moveaxis(value.reshape(*before, peers, -1, *after), dim, 0)


def sum_at_owner(value, axis, dim):
    parts = cut_along(value, dim, lax.axis_size(axis))
    arrived = lax.all_to_all(parts, axis, split_axis=0, concat_axis=0, tiled=True)
    return arrived.sum(axis=0)


def tile_weights(angle_number):
    radians = angle_number.astype(jnp.float32) * (math.pi / ALL_ANGLES)
    cosine = jnp.cos(radians)
    sine_value = jnp.sin(radians)
    centre = (TILE - 1) / 2.0
    position = jnp.arange(TILE, dtype=jnp.float32) - centre
    along_bins = (
        TILE / 2.0 + (position[:, None] * cosine + position[None, :] * sine_value) * inverse_root
    )
    centres = jnp.arange(TILE, dtype=jnp.float32) + 0.5
    hat_values = jnp.maximum(0.0, 1.0 - jnp.abs(along_bins.reshape(-1, 1) - centres[None, :]))
    return (hat_values * proj_scale).astype(jnp.bfloat16)


def ramp(offset):
    is_odd = offset % 2 != 0
    nonzero = jnp.where(offset == 0, 1, offset).astype(jnp.float32)
    values = jnp.where(is_odd, -1.0 / (math.pi * math.pi * nonzero * nonzero), 0.0)
    values = jnp.where(offset == 0, 0.25, values)
    return jnp.where(jnp.abs(offset) < TILE, values, 0.0)


def tv_gradient(padded):
    corner = padded[:, :-1, :-1]
    step_down = padded[:, 1:, :-1] - corner
    step_right = padded[:, :-1, 1:] - corner
    magnitude = jnp.sqrt(smoothing * smoothing + step_down * step_down + step_right * step_right)
    flow_down = step_down / magnitude
    flow_right = step_right / magnitude
    return (
        flow_down[:, :-1, 1:]
        - flow_down[:, 1:, 1:]
        + flow_right[:, 1:, :-1]
        - flow_right[:, 1:, 1:]
    )


def selector(offsets, kind):
    wide = jnp.arange(2 * TILE, dtype=jnp.int32)
    narrow = jnp.arange(TILE, dtype=jnp.int32)
    return (
        wide[None, :, None] == offsets.reshape(-1)[:, None, None] + narrow[None, None, :]
    ).astype(kind)


def place(partial_value, offsets):
    chooser = selector(offsets, jnp.float32)
    return jnp.einsum(
        "bsm,bkm->bsk",
        partial_value,
        chooser,
        precision=lax.Precision.HIGHEST,
        preferred_element_type=jnp.float32,
    )


def window(two_blocks, offsets):
    leading = offsets.shape
    inner = two_blocks.shape[len(leading) :]
    flat = two_blocks.reshape((-1,) + inner)
    chooser = selector(offsets, jnp.bfloat16)
    picked = jnp.einsum("bsk,bkm->bsm", flat, chooser, preferred_element_type=jnp.float32)
    return picked.astype(jnp.bfloat16).reshape(leading + inner[:-1] + (TILE,))


def pick_rows(table, first_rows, second_rows):
    leading = first_rows.shape
    total = table.shape[0]
    indices = jnp.stack([first_rows, second_rows], axis=-1).reshape(-1)
    onehot = (indices[:, None] == jnp.arange(total, dtype=jnp.int32)[None, :]).astype(jnp.bfloat16)
    picked = jnp.dot(onehot, table.reshape(total, -1), preferred_element_type=jnp.float32).astype(
        jnp.bfloat16
    )
    picked = picked.reshape(leading + (2,) + table.shape[1:])
    picked = jnp.moveaxis(picked, -3, -2)
    return picked.reshape(leading + table.shape[1:-1] + (2 * table.shape[-1],))


def smooth_deep(current, row_index, col_index, row_count, col_count):
    rows_here = current.shape[1]
    cols_here = current.shape[2]
    extended = with_halo(current, (("row", 1), ("col", 2)), TV_STEPS)
    for repeat in range(TV_STEPS):
        margin = TV_STEPS - repeat - 1
        inner = extended[:, 1:-1, 1:-1] - descent_step * tv_gradient(extended)
        row_place = (
            row_index * rows_here - margin + jnp.arange(rows_here + 2 * margin, dtype=jnp.int32)
        )
        col_place = (
            col_index * cols_here - margin + jnp.arange(cols_here + 2 * margin, dtype=jnp.int32)
        )
        row_inside = (row_place >= 0) & (row_place < rows_here * row_count)
        col_inside = (col_place >= 0) & (col_place < cols_here * col_count)
        inside = row_inside[:, None] & col_inside[None, :]
        extended = jnp.where(inside[None], inner, jnp.float32(0.0))
    return extended


def local(current_image, measured, ray_weight, angle_ids, shadow_start):
    row_index = lax.axis_index("row")
    col_index = lax.axis_index("col")
    row_count = lax.axis_size("row")
    col_count = lax.axis_size("col")
    slices = current_image.shape[0]
    local_width = current_image.shape[2]
    across = local_width // TILE
    angles_here = ANGLES // col_count
    tile_data = current_image.astype(jnp.bfloat16).reshape(slices, TILE, across, TILE)
    tile_data = tile_data.transpose(2, 0, 1, 3).reshape(across * slices, TILE * TILE)
    row_starts = shadow_start[row_index]
    own_starts = lax.dynamic_slice_in_dim(row_starts, col_index * across, across, 0)

    def forward(unused, angle_index):
        weights = tile_weights(angle_ids[angle_index])
        partial_value = jnp.dot(tile_data, weights, preferred_element_type=jnp.float32).reshape(
            across, slices, TILE
        )
        placed = place(partial_value, own_starts[:, angle_index] % TILE)
        return (unused, placed)

    unused, entries = lax.scan(forward, jnp.int32(0), jnp.arange(ANGLES, dtype=jnp.int32))
    entries = entries.reshape(ANGLES, across, slices, 2, TILE).transpose(0, 1, 3, 2, 4)
    pair_index = jnp.arange(2, dtype=jnp.int32)
    outgoing = entries.reshape(col_count, angles_here, across, 2, slices, TILE)
    incoming = lax.all_to_all(outgoing, "col", split_axis=0, concat_axis=0, tiled=True)
    theirs = lax.dynamic_slice_in_dim(row_starts, col_index * angles_here, angles_here, 1)
    theirs = (theirs.reshape(col_count, across, angles_here) // TILE).transpose(0, 2, 1)
    blocks = theirs[:, :, :, None] + pair_index[None, None, None, :]
    target = blocks * angles_here + jnp.arange(angles_here, dtype=jnp.int32)[None, :, None, None]
    targets_all = jnp.arange(row_count * angles_here, dtype=jnp.int32)
    onehot = (targets_all[:, None] == target.reshape(1, -1)).astype(jnp.float32)
    dense_sums = jnp.dot(
        onehot,
        incoming.reshape(-1, slices * TILE),
        precision=lax.Precision.HIGHEST,
        preferred_element_type=jnp.float32,
    )
    ray_sums = sum_at_owner(dense_sums, "row", 0)
    ray_sums = ray_sums.reshape(angles_here, 1, slices, TILE)
    residual = ray_weight[:, :, None, :] * (measured - ray_sums)
    padded = with_halo(residual, (("row", 1),), 1)
    in_bins = jnp.arange(TILE, dtype=jnp.int32)
    filtered = jnp.zeros((angles_here * slices, TILE), jnp.float32)
    for neighbour in (-1, 0, 1):
        ramp_block = ramp(in_bins[None, :] - in_bins[:, None] - neighbour * TILE)
        filtered = filtered + jnp.dot(
            padded[:, 1 + neighbour].reshape(-1, TILE),
            ramp_block,
            precision=lax.Precision.HIGHEST,
            preferred_element_type=jnp.float32,
        )
    filtered = filtered.astype(jnp.bfloat16).reshape(angles_here, slices, TILE)
    sinogram = lax.all_gather(filtered, ("row", "col"), axis=0, tiled=True)
    blocks = own_starts.T // TILE
    angle_rows = jnp.arange(ANGLES, dtype=jnp.int32)[:, None]
    first_rows = blocks * ANGLES + angle_rows
    second = jnp.minimum(blocks + 1, row_count - 1) * ANGLES + angle_rows
    two_blocks = pick_rows(sinogram, first_rows, second)
    shadows = window(two_blocks, own_starts.T % TILE)

    def backward(running, angle_index):
        weights = tile_weights(angle_ids[angle_index])
        shadow_piece = shadows[angle_index].reshape(across * slices, TILE)
        running = running + lax.dot_general(
            shadow_piece, weights, (((1,), (1,)), ((), ())), preferred_element_type=jnp.float32
        )
        return (running, None)

    update, unused = lax.scan(
        backward,
        jnp.zeros((across * slices, TILE * TILE), jnp.float32),
        jnp.arange(ANGLES, dtype=jnp.int32),
    )
    update = (
        update.reshape(across, slices, TILE, TILE)
        .transpose(1, 2, 0, 3)
        .reshape(slices, TILE, local_width)
    )
    current = current_image + relaxation * update
    current = smooth_deep(current, row_index, col_index, row_count, col_count)
    return current


def solution(mesh):
    return jax.shard_map(
        local,
        mesh=mesh,
        in_specs=(
            P(None, "row", "col"),
            P("col", "row", None, None),
            P("col", "row", None),
            P(),
            P(),
        ),
        out_specs=P(None, "row", "col"),
        check_vma=False,
    )
```

profile of v0, /device:TPU:9, one launch (start us, length us, event | category | flops | bytes accessed | tf_op | source)
XLA Modules:
  0.0 398.0 jit_solution(17073874723149607515)
XLA Ops:
  7.3 1.8 copy_bitcast_fusion.2
  9.9 106.5 %while.25 = (s32[]{:T(128)}, f32[16,2,16,256]{3,2,1,0:T(8,128)S(1)}, s32[16]{0:T(128)S(1)}, s32[16]{0:T(128)S(1)}, bf16[32,16384]{1,0:T(8,128)(2,1)S(1)}, /*inde...) while((s32[]{:T(128)}, f32[16,2,16,256]{3,2,1,0:T(8,128)S(1)}, s32[16]{0:T(128)S(1)}, ...), condition=%wide.region_1.2_spmd, body=%wide.region_0.1_spmd.sunk | while | flops 159499024 | bytes 1250539 | solution.py:165
  13.9 2.4 fusion.178
  20.5 2.4 fusion.178
  27.2 2.4 fusion.178
  33.9 2.4 fusion.178
  40.5 2.4 fusion.178
  47.2 2.4 fusion.178
  53.8 2.4 fusion.178
  60.5 2.4 fusion.178
  67.2 2.4 fusion.178
  73.8 2.4 fusion.178
  80.5 2.4 fusion.178
  87.1 2.4 fusion.178
  93.8 2.4 fusion.178
  100.5 2.4 fusion.178
  107.1 2.4 fusion.178
  113.8 2.4 fusion.178
  117.6 5.0 %all-to-all-start = ((f32[8,2,2,2,16,128]{5,4,3,2,1,0:T(8,128)}), f32[8,2,2,2,16,128]{5,4,3,2,1,0:T(8,128)S(1)}, u32[]{:S(2)}, u32[]{:S(2)}) async-start(f32[8,2,2,2,16,128]{5,4,3,2,1,0:T(8,128)} %bitcast.18), calls=%async_computation | async-start | bytes 1048576 | tf_op jit(solution)/shard_map/all_to_all | solution.py:169
  123.7 8.2 %all-to-all-done = f32[8,2,2,2,16,128]{5,4,3,2,1,0:T(8,128)S(1)} async-done(((f32[8,2,2,2,16,128]{5,4,3,2,1,0:T(8,128)}), f32[8,2,2,2,16,128]{5,4,3,2,1,0:T(8,128)S(1)}, u32[]{:S(2)}, u32[]{:S(2)}) %all-to-all-start) | async-done | bytes 524320 | tf_op jit(solution)/shard_map/all_to_all | solution.py:169
  133.2 7.8 %all-to-all-start.1 = ((f32[16,2,2048]{2,1,0:T(2,128)}), f32[16,2,2048]{2,1,0:T(2,128)S(1)}, u32[]{:S(2)}, u32[]{:S(2)}) async-start(f32[16,2,2048]{2,1,0:T(2,128)} %copy.42), calls=%async_computation.1 | async-start | bytes 524288 | tf_op jit(solution)/shard_map/all_to_all | solution.py:41
  141.1 6.1 %all-to-all-done.1 = f32[16,2,2048]{2,1,0:T(2,128)S(1)} async-done(((f32[16,2,2048]{2,1,0:T(2,128)}), f32[16,2,2048]{2,1,0:T(2,128)S(1)}, u32[]{:S(2)}, u32[]{:S(2)}) %all-to-all-start.1) | async-done | bytes 262176 | tf_op jit(solution)/shard_map/all_to_all | solution.py:41
  147.3 3.8 collective-permute-start.1
  151.1 2.1 collective-permute-start
  153.7 4.0 %collective-permute-done = f32[2,1,16,128]{3,2,1,0:T(8,128)S(1)} collective-permute-done((f32[2,1,16,128]{3,2,1,0:T(8,128)S(1)}, f32[2,1,16,128]{3,2,1,0:T(8,128)S(1)}, u32[]{:S(2)}, u32[]{:S(2)}) %collective-permute-start) | collective-permute-done | bytes 16416 | tf_op jit(solution)/shard_map/ppermute | solution.py:28
  160.2 59.9 %all-gather.2.cloned.1.call-done = bf16[256,16,128]{2,1,0:T(8,128)(2,1)} async-done(((bf16[2,16,128]{2,1,0:T(8,128)(2,1)}), bf16[256,16,128]{2,1,0:T(8,128)(2,1)}) %all-gather.2.cloned.1.call-update) | async-done | bytes 1048592 | tf_op jit(solution)/shard_map/all_gather | solution.py:197
  220.1 1.6 fusion.41
  222.9 107.3 %while.26 = (s32[]{:T(128)}, f32[32,16384]{1,0:T(8,128)S(1)}, s32[16]{0:T(128)S(1)}, bf16[16,2,16,128]{3,2,1,0:T(8,128)(2,1)S(1)}, s32[16]{0:T(128)S(1)}, /*index=5*/s32[]{:T(128)}, s32[]{:T(128)}, s32[]{:T(128)}, f32[1]{0:T(128)}) while((s32[]{:T(128)}, f32[32,16384]{1,0:T(8,128)S(1)}, s32[16]{0:T(128)S(1)}, ...), condition=%wide.region_4.5_spmd.clone, body=%wide.region_3.4_spmd.clone.sunk | while | flops 147898880 | bytes 4353233 | solution.py:213
  227.0 2.6 convolution_add_fusion.3
  233.7 2.6 convolution_add_fusion.3
  240.4 2.6 convolution_add_fusion.3
  247.1 2.6 convolution_add_fusion.3
  253.8 2.6 convolution_add_fusion.3
  260.5 2.6 convolution_add_fusion.3
  267.2 2.6 convolution_add_fusion.3
  273.9 2.6 convolution_add_fusion.3
  280.6 2.6 convolution_add_fusion.3
  287.3 2.6 convolution_add_fusion.3
  294.0 2.6 convolution_add_fusion.3
  300.7 2.6 convolution_add_fusion.3
  307.4 2.6 convolution_add_fusion.3
  314.1 2.6 convolution_add_fusion.3
  320.8 2.6 convolution_add_fusion.3
  327.6 2.6 convolution_add_fusion.3
  330.7 1.6 copy.68
  332.3 2.7 mul.248
  335.0 3.5 copy_add_fusion
  338.6 2.3 collective-permute-start.2
  340.8 5.1 %collective-permute-start.3 = (f32[16,4,256]{2,0,1:T(8,128)S(1)}, f32[16,4,256]{2,0,1:T(8,128)S(1)}, u32[]{:S(2)}, u32[]{:S(2)}) collective-permute-start(f32[16,4,256]{2,0,1:T(8,128)S(1)} %get-tuple-element.232), channel_id=1, source_target_pairs={{8,0},{16,8},{24,16},{32,24},{40,32},{48,40},{56,48},{64,56},{72,6... | collective-permute-start | bytes 196616 | tf_op jit(solution)/shard_map/ppermute | solution.py:29
  348.8 2.5 copy.47
  351.3 3.6 collective-permute-start.4
  356.2 2.1 collective-permute-start.5
  359.9 2.2 collective-permute-done.5
  362.1 2.3 copy.50
  364.4 2.5 pad_maximum_fusion
  366.9 2.1 fusion.21
  369.0 3.8 fusion.24
  372.8 2.1 fusion.26
  374.9 3.8 fusion.29
  378.7 1.8 fusion.31
  380.6 4.0 fusion.34
  384.6 1.8 fusion.36
  386.4 2.3 fusion.39
  388.7 2.5 copy.51
  (291 shorter events, 61.6 us)
Async XLA Ops:
  6.5 3.4 copy-start.2
  116.4 30.8 %copy-start = (f32[2,1,16,128]{3,2,1,0:T(8,128)S(1)}, f32[2,1,16,128]{3,2,1,0:T(8,128)}, u32[]{:S(2)}) copy-start(f32[2,1,16,128]{3,2,1,0:T(8,128)} %param.10) | copy-start | bytes 49156
  116.5 30.8 %copy-start.1 = (f32[2,1,128]{2,1,0:T(1,128)S(1)}, f32[2,1,128]{2,1,0:T(1,128)}, u32[]{:S(2)}) copy-start(f32[2,1,128]{2,1,0:T(1,128)} %param.11) | copy-start | bytes 3076
  117.6 14.3 %all-to-all-start = ((f32[8,2,2,2,16,128]{5,4,3,2,1,0:T(8,128)}), f32[8,2,2,2,16,128]{5,4,3,2,1,0:T(8,128)S(1)}, u32[]{:S(2)}, u32[]{:S(2)}) async-start(f32[8,2,2,2,16,128]{5,4,3,2,1,0:T(8,128)} %bitcast.18), calls=%async_computation | async-start | bytes 1048576 | tf_op jit(solution)/shard_map/all_to_all | solution.py:169
  133.2 14.0 %all-to-all-start.1 = ((f32[16,2,2048]{2,1,0:T(2,128)}), f32[16,2,2048]{2,1,0:T(2,128)S(1)}, u32[]{:S(2)}, u32[]{:S(2)}) async-start(f32[16,2,2048]{2,1,0:T(2,128)} %copy.42), calls=%async_computation.1 | async-start | bytes 524288 | tf_op jit(solution)/shard_map/all_to_all | solution.py:41
  141.1 79.0 %all-gather.2.cloned.1.call-start = ((), (), s32[]{:S(2)}) async-start(), calls=%async_computation.2 | async-start | bytes 1056768 | tf_op jit(solution)/shard_map/all_gather | solution.py:197
  147.3 6.2 %collective-permute-start.1 = (f32[2,1,16,128]{3,2,1,0:T(8,128)S(1)}, f32[2,1,16,128]{3,2,1,0:T(8,128)S(1)}, u32[]{:S(2)}, u32[]{:S(2)}) collective-permute-start(f32[2,1,16,128]{3,2,1,0:T(8,128)S(1)} %fusion.115), channel_id=1, source_target_pairs={{8,0},{16,8},{24,16},{32,24},{40,32},{48,40},{56,48},{64,56},{72,6... | collective-permute-start | bytes 49160 | tf_op jit(solution)/shard_map/ppermute | solution.py:29
  151.1 6.6 %collective-permute-start = (f32[2,1,16,128]{3,2,1,0:T(8,128)S(1)}, f32[2,1,16,128]{3,2,1,0:T(8,128)S(1)}, u32[]{:S(2)}, u32[]{:S(2)}) collective-permute-start(f32[2,1,16,128]{3,2,1,0:T(8,128)S(1)} %fusion.115), channel_id=1, source_target_pairs={{0,8},{8,16},{16,24},{24,32},{32,40},{40,48},{48,56},{56,64},{64,7... | collective-permute-start | bytes 49160 | tf_op jit(solution)/shard_map/ppermute | solution.py:28
  338.6 7.4 %collective-permute-start.2 = (f32[16,4,256]{2,0,1:T(8,128)S(1)}, f32[16,4,256]{2,0,1:T(8,128)S(1)}, u32[]{:S(2)}, u32[]{:S(2)}) collective-permute-start(f32[16,4,256]{2,0,1:T(8,128)S(1)} %get-tuple-element.231), channel_id=1, source_target_pairs={{0,8},{8,16},{16,24},{24,32},{32,40},{40,48},{48,56},{56,64},{64,7... | collective-permute-start | bytes 196616 | tf_op jit(solution)/shard_map/ppermute | solution.py:28
  340.8 6.4 %collective-permute-start.3 = (f32[16,4,256]{2,0,1:T(8,128)S(1)}, f32[16,4,256]{2,0,1:T(8,128)S(1)}, u32[]{:S(2)}, u32[]{:S(2)}) collective-permute-start(f32[16,4,256]{2,0,1:T(8,128)S(1)} %get-tuple-element.232), channel_id=1, source_target_pairs={{8,0},{16,8},{24,16},{32,24},{40,32},{48,40},{56,48},{64,56},{72,6... | collective-permute-start | bytes 196616 | tf_op jit(solution)/shard_map/ppermute | solution.py:29
  351.3 7.1 %collective-permute-start.4 = (f32[16,136,4]{1,0,2:T(8,128)}, f32[16,136,4]{1,0,2:T(8,128)}, u32[]{:S(2)}, u32[]{:S(2)}) collective-permute-start(f32[16,136,4]{1,0,2:T(8,128)} %copy.47), channel_id=1, source_target_pairs={{0,1},{1,2},{2,3},{3,4},{4,5},{5,6},{6,7},{8,9},{9,10},{10,11},{11... | collective-permute-start | bytes 104456 | tf_op jit(solution)/shard_map/ppermute | solution.py:28
  356.2 5.9 %collective-permute-start.5 = (f32[16,136,4]{1,0,2:T(8,128)}, f32[16,136,4]{1,0,2:T(8,128)}, u32[]{:S(2)}, u32[]{:S(2)}) collective-permute-start(f32[16,136,4]{1,0,2:T(8,128)} %copy.48), channel_id=1, source_target_pairs={{1,0},{2,1},{3,2},{4,3},{5,4},{6,5},{7,6},{9,8},{10,9},{11,10},{12... | collective-permute-start | bytes 104456 | tf_op jit(solution)/shard_map/ppermute | solution.py:29
Sparse Core Ops, SparseCore 0:
  158.7 61.3 all-gather.1
where the time goes:
time: 401 us; the launch traced here: 398 us
  loops' own time  88 us (22%)
  matrix products  87 us (22%)
  waiting for transfers between devices  81.8 us (20%)
  local copies, waits for them, and re-layouts  59.8 us (15%)
  other arithmetic  35.9 us (9%)
  starting transfers between devices  31.8 us (8%)
  between operations  13.9 us (3%)
    all_gather x1, waiting for transfers between devices, local(): sinogram = lax.all_gather(filtered, ('row', 'col'), axis=0, tiled=True)  59.9 us
    another operation x1, loops' own time, local(): lax.scan(backward, jnp.zeros((across * slices, TILE * TILE), jnp.float32)...  44.8 us
    another operation x1, loops' own time, local(): lax.scan(forward, jnp.int32(0), jnp.arange(ANGLES, dtype=jnp.int32))  43.2 us
    dot_general x16, matrix products, backward(): lax.dot_general(shadow_piece, weights, (((1,), (1,)), ((), ())), preferre...  42 us
    dot_general x16, matrix products, forward(): jnp.dot(tile_data, weights, preferred_element_type=jnp.float32)  37.6 us
    dynamic_slice x32, local copies, waits for them, and re-layouts, local(): lax.scan(forward, jnp.int32(0), jnp.arange(ANGLES, dtype=jnp.int32))  19.1 us
    select_n x4, other arithmetic, smooth_deep(): extended = jnp.where(inside[None], inner, jnp.float32(0.0))  13.9 us
    ppermute x3, starting transfers between devices, with_halo(): after = lax.ppermute(initial, axis, down)  11.1 us
  transfers between devices with their start and end apart: 9, of which 6 were waited for; matrix products, arithmetic and copies ran while one was open for 1% of the time, Pallas kernels for 0%

commit v1 on v0

v1 whole, which is shorter than its diff:
```python
import functools
import math

import jax
import jax.numpy as jnp
from jax import lax
from jax.experimental import pallas as pl
from jax.experimental.pallas import tpu as pltpu
from jax.sharding import PartitionSpec as P

TILE = 128
ANGLES = 16
ALL_ANGLES = 256
TV_STEPS = 4
SIDE = 16
PATCHES = TILE // SIDE
PIX = SIDE * SIDE
BINS = 24
ROWS = 32
BAND = ANGLES * BINS

inverse_root = 0.7071067811865476
smoothing = 0.25
descent_step = 0.05

VMEM = pltpu.VMEM
F32 = jnp.float32
BF16 = jnp.bfloat16


def geometry(angle_ids):
    radians = angle_ids.astype(F32) * (math.pi / ALL_ANGLES)
    cosine = jnp.cos(radians) * inverse_root
    sine = jnp.sin(radians) * inverse_root
    first = jnp.arange(PATCHES, dtype=F32) * SIDE - (TILE - 1) / 2.0
    corner = TILE / 2.0 + first[:, None, None] * cosine + first[None, :, None] * sine
    corner = corner.reshape(PATCHES * PATCHES, ANGLES)
    low = corner + (SIDE - 1) * (jnp.minimum(cosine, 0.0) + jnp.minimum(sine, 0.0))
    first_bin = jnp.floor(low - 1.5).astype(jnp.int32) + 1
    base = jnp.clip((first_bin >> 3) << 3, 0, TILE - BINS)
    delta = corner - base.astype(F32) - 0.5
    return cosine, sine, base, delta


def forward_kernel(
    base_ref, delta_ref, cs_ref, image0_ref, image1_ref, out_ref, xt, rel, band0, band1, sums
):
    slices = ROWS // 2
    lane = lax.broadcasted_iota(jnp.int32, (BINS, PIX), 1)
    bin_at = lax.broadcasted_iota(jnp.int32, (BINS, PIX), 0).astype(F32)
    down = (lane // SIDE).astype(F32)
    across = (lane % SIDE).astype(F32)
    for a in range(ANGLES):
        rel[a * BINS : (a + 1) * BINS, :] = down * cs_ref[0, a] + across * cs_ref[1, a] - bin_at
    sums[...] = jnp.zeros_like(sums)

    def flip(u, carry):
        both = [ref[pl.ds(u, slices, stride=TILE), :] for ref in (image0_ref, image1_ref)]
        stacked = jnp.concatenate(both, axis=0)
        xt[pl.ds(pl.multiple_of(u * TILE, TILE), TILE), :] = stacked.T.astype(BF16)
        return carry

    lax.fori_loop(0, TILE, flip, 0, unroll=4)

    def build(patch, band):
        for a in range(0, ANGLES, 2):
            pair = []
            for b in (a, a + 1):
                away = jnp.abs(rel[b * BINS : (b + 1) * BINS, :] + delta_ref[patch * ANGLES + b])
                pair.append(jnp.maximum(0.0, 1.0 - away))
            band[a * BINS : (a + 2) * BINS, :] = jnp.concatenate(pair, axis=0).astype(BF16)

    def project(patch, band):
        row = patch // PATCHES
        col = patch % PATCHES
        pieces = []
        for u in range(SIDE):
            start = pl.multiple_of((row * SIDE + u) * TILE + col * SIDE, SIDE)
            pieces.append(xt[pl.ds(start, SIDE), :])
        pixels = jnp.concatenate(pieces, axis=0)
        got = jnp.dot(band[...], pixels, preferred_element_type=F32)
        for a in range(ANGLES):
            start = pl.multiple_of(base_ref[patch * ANGLES + a], 8)
            sums[a, pl.ds(start, BINS), :] += got[a * BINS : (a + 1) * BINS, :]

    build(0, band0)

    def step(i, carry):
        build(2 * i + 1, band1)
        project(2 * i, band0)
        build(jnp.minimum(2 * i + 2, PATCHES * PATCHES - 1), band0)
        project(2 * i + 1, band1)
        return carry

    lax.fori_loop(0, PATCHES * PATCHES // 2, step, 0)
    for a in range(ANGLES):
        turned = sums[a].T * 0.03125
        for t in range(2):
            row = (a // 2) * 4 + t * 2 + a % 2
            out_ref[pl.ds(row, slices, stride=ROWS), :] = turned[t * slices : (t + 1) * slices, :]


def owner_kernel(starts_ref, own_ref, got_ref, given_ref, out_ref, low, high, wide, filt, staged):
    blocks = 16
    groups = got_ref.shape[0] // 8
    low[...] = jnp.zeros_like(low)
    high[...] = jnp.zeros_like(high)
    lane = lax.broadcasted_iota(jnp.int32, (8, TILE), 1)
    sub = lax.broadcasted_iota(jnp.int32, (8, TILE), 0)
    first = own_ref[0] * 2

    def where_of(g, k):
        tile = g * 4 + (k // 4) * 2 + (k // 2) % 2
        start = starts_ref[tile * ANGLES + first + k % 2]
        return start >> 7, start & (TILE - 1)

    def add(g, carry):
        rows = got_ref[pl.ds(pl.multiple_of(g * 8, 8), 8), :]
        for k in range(8):
            block, shift = where_of(g, k)
            turned = jnp.where(sub == k, pltpu.roll(rows, shift, 1), 0.0)
            tail = lane >= shift
            low[block] += jnp.where(tail, turned, 0.0)
            high[block] += jnp.where(tail, 0.0, turned)
        return carry

    lax.fori_loop(0, groups, add, 0)
    wide[...] = jnp.zeros_like(wide)
    for h in range(2):
        for b in range(blocks):
            total = low[b]
            if b:
                total = total + high[b - 1]
            total = jnp.sum(jnp.where(sub % 2 == h, total, 0.0), axis=0, keepdims=True)
            meas = given_ref[b * 4 + h : b * 4 + h + 1, :]
            weight = given_ref[b * 4 + 2 + h : b * 4 + 3 + h, :]
            wide[h * blocks + b : h * blocks + b + 1, TILE : 2 * TILE] = weight * (meas - total)
    centre = wide[:, TILE : 2 * TILE]
    at = lax.broadcasted_iota(jnp.int32, (2 * blocks, TILE), 0) % blocks
    wide[:, :TILE] = jnp.where(at == 0, 0.0, pltpu.roll(centre, 1, 0))
    wide[:, 2 * TILE :] = jnp.where(at == blocks - 1, 0.0, pltpu.roll(centre, 2 * blocks - 1, 0))
    offset = (
        lax.broadcasted_iota(jnp.int32, (3 * TILE, TILE), 1)
        + TILE
        - lax.broadcasted_iota(jnp.int32, (3 * TILE, TILE), 0)
    )
    nonzero = jnp.where(offset == 0, 1, offset).astype(F32)
    ramp = jnp.where((offset & 1) == 1, -1.0 / (math.pi * math.pi * nonzero * nonzero), 0.0)
    ramp = jnp.where(offset == 0, 0.25, ramp)
    ramp = jnp.where(jnp.abs(offset) < TILE, ramp, 0.0)
    done = jnp.dot(wide[...], ramp, precision=lax.Precision.HIGHEST, preferred_element_type=F32)
    wide[:, :TILE] = done.astype(BF16).astype(F32)
    filt[...] = jnp.zeros_like(filt)
    for h in range(2):
        for b in range(blocks):
            row = wide[h * blocks + b : h * blocks + b + 1, :TILE]
            filt[h, b] = jnp.broadcast_to(row, (8, TILE))

    def take(g, carry):
        rows = jnp.zeros((8, TILE), F32)
        for k in range(8):
            block, shift = where_of(g, k)
            mixed = jnp.where(lane >= shift, filt[k % 2, block], filt[k % 2, block + 1])
            rows = jnp.where(sub == k, pltpu.roll(mixed, (TILE - shift) & (TILE - 1), 1), rows)
        staged[pl.ds(pl.multiple_of(g * 8, 8), 8), :] = rows
        return carry

    lax.fori_loop(0, groups, take, 0)
    out_ref[...] = staged[...].astype(BF16)


def backward_kernel(
    base_ref, image0_ref, image1_ref, delta_ref, lanes_ref, got_ref, out_ref, left_ref, right_ref,
    rel, band0, band1, shadows, staged, update,
):
    slices = ROWS // 2
    pixel = lax.broadcasted_iota(jnp.int32, (PIX, BAND), 0)
    rel[...] = (
        (pixel // SIDE).astype(F32) * lanes_ref[0:1, :]
        + (pixel % SIDE).astype(F32) * lanes_ref[1:2, :]
    )
    staged[...] = got_ref[...].astype(F32)
    for a in range(ANGLES):
        parts = []
        for t in range(2):
            row = (a // 2) * 4 + t * 2 + a % 2
            parts.append(staged[pl.ds(row, slices, stride=ROWS), :])
        shadows[a] = jnp.concatenate(parts, axis=0).T

    def build(patch, band):
        shift = delta_ref[pl.ds(patch, 1), :]
        for r in range(0, PIX, 16):
            away = jnp.abs(rel[r : r + 16, :] + shift)
            band[r : r + 16, :] = jnp.maximum(0.0, 1.0 - away).astype(BF16)

    def spread(patch, band):
        row = patch // PATCHES
        col = patch % PATCHES
        pieces = []
        for a in range(ANGLES):
            start = pl.multiple_of(base_ref[patch * ANGLES + a], 8)
            pieces.append(shadows[a, pl.ds(start, BINS), :])
        seen = jnp.concatenate(pieces, axis=0).astype(BF16)
        got = jnp.dot(band[...], seen, preferred_element_type=F32)
        for u in range(SIDE):
            start = pl.multiple_of((row * SIDE + u) * TILE + col * SIDE, SIDE)
            update[pl.ds(start, SIDE), :] = got[u * SIDE : (u + 1) * SIDE, :]

    build(0, band0)

    def step(i, carry):
        build(2 * i + 1, band1)
        spread(2 * i, band0)
        build(jnp.minimum(2 * i + 2, PATCHES * PATCHES - 1), band0)
        spread(2 * i + 1, band1)
        return carry

    lax.fori_loop(0, PATCHES * PATCHES // 2, step, 0)

    lane = lax.broadcasted_iota(jnp.int32, (slices, TILE), 1)
    per = TILE // TV_STEPS

    def finish(g, carry):
        left = jnp.zeros((slices, TILE), F32)
        right = jnp.zeros((slices, TILE), F32)
        for j in range(per):
            u = g * per + j
            turned = update[pl.ds(pl.multiple_of(u * TILE, TILE), TILE), :].T
            for t in range(2):
                here = (image0_ref, image1_ref)[t][pl.ds(u, slices, stride=TILE), :]
                here = here + 0.25 * turned[t * slices : (t + 1) * slices, :]
                out_ref[u, :, t * TILE : (t + 1) * TILE] = here
                mine = (lane >= j * TV_STEPS) & (lane < (j + 1) * TV_STEPS)
                if t == 0:
                    left = jnp.where(mine, pltpu.roll(here, j * TV_STEPS, 1), left)
                else:
                    right = jnp.where(mine, pltpu.roll(here, (j + 1) * TV_STEPS % TILE, 1), right)
        left_ref[g] = left
        right_ref[g] = right
        return carry

    lax.fori_loop(0, TILE // per, finish, 0)


def smooth_kernel(
    place_ref, x_ref, above_ref, below_ref, before_ref, after_ref, out_ref, first, second,
    out0, out1, sems,
):
    slices = ROWS // 2
    high = TILE + 2 * TV_STEPS
    per = TILE // TV_STEPS
    lane = lax.broadcasted_iota(jnp.int32, (slices, TILE), 1)
    has_above, has_below, has_before, has_after = (place_ref[i] for i in range(4))
    keep = ((lane < TV_STEPS) & (has_after == 1)) | (
        (lane >= TILE - TV_STEPS) & (has_before == 1)
    )

    def margin(previous, following, j):
        following = pltpu.roll(following, (TILE - j * TV_STEPS) % TILE, 1)
        previous = pltpu.roll(previous, (TILE - (j + 1) * TV_STEPS) % TILE, 1)
        return jnp.where(keep, jnp.where(lane < TV_STEPS, following, previous), 0.0)

    for r in range(TV_STEPS):
        for ref, start, j in (
            (above_ref, 0, per - TV_STEPS + r),
            (below_ref, TILE + TV_STEPS, r),
        ):
            first[start + r, :, : 2 * TILE] = ref[r]
            first[start + r, :, 2 * TILE :] = margin(
                ref[TV_STEPS, :, :TILE], ref[TV_STEPS, :, TILE:], j
            )

    def load(g, carry):
        for j in range(per):
            u = g * per + j
            first[u + TV_STEPS, :, : 2 * TILE] = x_ref[u]
            first[u + TV_STEPS, :, 2 * TILE :] = margin(before_ref[g], after_ref[g], j)
        return carry

    lax.fori_loop(0, TILE // per, load, 0)

    def flows(here, under):
        down = under - here
        right = pltpu.roll(here, 3 * TILE - 1, 1) - here
        inverse = lax.rsqrt(smoothing * smoothing + down * down + right * right)
        return down * inverse, right * inverse

    edge = lax.broadcasted_iota(jnp.int32, (slices, 3 * TILE), 1)
    keep_all = (
        (edge < 2 * TILE)
        | ((edge < 2 * TILE + TV_STEPS) & (has_after == 1))
        | ((edge >= 3 * TILE - TV_STEPS) & (has_before == 1))
    )

    for k in range(TV_STEPS):
        source, target = (first, second) if k % 2 == 0 else (second, first)
        last = k == TV_STEPS - 1

        def row(r, carry, source=source, target=target, last=last):
            here, came = carry
            under = source[r + 1]
            down, right = flows(here, under)
            change = came - down + pltpu.roll(right, 1, 1) - right
            fresh = here - descent_step * change
            if last:
                out0[pl.ds(r - TV_STEPS, slices, stride=TILE), :] = fresh[:, :TILE]
                out1[pl.ds(r - TV_STEPS, slices, stride=TILE), :] = fresh[:, TILE : 2 * TILE]
            else:
                inside = ((r >= TV_STEPS) | (has_above == 1)) & (
                    (r < TILE + TV_STEPS) | (has_below == 1)
                )
                target[r] = jnp.where(keep_all & inside, fresh, 0.0)
            return under, down

        start = source[k]
        below = source[k + 1]
        came, unused = flows(start, below)
        lax.fori_loop(k + 1, high - k - 1, row, (below, came), unroll=2)
    copies = [
        pltpu.make_async_copy(ref, out_ref.at[:, pl.ds(t * TILE, TILE)], sems.at[t])
        for t, ref in enumerate((out0, out1))
    ]
    for copy in copies:
        copy.start()
    for copy in copies:
        copy.wait()


def call(kernel, scalars, arrays, outs, scratch, flops, halves=(), out_space=VMEM):
    smem = pl.BlockSpec(memory_space=pltpu.SMEM)
    vmem = pl.BlockSpec(memory_space=VMEM)
    specs = [smem] * len(scalars)
    operands = list(scalars)
    for half in halves:
        for t in range(2):
            specs.append(pl.BlockSpec((half.shape[0], TILE), lambda i, t=t: (0, t)))
            operands.append(half)
    specs += [vmem] * len(arrays)
    operands += arrays
    moved = sum(x.size * x.dtype.itemsize for x in (*arrays, *halves))
    return pl.pallas_call(
        kernel,
        grid=(1,),
        out_shape=outs,
        in_specs=specs,
        out_specs=jax.tree.map(lambda x: pl.BlockSpec(memory_space=out_space), outs),
        scratch_shapes=scratch,
        cost_estimate=pl.CostEstimate(flops=flops, bytes_accessed=moved, transcendentals=0),
    )(*operands)


def local(current_image, measured, ray_weight, angle_ids, shadow_start):
    row_index = lax.axis_index("row")
    col_index = lax.axis_index("col")
    rows = lax.axis_size("row")
    cols = lax.axis_size("col")
    slices = current_image.shape[0]
    both = ("row", "col")
    image = current_image.reshape(slices * TILE, 2 * TILE)
    cosine, sine, base, delta = geometry(angle_ids)
    base = base.reshape(-1)

    given = measured[:, 0].transpose(1, 0, 2)
    weight = jnp.broadcast_to(ray_weight[:, 0][None], given.shape)
    given = jnp.concatenate([given, weight], axis=1)
    given = lax.all_to_all(given, "row", split_axis=0, concat_axis=0, tiled=True)

    sent = call(
        forward_kernel,
        (base, delta.reshape(-1), jnp.stack([cosine, sine])),
        (),
        jax.ShapeDtypeStruct((rows * cols * 4, TILE), F32),
        [
            VMEM((TILE * TILE, ROWS), BF16),
            VMEM((BAND, PIX), F32),
            VMEM((BAND, PIX), BF16),
            VMEM((BAND, PIX), BF16),
            VMEM((ANGLES, TILE, ROWS), F32),
        ],
        30_000_000_000,
        halves=(image,),
    )
    got = lax.all_to_all(
        sent.reshape(rows * cols, 4, TILE), both, split_axis=0, concat_axis=0, tiled=True
    )
    blocks = rows
    out = call(
        owner_kernel,
        (shadow_start.reshape(-1), col_index.reshape(1)),
        (got.reshape(-1, TILE), given.reshape(-1, TILE)),
        jax.ShapeDtypeStruct((rows * cols * 4, TILE), BF16),
        [
            VMEM((blocks, 8, TILE), F32),
            VMEM((blocks, 8, TILE), F32),
            VMEM((2 * blocks, 3 * TILE), F32),
            VMEM((2, blocks + 1, 8, TILE), F32),
            VMEM((rows * cols * 4, TILE), F32),
        ],
        10_000_000_000,
    )
    shadows = lax.all_to_all(
        out.reshape(rows * cols, 4, TILE), both, split_axis=0, concat_axis=0, tiled=True
    )
    bins = jnp.arange(BINS, dtype=F32)
    delta_lanes = (delta[:, :, None] - bins).reshape(-1, BAND)
    angle_lanes = jnp.repeat(jnp.stack([cosine, sine]), BINS, axis=1)
    groups = TV_STEPS
    side = jax.ShapeDtypeStruct((groups, slices, TILE), F32)
    x, left, right = call(
        backward_kernel,
        (base,),
        (delta_lanes, angle_lanes, shadows.reshape(-1, TILE)),
        (jax.ShapeDtypeStruct((TILE, slices, 2 * TILE), F32), side, side),
        [
            VMEM((PIX, BAND), F32),
            VMEM((PIX, BAND), BF16),
            VMEM((PIX, BAND), BF16),
            VMEM((ANGLES, TILE, ROWS), F32),
            VMEM((rows * cols * 4, TILE), F32),
            VMEM((TILE * TILE, ROWS), F32),
        ],
        30_000_000_000,
        halves=(image,),
    )
    right_going = [(i, i + 1) for i in range(cols - 1)]
    left_going = [(i + 1, i) for i in range(cols - 1)]
    before = lax.ppermute(right, "col", right_going)
    after = lax.ppermute(left, "col", left_going)
    top = jnp.concatenate(
        [x[:TV_STEPS], jnp.concatenate([before[:1], after[:1]], axis=2)], axis=0
    )
    bottom = jnp.concatenate(
        [x[-TV_STEPS:], jnp.concatenate([before[-1:], after[-1:]], axis=2)], axis=0
    )
    above = lax.ppermute(bottom, "row", [(i, i + 1) for i in range(rows - 1)])
    below = lax.ppermute(top, "row", [(i + 1, i) for i in range(rows - 1)])
    place = jnp.stack(
        [row_index > 0, row_index < rows - 1, col_index > 0, col_index < cols - 1]
    ).astype(jnp.int32)
    wide = VMEM((TILE + 2 * TV_STEPS, slices, 3 * TILE), F32)
    half = VMEM((slices * TILE, TILE), F32)
    smooth = call(
        smooth_kernel,
        (place,),
        (x, above, below, before, after),
        jax.ShapeDtypeStruct((slices * TILE, 2 * TILE), F32),
        [wide, wide, half, half, pltpu.SemaphoreType.DMA((2,))],
        10_000_000_000,
        out_space=pl.ANY,
    )
    return smooth.reshape(current_image.shape)


def solution(mesh):
    return jax.shard_map(
        local,
        mesh=mesh,
        in_specs=(
            P(None, "row", "col"),
            P("col", "row", None, None),
            P("col", "row", None),
            P(),
            P(),
        ),
        out_specs=P(None, "row", "col"),
        check_vma=False,
    )
```

time: 401 us -> 164 us (0.41)
  Pallas kernels: 0 us -> 97.1 us
  loops' own time: 88 us -> 0 us
  matrix products: 87 us -> 0 us
  waiting for transfers between devices: 81.8 us -> 19.9 us
  local copies, waits for them, and re-layouts: 59.8 us -> 6.18 us
  other arithmetic: 35.9 us -> 4.6 us
  between operations: 13.9 us -> 0.16 us
    pallas_call x0 -> x4, Pallas kernels: none -> 97.1 us  [call(): pl.pallas_call(kernel, grid=(1,), out_shape=outs, in_specs=specs, out_spe...]
    another operation x2 -> x0, loops' own time: 88 us -> none  [the longest x1 44.8 us: local(): lax.scan(backward, jnp.zeros((across * slices, TILE * TILE), jnp.float32)...]
    dot_general x54 -> x0, matrix products: 87 us -> none  [the longest x16 42 us: backward(): lax.dot_general(shadow_piece, weights, (((1,), (1,)), ((), ())), preferre...]
    all_gather x1 -> x0, waiting for transfers between devices: 59.9 us -> none  [local(): sinogram = lax.all_gather(filtered, ('row', 'col'), axis=0, tiled=True)]
    dynamic_slice x82 -> x0, local copies, waits for them, and re-layouts: 39.6 us -> none  [the longest x32 19.1 us: local(): lax.scan(forward, jnp.int32(0), jnp.arange(ANGLES, dtype=jnp.int32))]
    select_n x20 -> x0, other arithmetic: 14.2 us -> none  [the longest x4 13.9 us: smooth_deep(): extended = jnp.where(inside[None], inner, jnp.float32(0.0))]
    all_to_all x2 -> x3, starting transfers between devices: 12.8 us -> 23.4 us  [the longest x1 10.1 us: local(): lax.all_to_all(sent.reshape(rows * cols, 4, TILE), both, split_axis=0, co...]
    div x4 -> x0, other arithmetic: 7.81 us -> none  [tv_gradient(): flow_down = step_down / magnitude]
  transfers between devices with their start and end apart: 9 -> 7, of which waited for: 6 -> 4; matrix products, arithmetic and copies ran while one was open for 1% -> 4% of each run, Pallas kernels for 0% -> 11%
where the time goes in v1:
time: 164 us; the launch traced here: 163 us
  Pallas kernels  97.1 us (59%)
  starting transfers between devices  35.2 us (21%)
  waiting for transfers between devices  19.9 us (12%)
  local copies, waits for them, and re-layouts  6.18 us (4%)
  other arithmetic  4.6 us (3%)
    pallas_call x4, Pallas kernels, call(): pl.pallas_call(kernel, grid=(1,), out_shape=outs, in_specs=specs, out_spe...  97.1 us
    all_to_all x1, starting transfers between devices, local(): lax.all_to_all(sent.reshape(rows * cols, 4, TILE), both, split_axis=0, co...  10.1 us
    all_to_all x1, waiting for transfers between devices, local(): lax.all_to_all(out.reshape(rows * cols, 4, TILE), both, split_axis=0, con...  8.32 us
    all_to_all x1, waiting for transfers between devices, local(): lax.all_to_all(sent.reshape(rows * cols, 4, TILE), both, split_axis=0, co...  8.14 us
    all_to_all x1, starting transfers between devices, local(): lax.all_to_all(given, 'row', split_axis=0, concat_axis=0, tiled=True)  7.85 us
    all_to_all x1, starting transfers between devices, local(): lax.all_to_all(out.reshape(rows * cols, 4, TILE), both, split_axis=0, con...  5.49 us
    ppermute x1, starting transfers between devices, local(): below = lax.ppermute(top, 'row', [(i + 1, i) for i in range(rows - 1)])  5.27 us
  transfers between devices with their start and end apart: 7, of which 4 were waited for; matrix products, arithmetic and copies ran while one was open for 4% of the time, Pallas kernels for 11%

profile of v1, /device:TPU:9, one launch (start us, length us, event | category | flops | bytes accessed | tf_op | source)
XLA Modules:
  0.0 163.1 jit_solution(5810155109649169227)
XLA Ops:
  0.0 0.7 copy.22
  0.7 0.7 broadcast_in_dim.8
  1.4 0.6 pad_maximum_fusion
  2.0 7.8 %all-to-all-start.1 = ((f32[16,4,128]{2,1,0:T(4,128)}), f32[16,4,128]{2,1,0:T(4,128)S(1)}, u32[]{:S(2)}, u32[]{:S(2)}) async-start(f32[16,4,128]{2,1,0:T(4,128)} %pad_maximum_fusion), calls=%async_computation.1 | async-start | bytes 65536 | tf_op jit(solution)/shard_map/all_to_all | solution.py:366
  9.9 0.7 fusion.1
  10.6 0.1 add.104
  10.7 0.1 multiply_add_fusion
  10.8 0.1 add.101
  10.8 0.6 shift-left_clamp_fusion.base_ref
  11.5 0.6 subtract_add_fusion.1.delta_ref
  12.1 0.6 pad_maximum_fusion.1.cs_ref
  12.6 0.0 copy-start.6
  12.7 0.0 copy-start.1
  12.7 18.0 %shard_map.55 = f32[512,128]{1,0:T(8,128)} custom-call(s32[1024]{0:T(1024)} %shift-left_clamp_fusion.base_ref, f32[1024]{0:T(1024)} %subtract_add_fusion.1.delta_ref, f32[2,16]{1,0:T(2,128)} %pad_maximum_fusion.1.cs_ref, f32[2048,256]{1,0:T(8,128)} %bitcast.33, f32[2048,256]{1,0:T(8,128)} %bitcast.34), custom_call_target="tpu_custom_call" | custom-call | flops 30000001024 | bytes 2097152 | tf_op jit(solution)/shard_map/pallas_call | solution.py:341
  30.7 0.0 all-to-all-done.1
  30.7 0.0 copy-start.3
  30.7 10.1 %all-to-all-start = ((f32[128,4,128]{2,1,0:T(4,128)}), f32[128,4,128]{2,1,0:T(4,128)S(1)}, u32[]{:S(2)}, u32[]{:S(2)}) async-start(f32[128,4,128]{2,1,0:T(4,128)} %bitcast.26), calls=%async_computation | async-start | bytes 524288 | tf_op jit(solution)/shard_map/all_to_all | solution.py:383
  40.8 0.1 sub.55
  40.9 0.0 copy-done.6
  40.9 0.1 broadcast_in_dim.6
  41.0 0.7 reshape.152.lanes_ref
  41.7 0.0 copy-done.1
  41.7 0.7 reshape.153.starts_ref
  42.4 0.1 copy.18
  42.5 0.1 subtract_add_fusion
  42.6 0.1 copy.19
  42.7 8.1 %all-to-all-done = f32[128,4,128]{2,1,0:T(4,128)S(1)} async-done(((f32[128,4,128]{2,1,0:T(4,128)}), f32[128,4,128]{2,1,0:T(4,128)S(1)}, u32[]{:S(2)}, u32[]{:S(2)}) %all-to-all-start) | async-done | bytes 262176 | tf_op jit(solution)/shard_map/all_to_all | solution.py:383
  50.8 0.0 copy-start
  50.8 0.0 copy-done.3
  50.8 0.7 copy-done
  51.5 13.6 %shard_map.56 = bf16[512,128]{1,0:T(8,128)(2,1)} custom-call(s32[4096]{0:T(1024)} %reshape.153.starts_ref, s32[1]{0:T(128)} %bitcast.9.own_ref, f32[512,128]{1,0:T(8,128)} %bitcast.27, f32[64,128]{1,0:T(8,128)} %bitcast.31), custom_call_target="tpu_custom_call" | custom-call | flops 10000000000 | bytes 294912 | tf_op jit(solution)/shard_map/pallas_call | solution.py:341
  65.1 5.5 %all-to-all-start.2 = ((bf16[128,4,128]{2,1,0:T(4,128)(2,1)}), bf16[128,4,128]{2,1,0:T(4,128)(2,1)S(1)}, u32[]{:S(2)}, u32[]{:S(2)}) async-start(bf16[128,4,128]{2,1,0:T(4,128)(2,1)} %bitcast.29), calls=%async_computation.2 | async-start | bytes 262144 | tf_op jit(solution)/shard_map/all_to_all | solution.py:401
  70.6 0.7 broadcast_subtract_fusion.delta_ref
  71.3 8.3 %all-to-all-done.2 = bf16[128,4,128]{2,1,0:T(4,128)(2,1)S(1)} async-done(((bf16[128,4,128]{2,1,0:T(4,128)(2,1)}), bf16[128,4,128]{2,1,0:T(4,128)(2,1)S(1)}, u32[]{:S(2)}, u32[]{:S(2)}) %all-to-all-start.2) | async-done | bytes 131104 | tf_op jit(solution)/shard_map/all_to_all | solution.py:401
  79.6 0.0 copy-start.2
  79.6 0.7 copy-done.2
  80.2 16.4 %shard_map.57 = (f32[128,16,256]{2,1,0:T(8,128)}, f32[4,16,128]{2,1,0:T(8,128)}, f32[4,16,128]{2,1,0:T(8,128)}) custom-call(s32[1024]{0:T(1024)} %shift-left_clamp_fusion.base_ref, f32[2048,256]{1,0:T(8,128)} %bitcast.35, f32[2048,256]{1,0:T(8,128)} %bitcast.36, f32[64,384]{1,0:T(8,128)} %broadcast_subtract_fusion.delta_ref, f32[2,384]{1,0:T(2,128)} %reshape.152.lanes_ref, ...), custom_call_target="tpu_custom_call" | custom-call | flops 30000001024 | bytes 2329600 | tf_op jit(solution)/shard_map/pallas_call | solution.py:341
  96.7 2.4 %collective-permute-start = (f32[4,16,128]{2,1,0:T(8,128)}, f32[4,16,128]{2,1,0:T(8,128)S(1)}, u32[]{:S(2)}, u32[]{:S(2)}) collective-permute-start(f32[4,16,128]{2,1,0:T(8,128)} %get-tuple-element.9), channel_id=1, source_target_pairs={{0,1},{1,2},{2,3},{3,4},{4,5},{5,6},{6,7},{8,9},{9,10},{10,11},{11... | collective-permute-start | bytes 98312 | tf_op jit(solution)/shard_map/ppermute | solution.py:427
  99.1 1.9 %collective-permute-start.1 = (f32[4,16,128]{2,1,0:T(8,128)}, f32[4,16,128]{2,1,0:T(8,128)S(1)}, u32[]{:S(2)}, u32[]{:S(2)}) collective-permute-start(f32[4,16,128]{2,1,0:T(8,128)} %get-tuple-element.10), channel_id=1, source_target_pairs={{1,0},{2,1},{3,2},{4,3},{5,4},{6,5},{7,6},{9,8},{10,9},{11,10},{12... | collective-permute-start | bytes 98312 | tf_op jit(solution)/shard_map/ppermute | solution.py:428
  101.0 0.9 fusion.3
  101.9 0.0 collective-permute-done.before_ref
  101.9 0.0 copy-start.4
  101.9 2.6 %collective-permute-done.1.after_ref = f32[4,16,128]{2,1,0:T(8,128)S(1)} collective-permute-done((f32[4,16,128]{2,1,0:T(8,128)}, f32[4,16,128]{2,1,0:T(8,128)S(1)}, u32[]{:S(2)}, u32[]{:S(2)}) %collective-permute-start.1) | collective-permute-done | bytes 32800 | tf_op jit(solution)/shard_map/ppermute | solution.py:428
  104.5 0.0 copy-start.5
  104.6 2.1 %collective-permute-start.2 = (f32[5,16,256]{2,1,0:T(8,128)S(1)}, f32[5,16,256]{2,1,0:T(8,128)S(1)}, u32[]{:S(2)}, u32[]{:S(2)}) collective-permute-start(f32[5,16,256]{2,1,0:T(8,128)S(1)} %maximum_maximum_fusion), channel_id=1, source_target_pairs={{0,8},{8,16},{16,24},{24,32},{32,40},{40,48},{48,56},{56,64},{64,7... | collective-permute-start | bytes 245768 | tf_op jit(solution)/shard_map/ppermute | solution.py:435
  106.7 5.3 %collective-permute-start.3 = (f32[5,16,256]{2,1,0:T(8,128)S(1)}, f32[5,16,256]{2,1,0:T(8,128)S(1)}, u32[]{:S(2)}, u32[]{:S(2)}) collective-permute-start(f32[5,16,256]{2,1,0:T(8,128)S(1)} %maximum_maximum_fusion.1), channel_id=1, source_target_pairs={{8,0},{16,8},{24,16},{32,24},{40,32},{48,40},{56,48},{64,56},{72,6... | collective-permute-start | bytes 245768 | tf_op jit(solution)/shard_map/ppermute | solution.py:436
  112.0 0.6 add_convert_fusion.place_ref
  112.6 0.0 collective-permute-done.2.above_ref
  112.6 0.0 copy-start.7
  112.6 0.8 collective-permute-done.3.below_ref
  113.5 0.0 copy-done.4
  113.5 0.0 copy-done.5
  113.5 0.0 copy-done.7
  113.5 0.0 copy-start.8
  113.5 0.6 copy-done.8
  114.1 49.1 %shard_map.58 = f32[2048,256]{1,0:T(8,128)} custom-call(s32[4]{0:T(128)} %add_convert_fusion.place_ref, f32[128,16,256]{2,1,0:T(8,128)} %get-tuple-element.8.x_ref, f32[5,16,256]{2,1,0:T(8,128)} %copy-done.7, f32[5,16,256]{2,1,0:T(8,128)} %copy-done.8, f32[4,16,128]{2,1,0:T(8,128)} %copy-done.4, f32[4,16,128]{2,1,0:T(8,128)} %copy-done.5), custom_call_target="tpu_custom_call" | custom-call | flops 10000000000 | bytes 2326528 | tf_op jit(solution)/shard_map/pallas_call | solution.py:341
  (9 shorter events, 0.1 us)
Async XLA Ops:
  2.0 28.7 %all-to-all-start.1 = ((f32[16,4,128]{2,1,0:T(4,128)}), f32[16,4,128]{2,1,0:T(4,128)S(1)}, u32[]{:S(2)}, u32[]{:S(2)}) async-start(f32[16,4,128]{2,1,0:T(4,128)} %pad_maximum_fusion), calls=%async_computation.1 | async-start | bytes 65536 | tf_op jit(solution)/shard_map/all_to_all | solution.py:366
  12.6 28.3 %copy-start.6 = (f32[2,16]{1,0:T(2,128)S(1)}, f32[2,16]{1,0:T(2,128)}, u32[]{:S(2)}) copy-start(f32[2,16]{1,0:T(2,128)} %pad_maximum_fusion.1.cs_ref) | copy-start | bytes 388
  12.7 29.1 %copy-start.1 = (s32[16,16,16]{2,1,0:T(8,128)S(1)}, s32[16,16,16]{2,1,0:T(8,128)}, u32[]{:S(2)}) copy-start(s32[16,16,16]{2,1,0:T(8,128)} %param.9) | copy-start | bytes 49156
  30.7 20.1 %copy-start.3 = (f32[16,4,128]{2,1,0:T(4,128)}, f32[16,4,128]{2,1,0:T(4,128)S(1)}, u32[]{:S(2)}) copy-start(f32[16,4,128]{2,1,0:T(4,128)S(1)} %all-to-all-done.1) | copy-start | bytes 98308
  30.7 20.1 %all-to-all-start = ((f32[128,4,128]{2,1,0:T(4,128)}), f32[128,4,128]{2,1,0:T(4,128)S(1)}, u32[]{:S(2)}, u32[]{:S(2)}) async-start(f32[128,4,128]{2,1,0:T(4,128)} %bitcast.26), calls=%async_computation | async-start | bytes 524288 | tf_op jit(solution)/shard_map/all_to_all | solution.py:383
  50.8 0.7 copy-start
  65.1 14.5 %all-to-all-start.2 = ((bf16[128,4,128]{2,1,0:T(4,128)(2,1)}), bf16[128,4,128]{2,1,0:T(4,128)(2,1)S(1)}, u32[]{:S(2)}, u32[]{:S(2)}) async-start(bf16[128,4,128]{2,1,0:T(4,128)(2,1)} %bitcast.29), calls=%async_computation.2 | async-start | bytes 262144 | tf_op jit(solution)/shard_map/all_to_all | solution.py:401
  79.6 0.7 copy-start.2
  96.7 5.3 %collective-permute-start = (f32[4,16,128]{2,1,0:T(8,128)}, f32[4,16,128]{2,1,0:T(8,128)S(1)}, u32[]{:S(2)}, u32[]{:S(2)}) collective-permute-start(f32[4,16,128]{2,1,0:T(8,128)} %get-tuple-element.9), channel_id=1, source_target_pairs={{0,1},{1,2},{2,3},{3,4},{4,5},{5,6},{6,7},{8,9},{9,10},{10,11},{11... | collective-permute-start | bytes 98312 | tf_op jit(solution)/shard_map/ppermute | solution.py:427
  99.1 5.4 %collective-permute-start.1 = (f32[4,16,128]{2,1,0:T(8,128)}, f32[4,16,128]{2,1,0:T(8,128)S(1)}, u32[]{:S(2)}, u32[]{:S(2)}) collective-permute-start(f32[4,16,128]{2,1,0:T(8,128)} %get-tuple-element.10), channel_id=1, source_target_pairs={{1,0},{2,1},{3,2},{4,3},{5,4},{6,5},{7,6},{9,8},{10,9},{11,10},{12... | collective-permute-start | bytes 98312 | tf_op jit(solution)/shard_map/ppermute | solution.py:428
  101.9 11.5 %copy-start.4 = (f32[4,16,128]{2,1,0:T(8,128)}, f32[4,16,128]{2,1,0:T(8,128)S(1)}, u32[]{:S(2)}) copy-start(f32[4,16,128]{2,1,0:T(8,128)S(1)} %collective-permute-done.before_ref) | copy-start | bytes 98308
  104.5 8.9 %copy-start.5 = (f32[4,16,128]{2,1,0:T(8,128)}, f32[4,16,128]{2,1,0:T(8,128)S(1)}, u32[]{:S(2)}) copy-start(f32[4,16,128]{2,1,0:T(8,128)S(1)} %collective-permute-done.1.after_ref) | copy-start | bytes 98308
  104.6 8.1 %collective-permute-start.2 = (f32[5,16,256]{2,1,0:T(8,128)S(1)}, f32[5,16,256]{2,1,0:T(8,128)S(1)}, u32[]{:S(2)}, u32[]{:S(2)}) collective-permute-start(f32[5,16,256]{2,1,0:T(8,128)S(1)} %maximum_maximum_fusion), channel_id=1, source_target_pairs={{0,8},{8,16},{16,24},{24,32},{32,40},{40,48},{48,56},{56,64},{64,7... | collective-permute-start | bytes 245768 | tf_op jit(solution)/shard_map/ppermute | solution.py:435
  106.7 6.7 %collective-permute-start.3 = (f32[5,16,256]{2,1,0:T(8,128)S(1)}, f32[5,16,256]{2,1,0:T(8,128)S(1)}, u32[]{:S(2)}, u32[]{:S(2)}) collective-permute-start(f32[5,16,256]{2,1,0:T(8,128)S(1)} %maximum_maximum_fusion.1), channel_id=1, source_target_pairs={{8,0},{16,8},{24,16},{32,24},{40,32},{48,40},{56,48},{64,56},{72,6... | collective-permute-start | bytes 245768 | tf_op jit(solution)/shard_map/ppermute | solution.py:436
  112.6 0.8 copy-start.7
  113.5 0.6 copy-start.8

commit v2 on v1

--- a/solution.py
+++ b/solution.py
@@ -18,6 +18,7 @@
 BINS = 24
 ROWS = 32
 BAND = ANGLES * BINS
+MESSAGE = 8
 
 inverse_root = 0.7071067811865476
 smoothing = 0.25
@@ -43,7 +44,8 @@
 
 
 def forward_kernel(
-    base_ref, delta_ref, cs_ref, image0_ref, image1_ref, out_ref, xt, rel, band0, band1, sums
+    base_ref, delta_ref, cs_ref, own_ref, image0_ref, image1_ref, measured_ref, weight_ref,
+    out_ref, xt, rel, band0, band1, sums,
 ):
     slices = ROWS // 2
     lane = lax.broadcasted_iota(jnp.int32, (BINS, PIX), 1)
@@ -60,7 +62,7 @@
         xt[pl.ds(pl.multiple_of(u * TILE, TILE), TILE), :] = stacked.T.astype(BF16)
         return carry
 
-    lax.fori_loop(0, TILE, flip, 0, unroll=4)
+    lax.fori_loop(0, TILE, flip, 0, unroll=16)
 
     def build(patch, band):
         for a in range(0, ANGLES, 2):
@@ -93,48 +95,61 @@
         return carry
 
     lax.fori_loop(0, PATCHES * PATCHES // 2, step, 0)
+    stride = MESSAGE * ANGLES // 2
     for a in range(ANGLES):
         turned = sums[a].T * 0.03125
         for t in range(2):
-            row = (a // 2) * 4 + t * 2 + a % 2
-            out_ref[pl.ds(row, slices, stride=ROWS), :] = turned[t * slices : (t + 1) * slices, :]
-
-
-def owner_kernel(starts_ref, own_ref, got_ref, given_ref, out_ref, low, high, wide, filt, staged):
+            row = (a // 2) * MESSAGE + t * 2 + a % 2
+            out_ref[pl.ds(row, slices, stride=stride), :] = turned[t * slices : (t + 1) * slices, :]
+    row = own_ref[0] * MESSAGE + 4
+    for h in range(2):
+        out_ref[pl.ds(row + h, slices, stride=stride), :] = measured_ref[h]
+        weight = jnp.broadcast_to(weight_ref[h : h + 1, :], (slices, TILE))
+        out_ref[pl.ds(row + 2 + h, slices, stride=stride), :] = weight
+
+
+def owner_kernel(starts_ref, own_ref, got_ref, out_ref, low, high, wide, filt, staged):
     blocks = 16
-    groups = got_ref.shape[0] // 8
+    per = 8
+    groups = staged.shape[0] // (8 * per)
     low[...] = jnp.zeros_like(low)
     high[...] = jnp.zeros_like(high)
     lane = lax.broadcasted_iota(jnp.int32, (8, TILE), 1)
     sub = lax.broadcasted_iota(jnp.int32, (8, TILE), 0)
-    first = own_ref[0] * 2
-
-    def where_of(g, k):
-        tile = g * 4 + (k // 4) * 2 + (k // 2) % 2
-        start = starts_ref[tile * ANGLES + first + k % 2]
-        return start >> 7, start & (TILE - 1)
 
     def add(g, carry):
-        rows = got_ref[pl.ds(pl.multiple_of(g * 8, 8), 8), :]
-        for k in range(8):
-            block, shift = where_of(g, k)
-            turned = jnp.where(sub == k, pltpu.roll(rows, shift, 1), 0.0)
-            tail = lane >= shift
-            low[block] += jnp.where(tail, turned, 0.0)
-            high[block] += jnp.where(tail, 0.0, turned)
+        turned = []
+        for i in range(2 * per):
+            source = g * 2 * per + i
+            rows = got_ref[pl.ds(pl.multiple_of(source * MESSAGE, MESSAGE), MESSAGE), :]
+            for k in range(4):
+                start = starts_ref[source * 4 + k]
+                turned.append((start >> 7, start & (TILE - 1), rows, i % 2 * 4 + k, k))
+        turned = [
+            (block, shift, pltpu.roll(rows, shift, 1), slot) for block, shift, rows, slot, k in turned
+        ]
+        for block, shift, value, slot in turned:
+            tail = jnp.where(lane >= shift, value, 0.0)
+            low[slot, block] += tail
+            high[slot, block] += value - tail
         return carry
 
     lax.fori_loop(0, groups, add, 0)
     wide[...] = jnp.zeros_like(wide)
-    for h in range(2):
-        for b in range(blocks):
-            total = low[b]
+    for b in range(blocks):
+        total = jnp.zeros((8, TILE), F32)
+        for slot in range(8):
+            here = low[slot, b]
             if b:
-                total = total + high[b - 1]
-            total = jnp.sum(jnp.where(sub % 2 == h, total, 0.0), axis=0, keepdims=True)
-            meas = given_ref[b * 4 + h : b * 4 + h + 1, :]
-            weight = given_ref[b * 4 + 2 + h : b * 4 + 3 + h, :]
-            wide[h * blocks + b : h * blocks + b + 1, TILE : 2 * TILE] = weight * (meas - total)
+                here = here + high[slot, b - 1]
+            total = total + jnp.where(sub == slot % 4, here, 0.0)
+        home = pl.multiple_of((b * 8 + own_ref[0]) * MESSAGE, MESSAGE)
+        given = got_ref[pl.ds(home, MESSAGE), :]
+        for h in range(2):
+            row = total[h : h + 1, :] + total[2 + h : 3 + h, :]
+            wide[h * blocks + b : h * blocks + b + 1, TILE : 2 * TILE] = given[6 + h : 7 + h, :] * (
+                given[4 + h : 5 + h, :] - row
+            )
     centre = wide[:, TILE : 2 * TILE]
     at = lax.broadcasted_iota(jnp.int32, (2 * blocks, TILE), 0) % blocks
     wide[:, :TILE] = jnp.where(at == 0, 0.0, pltpu.roll(centre, 1, 0))
@@ -157,12 +172,19 @@
             filt[h, b] = jnp.broadcast_to(row, (8, TILE))
 
     def take(g, carry):
-        rows = jnp.zeros((8, TILE), F32)
-        for k in range(8):
-            block, shift = where_of(g, k)
-            mixed = jnp.where(lane >= shift, filt[k % 2, block], filt[k % 2, block + 1])
-            rows = jnp.where(sub == k, pltpu.roll(mixed, (TILE - shift) & (TILE - 1), 1), rows)
-        staged[pl.ds(pl.multiple_of(g * 8, 8), 8), :] = rows
+        mixed = []
+        for i in range(per):
+            for k in range(8):
+                start = starts_ref[(g * per + i) * 8 + k]
+                block, shift = start >> 7, start & (TILE - 1)
+                value = jnp.where(lane >= shift, filt[k % 2, block], filt[k % 2, block + 1])
+                mixed.append((value, (TILE - shift) & (TILE - 1)))
+        turned = [pltpu.roll(value, shift, 1) for value, shift in mixed]
+        for i in range(per):
+            rows = turned[i * 8]
+            for k in range(1, 8):
+                rows = jnp.where(sub == k, turned[i * 8 + k], rows)
+            staged[pl.ds(pl.multiple_of((g * per + i) * 8, 8), 8), :] = rows
         return carry
 
     lax.fori_loop(0, groups, take, 0)
@@ -243,12 +265,27 @@
 
 
 def smooth_kernel(
-    place_ref, x_ref, above_ref, below_ref, before_ref, after_ref, out_ref, first, second,
-    out0, out1, sems,
+    place_ref, before_ref, after_ref, above_side_ref, below_side_ref, x_ref, above_ref, below_ref,
+    out_ref, first, second, out0, out1, sems,
 ):
     slices = ROWS // 2
     high = TILE + 2 * TV_STEPS
     per = TILE // TV_STEPS
+    width = 2 * TILE
+    coming = [
+        pltpu.make_async_copy(
+            ref.at[pl.ds(0, count)], first.at[pl.ds(start, count), :, pl.ds(0, width)], sems.at[i]
+        )
+        for i, (ref, start, count) in enumerate(
+            (
+                (x_ref, TV_STEPS, TILE),
+                (above_ref, 0, TV_STEPS),
+                (below_ref, TILE + TV_STEPS, TV_STEPS),
+            )
+        )
+    ]
+    for copy in coming:
+        copy.start()
     lane = lax.broadcasted_iota(jnp.int32, (slices, TILE), 1)
     has_above, has_below, has_before, has_after = (place_ref[i] for i in range(4))
     keep = ((lane < TV_STEPS) & (has_after == 1)) | (
@@ -262,71 +299,82 @@
 
     for r in range(TV_STEPS):
         for ref, start, j in (
-            (above_ref, 0, per - TV_STEPS + r),
-            (below_ref, TILE + TV_STEPS, r),
+            (above_side_ref, 0, per - TV_STEPS + r),
+            (below_side_ref, TILE + TV_STEPS, r),
         ):
-            first[start + r, :, : 2 * TILE] = ref[r]
-            first[start + r, :, 2 * TILE :] = margin(
-                ref[TV_STEPS, :, :TILE], ref[TV_STEPS, :, TILE:], j
-            )
+            first[start + r, :, width:] = margin(ref[:, :TILE], ref[:, TILE:], j)
 
     def load(g, carry):
+        previous = before_ref[g]
+        following = after_ref[g]
         for j in range(per):
-            u = g * per + j
-            first[u + TV_STEPS, :, : 2 * TILE] = x_ref[u]
-            first[u + TV_STEPS, :, 2 * TILE :] = margin(before_ref[g], after_ref[g], j)
+            first[g * per + j + TV_STEPS, :, width:] = margin(previous, following, j)
         return carry
 
     lax.fori_loop(0, TILE // per, load, 0)
+    for copy in coming:
+        copy.wait()
+
+    edge = lax.broadcasted_iota(jnp.int32, (1, slices, 3 * TILE), 2)
+    keep_all = (
+        (edge < width)
+        | ((edge < width + TV_STEPS) & (has_after == 1))
+        | ((edge >= 3 * TILE - TV_STEPS) & (has_before == 1))
+    )
 
     def flows(here, under):
         down = under - here
-        right = pltpu.roll(here, 3 * TILE - 1, 1) - here
+        right = pltpu.roll(here, 3 * TILE - 1, here.ndim - 1) - here
         inverse = lax.rsqrt(smoothing * smoothing + down * down + right * right)
         return down * inverse, right * inverse
-
-    edge = lax.broadcasted_iota(jnp.int32, (slices, 3 * TILE), 1)
-    keep_all = (
-        (edge < 2 * TILE)
-        | ((edge < 2 * TILE + TV_STEPS) & (has_after == 1))
-        | ((edge >= 3 * TILE - TV_STEPS) & (has_before == 1))
-    )
 
     for k in range(TV_STEPS):
         source, target = (first, second) if k % 2 == 0 else (second, first)
         last = k == TV_STEPS - 1
 
-        def row(r, carry, source=source, target=target, last=last):
-            here, came = carry
-            under = source[r + 1]
-            down, right = flows(here, under)
-            change = came - down + pltpu.roll(right, 1, 1) - right
+        def rows(r, count, came, inside, source=source, target=target, last=last):
+            here = source[pl.ds(r, count)]
+            down, right = flows(here, source[pl.ds(r + 1, count)])
+            came = came[None]
+            if count > 1:
+                came = jnp.concatenate([came, down[:-1]], axis=0)
+            change = came - down + pltpu.roll(right, 1, 2) - right
             fresh = here - descent_step * change
             if last:
-                out0[pl.ds(r - TV_STEPS, slices, stride=TILE), :] = fresh[:, :TILE]
-                out1[pl.ds(r - TV_STEPS, slices, stride=TILE), :] = fresh[:, TILE : 2 * TILE]
+                for i in range(count):
+                    spot = pl.ds(r + i - TV_STEPS, slices, stride=TILE)
+                    out0[spot, :] = fresh[i, :, :TILE]
+                    out1[spot, :] = fresh[i, :, TILE:width]
             else:
-                inside = ((r >= TV_STEPS) | (has_above == 1)) & (
-                    (r < TILE + TV_STEPS) | (has_below == 1)
-                )
-                target[r] = jnp.where(keep_all & inside, fresh, 0.0)
-            return under, down
-
-        start = source[k]
-        below = source[k + 1]
-        came, unused = flows(start, below)
-        lax.fori_loop(k + 1, high - k - 1, row, (below, came), unroll=2)
-    copies = [
+                keep_here = keep_all if inside is None else keep_all & inside
+                target[pl.ds(r, count)] = jnp.where(keep_here, fresh, 0.0)
+            return down[count - 1]
+
+        edges = TV_STEPS - 1 - k
+        came, unused = flows(source[k], source[k + 1])
+        if edges:
+            came = rows(k + 1, edges, came, has_above == 1)
+        block = 16
+
+        def body(i, came):
+            return rows(TV_STEPS + i * block, block, came, None)
+
+        came = lax.fori_loop(0, TILE // block, body, came)
+        if edges:
+            rows(TILE + TV_STEPS, edges, came, has_below == 1)
+    going = [
         pltpu.make_async_copy(ref, out_ref.at[:, pl.ds(t * TILE, TILE)], sems.at[t])
         for t, ref in enumerate((out0, out1))
     ]
-    for copy in copies:
+    for copy in going:
         copy.start()
-    for copy in copies:
+    for copy in going:
         copy.wait()
 
 
-def call(kernel, scalars, arrays, outs, scratch, flops, halves=(), out_space=VMEM):
+def call(
+    kernel, scalars, arrays, outs, scratch, flops, halves=(), left=(), out_space=VMEM
+):
     smem = pl.BlockSpec(memory_space=pltpu.SMEM)
     vmem = pl.BlockSpec(memory_space=VMEM)
     specs = [smem] * len(scalars)
@@ -337,7 +385,9 @@
             operands.append(half)
     specs += [vmem] * len(arrays)
     operands += arrays
-    moved = sum(x.size * x.dtype.itemsize for x in (*arrays, *halves))
+    specs += [pl.BlockSpec(memory_space=pl.ANY)] * len(left)
+    operands += left
+    moved = sum(x.size * x.dtype.itemsize for x in (*arrays, *halves, *left))
     return pl.pallas_call(
         kernel,
         grid=(1,),
@@ -360,16 +410,11 @@
     cosine, sine, base, delta = geometry(angle_ids)
     base = base.reshape(-1)
 
-    given = measured[:, 0].transpose(1, 0, 2)
-    weight = jnp.broadcast_to(ray_weight[:, 0][None], given.shape)
-    given = jnp.concatenate([given, weight], axis=1)
-    given = lax.all_to_all(given, "row", split_axis=0, concat_axis=0, tiled=True)
-
     sent = call(
         forward_kernel,
-        (base, delta.reshape(-1), jnp.stack([cosine, sine])),
-        (),
-        jax.ShapeDtypeStruct((rows * cols * 4, TILE), F32),
+        (base, delta.reshape(-1), jnp.stack([cosine, sine]), col_index.reshape(1)),
+        (measured[:, 0], ray_weight[:, 0]),
+        jax.ShapeDtypeStruct((rows * cols * MESSAGE, TILE), F32),
         [
             VMEM((TILE * TILE, ROWS), BF16),
             VMEM((BAND, PIX), F32),
@@ -381,17 +426,19 @@
         halves=(image,),
     )
     got = lax.all_to_all(
-        sent.reshape(rows * cols, 4, TILE), both, split_axis=0, concat_axis=0, tiled=True
+        sent.reshape(rows * cols, MESSAGE, TILE), both, split_axis=0, concat_axis=0, tiled=True
     )
     blocks = rows
+    starts = shadow_start.reshape(-1, ANGLES)
+    starts = lax.dynamic_slice_in_dim(starts, col_index * 2, 2, 1).reshape(-1)
     out = call(
         owner_kernel,
-        (shadow_start.reshape(-1), col_index.reshape(1)),
-        (got.reshape(-1, TILE), given.reshape(-1, TILE)),
+        (starts, col_index.reshape(1)),
+        (got.reshape(-1, TILE),),
         jax.ShapeDtypeStruct((rows * cols * 4, TILE), BF16),
         [
-            VMEM((blocks, 8, TILE), F32),
-            VMEM((blocks, 8, TILE), F32),
+            VMEM((8, blocks, 8, TILE), F32),
+            VMEM((8, blocks, 8, TILE), F32),
             VMEM((2 * blocks, 3 * TILE), F32),
             VMEM((2, blocks + 1, 8, TILE), F32),
             VMEM((rows * cols * 4, TILE), F32),
@@ -426,12 +473,10 @@
     left_going = [(i + 1, i) for i in range(cols - 1)]
     before = lax.ppermute(right, "col", right_going)
     after = lax.ppermute(left, "col", left_going)
-    top = jnp.concatenate(
-        [x[:TV_STEPS], jnp.concatenate([before[:1], after[:1]], axis=2)], axis=0
-    )
-    bottom = jnp.concatenate(
-        [x[-TV_STEPS:], jnp.concatenate([before[-1:], after[-1:]], axis=2)], axis=0
-    )
+    upward = jnp.concatenate([before[0], after[0]], axis=1)[None]
+    downward = jnp.concatenate([before[-1], after[-1]], axis=1)[None]
+    top = jnp.concatenate([x[:TV_STEPS], upward], axis=0)
+    bottom = jnp.concatenate([x[-TV_STEPS:], downward], axis=0)
     above = lax.ppermute(bottom, "row", [(i, i + 1) for i in range(rows - 1)])
     below = lax.ppermute(top, "row", [(i + 1, i) for i in range(rows - 1)])
     place = jnp.stack(
@@ -442,10 +487,11 @@
     smooth = call(
         smooth_kernel,
         (place,),
-        (x, above, below, before, after),
+        (before, after, above[TV_STEPS], below[TV_STEPS]),
         jax.ShapeDtypeStruct((slices * TILE, 2 * TILE), F32),
-        [wide, wide, half, half, pltpu.SemaphoreType.DMA((2,))],
+        [wide, wide, half, half, pltpu.SemaphoreType.DMA((3,))],
         10_000_000_000,
+        left=(x, above, below),
         out_space=pl.ANY,
     )
     return smooth.reshape(current_image.shape)

time: 164 us -> 116 us (0.71)
  Pallas kernels: 97.1 us -> 55.4 us
  starting transfers between devices: 35.2 us -> 28.6 us
    pallas_call x4, Pallas kernels: 97.1 us -> 55.4 us  [call(): pl.pallas_call(kernel, grid=(1,), out_shape=outs, in_specs=specs, out_spe...]
    all_to_all x2 -> x1, starting transfers between devices: 18 us -> 10.7 us  [local(): lax.all_to_all(sent.reshape(rows * cols, MESSAGE, TILE), both, split_axis...]
    all_to_all x2 -> x1, waiting for transfers between devices: 8.15 us -> 10.8 us  [local(): lax.all_to_all(sent.reshape(rows * cols, MESSAGE, TILE), both, split_axis...]
  transfers between devices with their start and end apart: 7 -> 6, of which waited for: 4 -> 4; matrix products, arithmetic and copies ran while one was open for 4% -> 4% of each run, Pallas kernels for 11% -> 0%
where the time goes in v2:
time: 116 us; the launch traced here: 115 us
  Pallas kernels  55.4 us (48%)
  starting transfers between devices  28.6 us (25%)
  waiting for transfers between devices  21.1 us (18%)
  local copies, waits for them, and re-layouts  5.65 us (5%)
  other arithmetic  4.05 us (3%)
    pallas_call x4, Pallas kernels, call(): pl.pallas_call(kernel, grid=(1,), out_shape=outs, in_specs=specs, out_spe...  55.4 us
    all_to_all x1, waiting for transfers between devices, local(): lax.all_to_all(sent.reshape(rows * cols, MESSAGE, TILE), both, split_axis...  10.8 us
    all_to_all x1, starting transfers between devices, local(): lax.all_to_all(sent.reshape(rows * cols, MESSAGE, TILE), both, split_axis...  10.7 us
    all_to_all x1, waiting for transfers between devices, local(): lax.all_to_all(out.reshape(rows * cols, 4, TILE), both, split_axis=0, con...  6.91 us
    all_to_all x1, starting transfers between devices, local(): lax.all_to_all(out.reshape(rows * cols, 4, TILE), both, split_axis=0, con...  6.17 us
    ppermute x1, starting transfers between devices, local(): below = lax.ppermute(top, 'row', [(i + 1, i) for i in range(rows - 1)])  5.27 us
    ppermute x1, waiting for transfers between devices, local(): after = lax.ppermute(left, 'col', left_going)  2.6 us
    ppermute x1, starting transfers between devices, local(): before = lax.ppermute(right, 'col', right_going)  2.43 us
  transfers between devices with their start and end apart: 6, of which 4 were waited for; matrix products, arithmetic and copies ran while one was open for 4% of the time, Pallas kernels for 0%

profile of v2, /device:TPU:9, one launch (start us, length us, event | category | flops | bytes accessed | tf_op | source)
XLA Modules:
  0.0 115.1 jit_solution(7067787232330412882)
XLA Ops:
  0.0 0.0 copy-start
  0.0 0.7 fusion.1
  0.8 0.1 add.107
  0.8 0.1 multiply_add_fusion
  0.9 0.1 add.104
  1.0 0.6 shift-left_clamp_fusion.base_ref
  1.6 0.6 subtract_add_fusion.1.delta_ref
  2.2 0.6 pad_maximum_fusion.2.cs_ref
  2.8 15.8 %shard_map.55 = f32[1024,128]{1,0:T(8,128)} custom-call(s32[1024]{0:T(1024)} %shift-left_clamp_fusion.base_ref, f32[1024]{0:T(1024)} %subtract_add_fusion.1.delta_ref, f32[2,16]{1,0:T(2,128)} %pad_maximum_fusion.2.cs_ref, s32[1]{0:T(128)} %bitcast.10.own_ref, f32[2048,256]{1,0:T(8,128)} %bitcast.43, f32[2048,256]{1,0:T(8,128)} %bitcast.44, ...), custom_call_target="tpu_custom_call" | custom-call | flops 30000001024 | bytes 2114560 | tf_op jit(solution)/shard_map/pallas_call | solution.py:391
  18.6 10.7 %all-to-all-start = ((f32[128,8,128]{2,1,0:T(8,128)}), f32[128,8,128]{2,1,0:T(8,128)S(1)}, u32[]{:S(2)}, u32[]{:S(2)}) async-start(f32[128,8,128]{2,1,0:T(8,128)} %bitcast.40), calls=%async_computation | async-start | bytes 1048576 | tf_op jit(solution)/shard_map/all_to_all | solution.py:428
  29.3 0.1 sub.55
  29.4 0.1 copy.12
  29.5 0.0 copy-done
  29.5 0.1 constant_dynamic-slice_fusion
  29.6 0.7 reshape.154.starts_ref
  30.3 0.1 subtract_add_fusion
  30.4 0.1 copy.13
  30.5 10.8 %all-to-all-done = f32[128,8,128]{2,1,0:T(8,128)S(1)} async-done(((f32[128,8,128]{2,1,0:T(8,128)}), f32[128,8,128]{2,1,0:T(8,128)S(1)}, u32[]{:S(2)}, u32[]{:S(2)}) %all-to-all-start) | async-done | bytes 524320 | tf_op jit(solution)/shard_map/all_to_all | solution.py:428
  41.4 0.0 copy-start.1
  41.4 0.8 copy-done.1
  42.1 0.0 copy-start.5
  42.1 6.7 %shard_map.56 = bf16[512,128]{1,0:T(8,128)(2,1)} custom-call(s32[512]{0:T(512)} %reshape.154.starts_ref, s32[1]{0:T(128)} %bitcast.10.own_ref, f32[1024,128]{1,0:T(8,128)} %bitcast.39), custom_call_target="tpu_custom_call" | custom-call | flops 10000000000 | bytes 524288 | tf_op jit(solution)/shard_map/pallas_call | solution.py:391
  48.8 6.2 %all-to-all-start.1 = ((bf16[128,4,128]{2,1,0:T(4,128)(2,1)}), bf16[128,4,128]{2,1,0:T(4,128)(2,1)S(1)}, u32[]{:S(2)}, u32[]{:S(2)}) async-start(bf16[128,4,128]{2,1,0:T(4,128)(2,1)} %bitcast.42), calls=%async_computation.1 | async-start | bytes 262144 | tf_op jit(solution)/shard_map/all_to_all | solution.py:448
  55.0 0.6 broadcast_subtract_fusion.delta_ref
  55.6 0.0 copy-done.5
  55.6 0.1 broadcast_in_dim.6
  55.7 0.7 reshape.152.lanes_ref
  56.4 0.7 add_convert_fusion.place_ref
  57.1 6.9 %all-to-all-done.1 = bf16[128,4,128]{2,1,0:T(4,128)(2,1)S(1)} async-done(((bf16[128,4,128]{2,1,0:T(4,128)(2,1)}), bf16[128,4,128]{2,1,0:T(4,128)(2,1)S(1)}, u32[]{:S(2)}, u32[]{:S(2)}) %all-to-all-start.1) | async-done | bytes 131104 | tf_op jit(solution)/shard_map/all_to_all | solution.py:448
  64.0 0.0 copy-start.2
  64.0 0.7 copy-done.2
  64.6 16.4 %shard_map.57 = (f32[128,16,256]{2,1,0:T(8,128)}, f32[4,16,128]{2,1,0:T(8,128)}, f32[4,16,128]{2,1,0:T(8,128)}) custom-call(s32[1024]{0:T(1024)} %shift-left_clamp_fusion.base_ref, f32[2048,256]{1,0:T(8,128)} %bitcast.45, f32[2048,256]{1,0:T(8,128)} %bitcast.46, f32[64,384]{1,0:T(8,128)} %broadcast_subtract_fusion.delta_ref, f32[2,384]{1,0:T(2,128)} %reshape.152.lanes_ref, ...), custom_call_target="tpu_custom_call" | custom-call | flops 30000001024 | bytes 2329600 | tf_op jit(solution)/shard_map/pallas_call | solution.py:391
  81.0 2.4 %collective-permute-start = (f32[4,16,128]{2,1,0:T(8,128)}, f32[4,16,128]{2,1,0:T(8,128)S(1)}, u32[]{:S(2)}, u32[]{:S(2)}) collective-permute-start(f32[4,16,128]{2,1,0:T(8,128)} %get-tuple-element.8), channel_id=1, source_target_pairs={{0,1},{1,2},{2,3},{3,4},{4,5},{5,6},{6,7},{8,9},{9,10},{10,11},{11... | collective-permute-start | bytes 98312 | tf_op jit(solution)/shard_map/ppermute | solution.py:474
  83.5 1.9 %collective-permute-start.1 = (f32[4,16,128]{2,1,0:T(8,128)}, f32[4,16,128]{2,1,0:T(8,128)S(1)}, u32[]{:S(2)}, u32[]{:S(2)}) collective-permute-start(f32[4,16,128]{2,1,0:T(8,128)} %get-tuple-element.9), channel_id=1, source_target_pairs={{1,0},{2,1},{3,2},{4,3},{5,4},{6,5},{7,6},{9,8},{10,9},{11,10},{12... | collective-permute-start | bytes 98312 | tf_op jit(solution)/shard_map/ppermute | solution.py:475
  85.4 0.9 fusion.3
  86.3 0.0 collective-permute-done.before_ref
  86.3 0.0 copy-start.3
  86.3 2.6 %collective-permute-done.1.after_ref = f32[4,16,128]{2,1,0:T(8,128)S(1)} collective-permute-done((f32[4,16,128]{2,1,0:T(8,128)}, f32[4,16,128]{2,1,0:T(8,128)S(1)}, u32[]{:S(2)}, u32[]{:S(2)}) %collective-permute-start.1) | collective-permute-done | bytes 32800 | tf_op jit(solution)/shard_map/ppermute | solution.py:475
  88.9 0.0 copy-start.4
  88.9 2.1 %collective-permute-start.2 = (f32[5,16,256]{2,1,0:T(8,128)S(1)}, f32[5,16,256]{2,1,0:T(8,128)S(1)}, u32[]{:S(2)}, u32[]{:S(2)}) collective-permute-start(f32[5,16,256]{2,1,0:T(8,128)S(1)} %pad_maximum_fusion), channel_id=1, source_target_pairs={{0,8},{8,16},{16,24},{24,32},{32,40},{40,48},{48,56},{56,64},{64,7... | collective-permute-start | bytes 245768 | tf_op jit(solution)/shard_map/ppermute | solution.py:480
  91.1 5.3 %collective-permute-start.3 = (f32[5,16,256]{2,1,0:T(8,128)S(1)}, f32[5,16,256]{2,1,0:T(8,128)S(1)}, u32[]{:S(2)}, u32[]{:S(2)}) collective-permute-start(f32[5,16,256]{2,1,0:T(8,128)S(1)} %pad_maximum_fusion.1), channel_id=1, source_target_pairs={{8,0},{16,8},{24,16},{32,24},{40,32},{48,40},{56,48},{64,56},{72,6... | collective-permute-start | bytes 245768 | tf_op jit(solution)/shard_map/ppermute | solution.py:481
  96.4 0.0 collective-permute-done.2.above_ref
  96.4 0.0 copy-start.6
  96.4 0.6 slice_bitcast_fusion.1.above_side_ref
  97.0 0.8 collective-permute-done.3.below_ref
  97.8 0.0 copy-start.7
  97.8 0.6 slice_bitcast_fusion.below_side_ref
  98.5 0.0 copy-done.3
  98.5 0.0 copy-done.4
  98.5 0.0 copy-done.6
  98.5 0.0 copy-done.7
  98.5 16.6 %shard_map.58 = f32[2048,256]{1,0:T(8,128)} custom-call(s32[4]{0:T(128)} %add_convert_fusion.place_ref, f32[4,16,128]{2,1,0:T(8,128)} %copy-done.3, f32[4,16,128]{2,1,0:T(8,128)} %copy-done.4, f32[16,256]{1,0:T(8,128)} %slice_bitcast_fusion.1.above_side_ref, f32[16,256]{1,0:T(8,128)} %slice_bitcast_fusion.below_side_ref, ...), custom_call_target="tpu_custom_call" | custom-call | flops 10000000000 | bytes 2359296 | tf_op jit(solution)/shard_map/pallas_call | solution.py:391
  (11 shorter events, 0.1 us)
Async XLA Ops:
  0.0 29.5 %copy-start = (s32[16,16,16]{2,1,0:T(8,128)S(1)}, s32[16,16,16]{2,1,0:T(8,128)}, u32[]{:S(2)}) copy-start(s32[16,16,16]{2,1,0:T(8,128)} %param.9) | copy-start | bytes 49156
  18.6 22.8 %all-to-all-start = ((f32[128,8,128]{2,1,0:T(8,128)}), f32[128,8,128]{2,1,0:T(8,128)S(1)}, u32[]{:S(2)}, u32[]{:S(2)}) async-start(f32[128,8,128]{2,1,0:T(8,128)} %bitcast.40), calls=%async_computation | async-start | bytes 1048576 | tf_op jit(solution)/shard_map/all_to_all | solution.py:428
  41.4 0.8 copy-start.1
  42.1 13.5 %copy-start.5 = (f32[2,16]{1,0:T(2,128)S(1)}, f32[2,16]{1,0:T(2,128)}, u32[]{:S(2)}) copy-start(f32[2,16]{1,0:T(2,128)} %pad_maximum_fusion.2.cs_ref) | copy-start | bytes 388
  48.8 15.2 %all-to-all-start.1 = ((bf16[128,4,128]{2,1,0:T(4,128)(2,1)}), bf16[128,4,128]{2,1,0:T(4,128)(2,1)S(1)}, u32[]{:S(2)}, u32[]{:S(2)}) async-start(bf16[128,4,128]{2,1,0:T(4,128)(2,1)} %bitcast.42), calls=%async_computation.1 | async-start | bytes 262144 | tf_op jit(solution)/shard_map/all_to_all | solution.py:448
  64.0 0.7 copy-start.2
  81.0 5.3 %collective-permute-start = (f32[4,16,128]{2,1,0:T(8,128)}, f32[4,16,128]{2,1,0:T(8,128)S(1)}, u32[]{:S(2)}, u32[]{:S(2)}) collective-permute-start(f32[4,16,128]{2,1,0:T(8,128)} %get-tuple-element.8), channel_id=1, source_target_pairs={{0,1},{1,2},{2,3},{3,4},{4,5},{5,6},{6,7},{8,9},{9,10},{10,11},{11... | collective-permute-start | bytes 98312 | tf_op jit(solution)/shard_map/ppermute | solution.py:474
  83.5 5.4 %collective-permute-start.1 = (f32[4,16,128]{2,1,0:T(8,128)}, f32[4,16,128]{2,1,0:T(8,128)S(1)}, u32[]{:S(2)}, u32[]{:S(2)}) collective-permute-start(f32[4,16,128]{2,1,0:T(8,128)} %get-tuple-element.9), channel_id=1, source_target_pairs={{1,0},{2,1},{3,2},{4,3},{5,4},{6,5},{7,6},{9,8},{10,9},{11,10},{12... | collective-permute-start | bytes 98312 | tf_op jit(solution)/shard_map/ppermute | solution.py:475
  86.3 12.2 %copy-start.3 = (f32[4,16,128]{2,1,0:T(8,128)}, f32[4,16,128]{2,1,0:T(8,128)S(1)}, u32[]{:S(2)}) copy-start(f32[4,16,128]{2,1,0:T(8,128)S(1)} %collective-permute-done.before_ref) | copy-start | bytes 98308
  88.9 9.6 %copy-start.4 = (f32[4,16,128]{2,1,0:T(8,128)}, f32[4,16,128]{2,1,0:T(8,128)S(1)}, u32[]{:S(2)}) copy-start(f32[4,16,128]{2,1,0:T(8,128)S(1)} %collective-permute-done.1.after_ref) | copy-start | bytes 98308
  88.9 7.4 %collective-permute-start.2 = (f32[5,16,256]{2,1,0:T(8,128)S(1)}, f32[5,16,256]{2,1,0:T(8,128)S(1)}, u32[]{:S(2)}, u32[]{:S(2)}) collective-permute-start(f32[5,16,256]{2,1,0:T(8,128)S(1)} %pad_maximum_fusion), channel_id=1, source_target_pairs={{0,8},{8,16},{16,24},{24,32},{32,40},{40,48},{48,56},{56,64},{64,7... | collective-permute-start | bytes 245768 | tf_op jit(solution)/shard_map/ppermute | solution.py:480
  91.1 6.7 %collective-permute-start.3 = (f32[5,16,256]{2,1,0:T(8,128)S(1)}, f32[5,16,256]{2,1,0:T(8,128)S(1)}, u32[]{:S(2)}, u32[]{:S(2)}) collective-permute-start(f32[5,16,256]{2,1,0:T(8,128)S(1)} %pad_maximum_fusion.1), channel_id=1, source_target_pairs={{8,0},{16,8},{24,16},{32,24},{40,32},{48,40},{56,48},{64,56},{72,6... | collective-permute-start | bytes 245768 | tf_op jit(solution)/shard_map/ppermute | solution.py:481
  96.4 2.1 %copy-start.6 = (f32[5,16,256]{2,1,0:T(8,128)}, f32[5,16,256]{2,1,0:T(8,128)S(1)}, u32[]{:S(2)}) copy-start(f32[5,16,256]{2,1,0:T(8,128)S(1)} %collective-permute-done.2.above_ref) | copy-start | bytes 245764
  97.8 0.7 copy-start.7

commit v3 on v2

v3 whole, which is shorter than its diff:
```python
import functools
import math

import jax
import jax.numpy as jnp
from jax import lax
from jax.experimental import pallas as pl
from jax.experimental.pallas import tpu as pltpu
from jax.sharding import PartitionSpec as P

TILE = 128
ANGLES = 16
ALL_ANGLES = 256
TV_STEPS = 4
SIDE = 16
PATCHES = TILE // SIDE
PIX = SIDE * SIDE
BINS = 24
ROWS = 32
BAND = ANGLES * BINS
PAIRS = PATCHES * PATCHES // 2
CHUNK = 16
MESSAGE = 8

inverse_root = 0.7071067811865476
smoothing = 0.25
descent_step = 0.05

VMEM = pltpu.VMEM
F32 = jnp.float32
BF16 = jnp.bfloat16


def geometry(angle_ids):
    radians = angle_ids.astype(F32) * (math.pi / ALL_ANGLES)
    cosine = jnp.cos(radians)[None] * inverse_root
    sine = jnp.sin(radians)[None] * inverse_root
    row = lax.broadcasted_iota(jnp.int32, (2 * PAIRS + 2, ANGLES), 0)
    patch = row % PAIRS
    down = (patch // PATCHES).astype(F32) * SIDE - (TILE - 1) / 2.0
    across = (patch % PATCHES).astype(F32) * SIDE - (TILE - 1) / 2.0
    corner = TILE / 2.0 + down * cosine + across * sine
    low = corner + (SIDE - 1) * (jnp.minimum(cosine, 0.0) + jnp.minimum(sine, 0.0))
    base = jnp.clip(jnp.floor((jnp.floor(low - 1.5) + 1.0) / 8.0) * 8.0, 0.0, TILE - BINS)
    delta = corner - base - 0.5
    ends = jnp.where(row == 2 * PAIRS, cosine, sine)
    return jnp.where(row < PAIRS, base, jnp.where(row < 2 * PAIRS, delta, ends))


def reversal():
    there = lax.broadcasted_iota(jnp.int32, (TILE, TILE), 0)
    here = lax.broadcasted_iota(jnp.int32, (TILE, TILE), 1)
    return jnp.where(there + here == TILE - 1, 1.0, 0.0).astype(BF16)


def reverse_lanes(value):
    high = value.astype(BF16)
    low = (value - high.astype(F32)).astype(BF16)
    both = jnp.concatenate([high, low], axis=1)
    turn = reversal()
    return jnp.dot(both, jnp.concatenate([turn, turn], axis=0), preferred_element_type=F32)


def halves_of(image, targets, sems):
    return [
        pltpu.make_async_copy(image.at[:, pl.ds(t * TILE, TILE)], target, sems.at[t])
        for t, target in enumerate(targets)
    ]


def forward_kernel(
    table_ref, own_ref, measured_ref, weight_ref, image_ref,
    out_ref, xt, rel, band0, band1, sums, tails, image0_ref, image1_ref, sems,
):
    coming = halves_of(image_ref, (image0_ref, image1_ref), sems)
    for copy in coming:
        copy.start()
    slices = ROWS // 2
    lane = lax.broadcasted_iota(jnp.int32, (BINS, PIX), 1)
    bin_at = lax.broadcasted_iota(jnp.int32, (BINS, PIX), 0).astype(F32)
    down = (lane // SIDE).astype(F32)
    across = (lane % SIDE).astype(F32)
    for a in range(ANGLES):
        rel[a * BINS : (a + 1) * BINS, :] = (
            down * table_ref[2 * PAIRS, a] + across * table_ref[2 * PAIRS + 1, a] - bin_at
        )
    sums[...] = jnp.zeros_like(sums)
    turn = reversal()
    for copy in coming:
        copy.wait()

    def rows_of(u):
        both = [ref[pl.ds(u, slices, stride=TILE), :] for ref in (image0_ref, image1_ref)]
        return jnp.concatenate(both, axis=0)

    def flip(i, carry):
        u0 = (i // SIDE) * 2 * SIDE + i % SIDE
        u1 = u0 + SIDE
        mirrored = jnp.concatenate([rows_of(TILE - 1 - u0), rows_of(TILE - 1 - u1)], axis=0)
        mirrored = jnp.dot(mirrored.astype(BF16), turn, preferred_element_type=F32)
        stacked = jnp.concatenate(
            [rows_of(u0), mirrored[:ROWS], rows_of(u1), mirrored[ROWS:]], axis=0
        )
        xt[pl.ds(pl.multiple_of(i * TILE, TILE), TILE), :] = stacked.astype(BF16).T
        return carry

    lax.fori_loop(0, 2 * SIDE, flip, 0, unroll=4)

    def build(patch, band):
        for a in range(0, ANGLES, 2):
            pair = []
            for b in (a, a + 1):
                away = jnp.abs(rel[b * BINS : (b + 1) * BINS, :] + table_ref[PAIRS + patch, b])
                pair.append(jnp.maximum(0.0, 1.0 - away))
            band[a * BINS : (a + 2) * BINS, :] = jnp.concatenate(pair, axis=0).astype(BF16)

    first_half = lax.broadcasted_iota(jnp.int32, (PIX, TILE), 1) < TILE // 2

    def project(patch, band, half, col, own):
        pieces = []
        for u in range(SIDE):
            start = pl.multiple_of((half * SIDE + u) * TILE + col * SIDE, SIDE)
            pieces.append(xt[pl.ds(start, SIDE), :])
        pixels = jnp.concatenate(pieces, axis=0)
        nothing = jnp.zeros_like(pixels)
        pixels = jnp.where(first_half, *((nothing, pixels) if own else (pixels, nothing)))
        got = jnp.dot(band[...], pixels, preferred_element_type=F32)
        for a in range(ANGLES):
            start = pl.multiple_of(table_ref[patch, a].astype(jnp.int32), 8)
            sums[a, pl.ds(start, BINS), :] += got[a * BINS : (a + 1) * BINS, :]

    def patch_of(i):
        return (i // PATCHES) * 2 * PATCHES + i % PATCHES

    build(0, band0)

    def step(i, carry):
        half = i // PATCHES
        col = i % PATCHES
        patch = patch_of(i)
        build(patch + PATCHES, band1)
        project(patch, band0, half, col, 0)
        build(patch_of(jnp.minimum(i + 1, 2 * PATCHES - 1)), band0)
        project(patch + PATCHES, band1, half, col, 1)
        return carry

    lax.fori_loop(0, 2 * PATCHES, step, 0)
    stride = MESSAGE * ANGLES // 2
    for a in range(ANGLES):
        tails[a * TILE : (a + 1) * TILE, :] = sums[a].T * 0.03125
    mirrored = [
        tails[a * TILE + ROWS : a * TILE + 2 * ROWS, :]
        + tails[a * TILE + 3 * ROWS : (a + 1) * TILE, :]
        for a in range(ANGLES)
    ]
    mirrored = reverse_lanes(jnp.concatenate(mirrored, axis=0))
    for a in range(ANGLES):
        total = tails[a * TILE : a * TILE + ROWS, :] + tails[a * TILE + 2 * ROWS : a * TILE + 3 * ROWS, :]
        total = total + mirrored[a * ROWS : (a + 1) * ROWS, :]
        for t in range(2):
            row = (a // 2) * MESSAGE + t * 2 + a % 2
            out_ref[pl.ds(row, slices, stride=stride), :] = total[t * slices : (t + 1) * slices, :]
    row = own_ref[0] * MESSAGE + 4
    for h in range(2):
        out_ref[pl.ds(row + h, slices, stride=stride), :] = measured_ref[h]
        weight = jnp.broadcast_to(weight_ref[h : h + 1, :], (slices, TILE))
        out_ref[pl.ds(row + 2 + h, slices, stride=stride), :] = weight


def owner_kernel(starts_ref, own_ref, got_ref, out_ref, wide, filt, staged, *sums):
    low, high = sums[:8], sums[8:]
    blocks = 16
    per = 8
    groups = staged.shape[0] // (8 * per)
    for ref in sums:
        ref[...] = jnp.zeros_like(ref)
    lane = lax.broadcasted_iota(jnp.int32, (8, TILE), 1)
    sub = lax.broadcasted_iota(jnp.int32, (8, TILE), 0)

    def add(g, carry):
        turned = []
        for i in range(2 * per):
            source = g * 2 * per + i
            rows = got_ref[pl.ds(pl.multiple_of(source * MESSAGE, MESSAGE), MESSAGE), :]
            for k in range(4):
                start = starts_ref[source * 4 + k]
                turned.append((start >> 7, start & (TILE - 1), rows, i % 2 * 4 + k, k))
        turned = [
            (block, shift, pltpu.roll(rows, shift, 1), slot) for block, shift, rows, slot, k in turned
        ]
        for block, shift, value, slot in turned:
            tail = jnp.where(lane >= shift, value, 0.0)
            low[slot][block] += tail
            high[slot][block] += value - tail
        return carry

    lax.fori_loop(0, groups, add, 0)
    wide[...] = jnp.zeros_like(wide)
    for b in range(blocks):
        total = jnp.zeros((8, TILE), F32)
        for slot in range(8):
            here = low[slot][b]
            if b:
                here = here + high[slot][b - 1]
            total = total + jnp.where(sub == slot % 4, here, 0.0)
        home = pl.multiple_of((b * 8 + own_ref[0]) * MESSAGE, MESSAGE)
        given = got_ref[pl.ds(home, MESSAGE), :]
        for h in range(2):
            row = total[h : h + 1, :] + total[2 + h : 3 + h, :]
            wide[h * blocks + b : h * blocks + b + 1, TILE : 2 * TILE] = given[6 + h : 7 + h, :] * (
                given[4 + h : 5 + h, :] - row
            )
    centre = wide[:, TILE : 2 * TILE]
    at = lax.broadcasted_iota(jnp.int32, (2 * blocks, TILE), 0) % blocks
    wide[:, :TILE] = jnp.where(at == 0, 0.0, pltpu.roll(centre, 1, 0))
    wide[:, 2 * TILE :] = jnp.where(at == blocks - 1, 0.0, pltpu.roll(centre, 2 * blocks - 1, 0))
    offset = (
        lax.broadcasted_iota(jnp.int32, (3 * TILE, TILE), 1)
        + TILE
        - lax.broadcasted_iota(jnp.int32, (3 * TILE, TILE), 0)
    )
    nonzero = jnp.where(offset == 0, 1, offset).astype(F32)
    ramp = jnp.where((offset & 1) == 1, -1.0 / (math.pi * math.pi * nonzero * nonzero), 0.0)
    ramp = jnp.where(offset == 0, 0.25, ramp)
    ramp = jnp.where(jnp.abs(offset) < TILE, ramp, 0.0)
    done = jnp.dot(wide[...], ramp, precision=lax.Precision.HIGHEST, preferred_element_type=F32)
    wide[:, :TILE] = done.astype(BF16).astype(F32)
    filt[...] = jnp.zeros_like(filt)
    for h in range(2):
        for b in range(blocks):
            row = wide[h * blocks + b : h * blocks + b + 1, :TILE]
            filt[h, b] = jnp.broadcast_to(row, (8, TILE))

    def take(g, carry):
        mixed = []
        for i in range(per):
            for k in range(8):
                start = starts_ref[(g * per + i) * 8 + k]
                block, shift = start >> 7, start & (TILE - 1)
                value = jnp.where(lane >= shift, filt[k % 2, block], filt[k % 2, block + 1])
                mixed.append((value, (TILE - shift) & (TILE - 1)))
        turned = [pltpu.roll(value, shift, 1) for value, shift in mixed]
        for i in range(per):
            rows = turned[i * 8]
            for k in range(1, 8):
                rows = jnp.where(sub == k, turned[i * 8 + k], rows)
            staged[pl.ds(pl.multiple_of((g * per + i) * 8, 8), 8), :] = rows
        return carry

    lax.fori_loop(0, groups, take, 0)
    out_ref[...] = staged[...].astype(BF16)


def backward_kernel(
    table_ref, delta_ref, lanes_ref, got_ref, image_ref, final_ref, left_ref, right_ref,
    rel, band0, band1, shadows, staged, mirror, update, out_ref, image0_ref, image1_ref, sems,
):
    slices = ROWS // 2
    coming = halves_of(image_ref, (image0_ref, image1_ref), sems)
    for copy in coming:
        copy.start()
    pixel = lax.broadcasted_iota(jnp.int32, (PIX, BAND), 0)
    rel[...] = (
        (pixel // SIDE).astype(F32) * lanes_ref[0:1, :]
        + (pixel % SIDE).astype(F32) * lanes_ref[1:2, :]
    )
    staged[...] = got_ref[...].astype(F32)
    mirror[...] = jnp.dot(got_ref[...], reversal(), preferred_element_type=F32)
    for a in range(ANGLES):
        parts = []
        for ref in (staged, mirror):
            for t in range(2):
                row = (a // 2) * 4 + t * 2 + a % 2
                parts.append(ref[pl.ds(row, slices, stride=ROWS), :])
        shadows[a] = jnp.concatenate(parts + parts, axis=0).T

    def build(patch, band):
        shift = delta_ref[pl.ds(patch, 1), :]
        for r in range(0, PIX, 16):
            away = jnp.abs(rel[r : r + 16, :] + shift)
            band[r : r + 16, :] = jnp.maximum(0.0, 1.0 - away).astype(BF16)

    def spread(patch, band, half, col, own):
        pieces = []
        for a in range(ANGLES):
            start = pl.multiple_of(table_ref[patch, a].astype(jnp.int32), 8)
            pieces.append(shadows[a, pl.ds(start, BINS), :])
        seen = jnp.concatenate(pieces, axis=0).astype(BF16)
        got = jnp.dot(band[...], seen, preferred_element_type=F32)
        for u in range(SIDE):
            start = pl.multiple_of((half * SIDE + u) * TILE + col * SIDE, SIDE)
            piece = got[u * SIDE : (u + 1) * SIDE, :]
            if own:
                update[pl.ds(start, SIDE), TILE // 2 :] = piece[:, TILE // 2 :]
            else:
                update[pl.ds(start, SIDE), :] = piece

    def patch_of(i):
        return (i // PATCHES) * 2 * PATCHES + i % PATCHES

    build(0, band0)

    def step(i, carry):
        half = i // PATCHES
        col = i % PATCHES
        patch = patch_of(i)
        build(patch + PATCHES, band1)
        spread(patch, band0, half, col, 0)
        build(patch_of(jnp.minimum(i + 1, 2 * PATCHES - 1)), band0)
        spread(patch + PATCHES, band1, half, col, 1)
        return carry

    lax.fori_loop(0, 2 * PATCHES, step, 0)

    def finish(i, carry):
        u0 = (i // SIDE) * 2 * SIDE + i % SIDE
        u1 = u0 + SIDE
        turned = update[pl.ds(pl.multiple_of(i * TILE, TILE), TILE), :].T
        mirrored = jnp.concatenate([turned[ROWS : 2 * ROWS], turned[3 * ROWS :]], axis=0)
        mirrored = reverse_lanes(mirrored)
        for u, value in (
            (u0, turned[:ROWS]),
            (u1, turned[2 * ROWS : 3 * ROWS]),
            (TILE - 1 - u0, mirrored[:ROWS]),
            (TILE - 1 - u1, mirrored[ROWS:]),
        ):
            for t, ref in enumerate((image0_ref, image1_ref)):
                here = ref[pl.ds(u, slices, stride=TILE), :]
                here = here + 0.25 * value[t * slices : (t + 1) * slices, :]
                out_ref[u, :, t * TILE : (t + 1) * TILE] = here
        return carry

    def leave(start, count, sem):
        spot = pl.ds(start, count)
        return pltpu.make_async_copy(out_ref.at[spot], final_ref.at[spot], sems.at[sem])

    for copy in coming:
        copy.wait()
    lax.fori_loop(0, SIDE, finish, 0, unroll=2)
    going = [leave(0, 2 * SIDE, 2), leave(TILE - 2 * SIDE, 2 * SIDE, 3)]
    for copy in going:
        copy.start()
    lax.fori_loop(SIDE, 2 * SIDE, finish, 0, unroll=2)
    going.append(leave(2 * SIDE, TILE - 4 * SIDE, 4))
    going[-1].start()

    lane = lax.broadcasted_iota(jnp.int32, (slices, TILE), 1)
    per = TILE // TV_STEPS

    def sides(g, carry):
        left = jnp.zeros((slices, TILE), F32)
        right = jnp.zeros((slices, TILE), F32)
        for j in range(per):
            u = g * per + j
            mine = (lane >= j * TV_STEPS) & (lane < (j + 1) * TV_STEPS)
            left = jnp.where(mine, pltpu.roll(out_ref[u, :, :TILE], j * TV_STEPS, 1), left)
            shift = (j + 1) * TV_STEPS % TILE
            right = jnp.where(mine, pltpu.roll(out_ref[u, :, TILE:], shift, 1), right)
        left_ref[g] = left
        right_ref[g] = right
        return carry

    lax.fori_loop(0, TILE // per, sides, 0)
    for copy in going:
        copy.wait()


def smooth_kernel(
    place_ref, before_ref, after_ref, above_ref, below_ref, x_ref,
    out_ref, first, second, out0, out1, sems,
):
    per = TILE // TV_STEPS
    half = TILE // 2
    width = 2 * TILE
    coming = [
        pltpu.make_async_copy(
            x_ref.at[:, pl.ds(h * 8, 8), :],
            first.at[pl.ds(TV_STEPS, TILE), :, pl.ds(h * width, width)],
            sems.at[h],
        )
        for h in range(2)
    ]
    for copy in coming:
        copy.start()
    lane = lax.broadcasted_iota(jnp.int32, (8, TILE), 1)
    has_above, has_below, has_before, has_after = (place_ref[i] for i in range(4))
    folded = lane & (half - 1)
    keep = ((folded < TV_STEPS) & (has_after == 1)) | (
        (folded >= half - TV_STEPS) & (has_before == 1)
    )

    def margin(previous, following, j):
        def spot(value, lanes):
            return pltpu.roll(value, (lanes - j * TV_STEPS) % TILE, 1)

        following = jnp.where(
            lane < half, spot(following[:8], 0), spot(following[8:], half)
        )
        previous = jnp.where(
            lane < half, spot(previous[8:], half - TV_STEPS), spot(previous[:8], -TV_STEPS)
        )
        return jnp.where(keep, jnp.where(folded < TV_STEPS, following, previous), 0.0)

    for r in range(TV_STEPS):
        for ref, start, j in (
            (above_ref, 0, per - TV_STEPS + r),
            (below_ref, TILE + TV_STEPS, r),
        ):
            for h in range(2):
                first[start + r, :, h * width : (h + 1) * width] = ref[r, h * 8 : (h + 1) * 8, :]
            first[start + r, :, 2 * width :] = margin(
                ref[TV_STEPS, :, :TILE], ref[TV_STEPS, :, TILE:], j
            )

    def load(g, carry):
        previous = before_ref[g]
        following = after_ref[g]
        for j in range(per):
            first[g * per + j + TV_STEPS, :, 2 * width :] = margin(previous, following, j)
        return carry

    lax.fori_loop(0, TILE // per, load, 0)
    for copy in coming:
        copy.wait()

    def roll(value, shift):
        return pltpu.roll(value.reshape(-1, TILE), shift, 1).reshape(value.shape)

    def blocks_of(ref, r, count):
        return [ref[pl.ds(r, count), :, i * TILE : (i + 1) * TILE] for i in range(5)]

    end = (lane == TILE - 1)[None]
    middle = (lane == half - 1)[None]

    def next_column(tiles):
        a0, a1, b0, b1, m = (roll(t, TILE - 1) for t in tiles)
        return [
            jnp.where(end, a1, a0),
            jnp.where(end, m, a1),
            jnp.where(end, b1, b0),
            jnp.where(end, roll(tiles[4], half - 1), b1),
            jnp.where(end, a0, jnp.where(middle, roll(tiles[2], half - 1), m)),
        ]

    begin = (lane == 0)[None]
    centre = (lane == half)[None]

    def previous_column(tiles):
        a0, a1, b0, b1, m = (roll(t, 1) for t in tiles)
        return [
            jnp.where(begin, m, a0),
            jnp.where(begin, a0, a1),
            jnp.where(begin, roll(tiles[4], half + 1), b0),
            jnp.where(begin, b0, b1),
            jnp.where(begin, a1, jnp.where(centre, roll(tiles[3], half + 1), m)),
        ]

    def flows(here, under):
        downs, rights = [], []
        for h, u, n in zip(here, under, next_column(here)):
            down = u - h
            right = n - h
            inverse = lax.rsqrt(smoothing * smoothing + down * down + right * right)
            downs.append(down * inverse)
            rights.append(right * inverse)
        return downs, rights

    for k in range(TV_STEPS):
        source, target = (first, second) if k % 2 == 0 else (second, first)
        last = k == TV_STEPS - 1

        def rows(r, count, came, inside, source=source, target=target, last=last):
            here = blocks_of(source, r, count)
            downs, rights = flows(here, blocks_of(source, r + 1, count))
            for i, (h, down, right, left) in enumerate(
                zip(here, downs, rights, previous_column(rights))
            ):
                above = came[i][None]
                if count > 1:
                    above = jnp.concatenate([above, down[:-1]], axis=0)
                fresh = h - descent_step * (above - down + left - right)
                if last:
                    if i < 4:
                        for c in range(count):
                            start = (i // 2) * 8 * TILE + r + c - TV_STEPS
                            (out0, out1)[i % 2][pl.ds(start, 8, stride=TILE), :] = fresh[c]
                    continue
                kept = keep[None] if i == 4 else None
                if inside is not None:
                    kept = inside if kept is None else kept & inside
                if kept is not None:
                    fresh = jnp.where(kept, fresh, 0.0)
                target[pl.ds(r, count), :, i * TILE : (i + 1) * TILE] = fresh
            return [down[count - 1] for down in downs]

        edges = TV_STEPS - 1 - k
        came, unused = flows(blocks_of(source, k, 1), blocks_of(source, k + 1, 1))
        came = [c[0] for c in came]
        if edges:
            came = rows(k + 1, edges, came, has_above == 1)

        def body(i, came):
            return rows(TV_STEPS + i * CHUNK, CHUNK, came, None)

        came = lax.fori_loop(0, TILE // CHUNK, body, came)
        if edges:
            rows(TILE + TV_STEPS, edges, came, has_below == 1)
    going = [
        pltpu.make_async_copy(ref, out_ref.at[:, pl.ds(t * TILE, TILE)], sems.at[t])
        for t, ref in enumerate((out0, out1))
    ]
    for copy in going:
        copy.start()
    for copy in going:
        copy.wait()


def call(kernel, scalars, arrays, left, outs, scratch, flops):
    vmem = pl.BlockSpec(memory_space=VMEM)
    stays = pl.BlockSpec(memory_space=pl.ANY)
    smem = pl.BlockSpec(memory_space=pltpu.SMEM)
    operands = (*scalars, *arrays, *left)
    moved = sum(x.size * x.dtype.itemsize for x in operands)
    big = 1 << 20
    return pl.pallas_call(
        kernel,
        out_shape=outs,
        in_specs=[smem] * len(scalars) + [vmem] * len(arrays) + [stays] * len(left),
        out_specs=jax.tree.map(lambda x: stays if x.size * 4 > big else vmem, outs),
        scratch_shapes=scratch,
        cost_estimate=pl.CostEstimate(flops=flops, bytes_accessed=moved, transcendentals=0),
    )(*operands)


def local(current_image, measured, ray_weight, angle_ids, shadow_start):
    row_index = lax.axis_index("row")
    col_index = lax.axis_index("col")
    rows = lax.axis_size("row")
    cols = lax.axis_size("col")
    slices = current_image.shape[0]
    both = ("row", "col")
    image = current_image.reshape(slices * TILE, 2 * TILE)
    table = geometry(angle_ids)
    half = VMEM((slices * TILE, TILE), F32)
    band = VMEM((BAND, PIX), BF16)

    sent = call(
        forward_kernel,
        (table, col_index.reshape(1)),
        (measured[:, 0], ray_weight[:, 0]),
        (image,),
        jax.ShapeDtypeStruct((rows * cols * MESSAGE, TILE), F32),
        [
            VMEM((2 * SIDE * TILE, TILE), BF16),
            VMEM((BAND, PIX), F32),
            band,
            band,
            VMEM((ANGLES, TILE, TILE), F32),
            VMEM((ANGLES * TILE, TILE), F32),
            half,
            half,
            pltpu.SemaphoreType.DMA((2,)),
        ],
        30_000_000_000,
    )
    got = lax.all_to_all(
        sent.reshape(rows * cols, MESSAGE, TILE), both, split_axis=0, concat_axis=0, tiled=True
    )
    blocks = rows
    starts = shadow_start.reshape(-1, ANGLES)
    starts = lax.dynamic_slice_in_dim(starts, col_index * 2, 2, 1).reshape(-1)
    out = call(
        owner_kernel,
        (starts, col_index.reshape(1)),
        (got.reshape(-1, TILE),),
        (),
        jax.ShapeDtypeStruct((rows * cols * 4, TILE), BF16),
        [
            VMEM((2 * blocks, 3 * TILE), F32),
            VMEM((2, blocks + 1, 8, TILE), F32),
            VMEM((rows * cols * 4, TILE), F32),
        ]
        + [VMEM((blocks, 8, TILE), F32)] * 16,
        10_000_000_000,
    )
    shadows = lax.all_to_all(
        out.reshape(rows * cols, 4, TILE), both, split_axis=0, concat_axis=0, tiled=True
    )
    bins = jnp.arange(BINS, dtype=F32)
    delta_lanes = (table[PAIRS : 2 * PAIRS, :, None] - bins).reshape(-1, BAND)
    angle_lanes = jnp.repeat(table[2 * PAIRS :], BINS, axis=1)
    side = jax.ShapeDtypeStruct((TV_STEPS, slices, TILE), F32)
    whole = VMEM((TILE, slices, 2 * TILE), F32)
    x, left, right = call(
        backward_kernel,
        (table,),
        (delta_lanes, angle_lanes, shadows.reshape(-1, TILE)),
        (image,),
        (jax.ShapeDtypeStruct(whole.shape, F32), side, side),
        [
            VMEM((PIX, BAND), F32),
            VMEM((PIX, BAND), BF16),
            VMEM((PIX, BAND), BF16),
            VMEM((ANGLES, TILE, TILE), F32),
            VMEM((rows * cols * 4, TILE), F32),
            VMEM((rows * cols * 4, TILE), F32),
            VMEM((2 * SIDE * TILE, TILE), F32),
            whole,
            half,
            half,
            pltpu.SemaphoreType.DMA((5,)),
        ],
        30_000_000_000,
    )
    before = lax.ppermute(right, "col", [(i, i + 1) for i in range(cols - 1)])
    after = lax.ppermute(left, "col", [(i + 1, i) for i in range(cols - 1)])
    upward = jnp.concatenate([before[0], after[0]], axis=1)[None]
    downward = jnp.concatenate([before[-1], after[-1]], axis=1)[None]
    top = jnp.concatenate([x[:TV_STEPS], upward], axis=0)
    bottom = jnp.concatenate([x[-TV_STEPS:], downward], axis=0)
    above = lax.ppermute(bottom, "row", [(i, i + 1) for i in range(rows - 1)])
    below = lax.ppermute(top, "row", [(i + 1, i) for i in range(rows - 1)])
    place = jnp.stack(
        [row_index > 0, row_index < rows - 1, col_index > 0, col_index < cols - 1]
    ).astype(jnp.int32)
    wide = VMEM((TILE + 2 * TV_STEPS, 8, 5 * TILE), F32)
    smooth = call(
        smooth_kernel,
        (place,),
        (before, after, above, below),
        (x,),
        jax.ShapeDtypeStruct((slices * TILE, 2 * TILE), F32),
        [wide, wide, half, half, pltpu.SemaphoreType.DMA((2,))],
        10_000_000_000,
    )
    return smooth.reshape(current_image.shape)


def solution(mesh):
    return jax.shard_map(
        local,
        mesh=mesh,
        in_specs=(
            P(None, "row", "col"),
            P("col", "row", None, None),
            P("col", "row", None),
            P(),
            P(),
        ),
        out_specs=P(None, "row", "col"),
        check_vma=False,
    )
```

time: 116 us -> 106 us (0.914)
  Pallas kernels: 55.4 us -> 46.2 us
  other arithmetic: 4.05 us -> 2.74 us
    pallas_call x4, Pallas kernels: 55.4 us -> 46.2 us  [call(): pl.pallas_call(kernel, out_shape=outs, in_specs=[smem] * len(scalars) + [...]
    all_to_all x1, waiting for transfers between devices: 6.91 us -> 8.35 us  [local(): lax.all_to_all(out.reshape(rows * cols, 4, TILE), both, split_axis=0, con...]
    another operation x2 -> x0, other arithmetic: 1.32 us -> none  [local(): angle_lanes = jnp.repeat(jnp.stack([cosine, sine]), BINS, axis=1)]
    squeeze x2 -> x0, local copies, waits for them, and re-layouts: 1.26 us -> none  [the longest x1 0.63 us: local(): below[TV_STEPS]]
where the time goes in v3:
time: 106 us; the launch traced here: 105 us
  Pallas kernels  46.2 us (44%)
  starting transfers between devices  28.6 us (27%)
  waiting for transfers between devices  21.9 us (21%)
  local copies, waits for them, and re-layouts  4.93 us (5%)
  other arithmetic  2.74 us (3%)
    pallas_call x4, Pallas kernels, call(): pl.pallas_call(kernel, out_shape=outs, in_specs=[smem] * len(scalars) + [...  46.2 us
    all_to_all x1, starting transfers between devices, local(): lax.all_to_all(sent.reshape(rows * cols, MESSAGE, TILE), both, split_axis...  10.7 us
    all_to_all x1, waiting for transfers between devices, local(): lax.all_to_all(sent.reshape(rows * cols, MESSAGE, TILE), both, split_axis...  10 us
    all_to_all x1, waiting for transfers between devices, local(): lax.all_to_all(out.reshape(rows * cols, 4, TILE), both, split_axis=0, con...  8.35 us
    all_to_all x1, starting transfers between devices, local(): lax.all_to_all(out.reshape(rows * cols, 4, TILE), both, split_axis=0, con...  6.17 us
    ppermute x1, starting transfers between devices, local(): below = lax.ppermute(top, 'row', [(i + 1, i) for i in range(rows - 1)])  5.27 us
    ppermute x1, waiting for transfers between devices, local(): after = lax.ppermute(left, 'col', [(i + 1, i) for i in range(cols - 1)])  2.6 us
    ppermute x1, starting transfers between devices, local(): before = lax.ppermute(right, 'col', [(i, i + 1) for i in range(cols - 1)])  2.44 us
  transfers between devices with their start and end apart: 6, of which 4 were waited for; matrix products, arithmetic and copies ran while one was open for 4% of the time, Pallas kernels for 0%

profile of v3, /device:TPU:9, one launch (start us, length us, event | category | flops | bytes accessed | tf_op | source)
XLA Modules:
  0.0 104.6 jit_solution(6927813645344197106)
XLA Ops:
  0.0 0.0 copy-start
  0.0 0.7 cosine_multiply_fusion
  0.8 0.8 select_select_fusion.1.table_ref
  1.5 0.0 slice-start
  1.5 0.0 slice-start.1
  1.5 12.5 %shard_map.55 = f32[1024,128]{1,0:T(8,128)} custom-call(f32[66,16]{1,0:T(8,128)} %select_select_fusion.1.table_ref, s32[1]{0:T(128)} %bitcast.5.own_ref, f32[2,16,128]{2,1,0:T(8,128)} %bitcast.33, f32[2,128]{1,0:T(2,128)} %bitcast.34, f32[2048,256]{1,0:T(8,128)} %bitcast.31), custom_call_target="tpu_custom_call" | custom-call | flops 30000001024 | bytes 2118788 | tf_op jit(solution)/shard_map/pallas_call | solution.py:525
  14.0 10.7 %all-to-all-start = ((f32[128,8,128]{2,1,0:T(8,128)}), f32[128,8,128]{2,1,0:T(8,128)S(1)}, u32[]{:S(2)}, u32[]{:S(2)}) async-start(f32[128,8,128]{2,1,0:T(8,128)} %bitcast.28), calls=%async_computation | async-start | bytes 1048576 | tf_op jit(solution)/shard_map/all_to_all | solution.py:566
  24.8 0.1 sub.52
  24.9 0.0 slice-done
  24.9 0.1 broadcast_in_dim.18
  24.9 0.7 reshape.44.lanes_ref
  25.6 0.0 copy-done
  25.6 0.1 constant_dynamic-slice_fusion
  25.7 0.7 reshape.46.starts_ref
  26.5 0.0 slice-done.1
  26.5 0.1 sub.49
  26.6 0.2 sub.50
  26.7 10.0 %all-to-all-done = f32[128,8,128]{2,1,0:T(8,128)S(1)} async-done(((f32[128,8,128]{2,1,0:T(8,128)}), f32[128,8,128]{2,1,0:T(8,128)S(1)}, u32[]{:S(2)}, u32[]{:S(2)}) %all-to-all-start) | async-done | bytes 524320 | tf_op jit(solution)/shard_map/all_to_all | solution.py:566
  36.8 0.0 copy-start.1
  36.8 0.8 copy-done.1
  37.6 5.2 %shard_map.56 = bf16[512,128]{1,0:T(8,128)(2,1)} custom-call(s32[512]{0:T(512)} %reshape.46.starts_ref, s32[1]{0:T(128)} %bitcast.5.own_ref, f32[1024,128]{1,0:T(8,128)} %bitcast.27), custom_call_target="tpu_custom_call" | custom-call | flops 10000000000 | bytes 526340 | tf_op jit(solution)/shard_map/pallas_call | solution.py:525
  42.7 6.2 %all-to-all-start.1 = ((bf16[128,4,128]{2,1,0:T(4,128)(2,1)}), bf16[128,4,128]{2,1,0:T(4,128)(2,1)S(1)}, u32[]{:S(2)}, u32[]{:S(2)}) async-start(bf16[128,4,128]{2,1,0:T(4,128)(2,1)} %bitcast.30), calls=%async_computation.1 | async-start | bytes 262144 | tf_op jit(solution)/shard_map/all_to_all | solution.py:586
  48.9 0.6 broadcast_subtract_fusion.delta_ref
  49.5 8.4 %all-to-all-done.1 = bf16[128,4,128]{2,1,0:T(4,128)(2,1)S(1)} async-done(((bf16[128,4,128]{2,1,0:T(4,128)(2,1)}), bf16[128,4,128]{2,1,0:T(4,128)(2,1)S(1)}, u32[]{:S(2)}, u32[]{:S(2)}) %all-to-all-start.1) | async-done | bytes 131104 | tf_op jit(solution)/shard_map/all_to_all | solution.py:586
  57.9 0.0 copy-start.2
  57.9 0.7 copy-done.2
  58.5 12.8 %shard_map.57 = (f32[128,16,256]{2,1,0:T(8,128)}, f32[4,16,128]{2,1,0:T(8,128)}, f32[4,16,128]{2,1,0:T(8,128)}) custom-call(f32[66,16]{1,0:T(8,128)} %select_select_fusion.1.table_ref, f32[32,384]{1,0:T(8,128)} %broadcast_subtract_fusion.delta_ref, f32[2,384]{1,0:T(2,128)} %reshape.44.lanes_ref, bf16[512,128]{1,0:T(8,128)(2,1)} %bitcast.29, f32[2048,256]{1,0:T(8,128)} %bitcast.32), custom_call_target="tpu_custom_call" | custom-call | flops 30000001024 | bytes 2284672 | tf_op jit(solution)/shard_map/pallas_call | solution.py:525
  71.3 2.4 %collective-permute-start = (f32[4,16,128]{2,1,0:T(8,128)}, f32[4,16,128]{2,1,0:T(8,128)S(1)}, u32[]{:S(2)}, u32[]{:S(2)}) collective-permute-start(f32[4,16,128]{2,1,0:T(8,128)} %get-tuple-element.8), channel_id=1, source_target_pairs={{0,1},{1,2},{2,3},{3,4},{4,5},{5,6},{6,7},{8,9},{9,10},{10,11},{11... | collective-permute-start | bytes 98312 | tf_op jit(solution)/shard_map/ppermute | solution.py:615
  73.8 1.9 %collective-permute-start.1 = (f32[4,16,128]{2,1,0:T(8,128)}, f32[4,16,128]{2,1,0:T(8,128)S(1)}, u32[]{:S(2)}, u32[]{:S(2)}) collective-permute-start(f32[4,16,128]{2,1,0:T(8,128)} %get-tuple-element.9), channel_id=1, source_target_pairs={{1,0},{2,1},{3,2},{4,3},{5,4},{6,5},{7,6},{9,8},{10,9},{11,10},{12... | collective-permute-start | bytes 98312 | tf_op jit(solution)/shard_map/ppermute | solution.py:616
  75.7 0.9 fusion.14
  76.6 0.0 collective-permute-done.before_ref
  76.6 0.0 copy-start.3
  76.6 2.6 %collective-permute-done.1.after_ref = f32[4,16,128]{2,1,0:T(8,128)S(1)} collective-permute-done((f32[4,16,128]{2,1,0:T(8,128)}, f32[4,16,128]{2,1,0:T(8,128)S(1)}, u32[]{:S(2)}, u32[]{:S(2)}) %collective-permute-start.1) | collective-permute-done | bytes 32800 | tf_op jit(solution)/shard_map/ppermute | solution.py:616
  79.2 0.0 copy-start.4
  79.2 2.1 %collective-permute-start.2 = (f32[5,16,256]{2,1,0:T(8,128)S(1)}, f32[5,16,256]{2,1,0:T(8,128)S(1)}, u32[]{:S(2)}, u32[]{:S(2)}) collective-permute-start(f32[5,16,256]{2,1,0:T(8,128)S(1)} %pad_maximum_fusion), channel_id=1, source_target_pairs={{0,8},{8,16},{16,24},{24,32},{32,40},{40,48},{48,56},{56,64},{64,7... | collective-permute-start | bytes 245768 | tf_op jit(solution)/shard_map/ppermute | solution.py:621
  81.4 5.3 %collective-permute-start.3 = (f32[5,16,256]{2,1,0:T(8,128)S(1)}, f32[5,16,256]{2,1,0:T(8,128)S(1)}, u32[]{:S(2)}, u32[]{:S(2)}) collective-permute-start(f32[5,16,256]{2,1,0:T(8,128)S(1)} %pad_maximum_fusion.1), channel_id=1, source_target_pairs={{8,0},{16,8},{24,16},{32,24},{40,32},{48,40},{56,48},{64,56},{72,6... | collective-permute-start | bytes 245768 | tf_op jit(solution)/shard_map/ppermute | solution.py:622
  86.7 0.6 add_convert_fusion.place_ref
  87.2 0.0 collective-permute-done.2.above_ref
  87.2 0.0 copy-start.5
  87.2 0.9 collective-permute-done.3.below_ref
  88.1 0.0 copy-done.3
  88.1 0.0 copy-done.4
  88.1 0.0 copy-done.5
  88.1 0.0 copy-start.6
  88.1 0.6 copy-done.6
  88.8 15.8 %shard_map.58 = f32[2048,256]{1,0:T(8,128)} custom-call(s32[4]{0:T(128)} %add_convert_fusion.place_ref, f32[4,16,128]{2,1,0:T(8,128)} %copy-done.3, f32[4,16,128]{2,1,0:T(8,128)} %copy-done.4, f32[5,16,256]{2,1,0:T(8,128)} %copy-done.5, f32[5,16,256]{2,1,0:T(8,128)} %copy-done.6, f32[128,16,256]{2,1,0:T(8,128)} %get-tuple-element.10.x_ref), custom_call_target="tpu_custom_call" | custom-call | flops 10000000000 | bytes 2326544 | tf_op jit(solution)/shard_map/pallas_call | solution.py:525
  (10 shorter events, 0.1 us)
Async XLA Ops:
  0.0 25.6 %copy-start = (s32[16,16,16]{2,1,0:T(8,128)S(1)}, s32[16,16,16]{2,1,0:T(8,128)}, u32[]{:S(2)}) copy-start(s32[16,16,16]{2,1,0:T(8,128)} %param.9) | copy-start | bytes 49156
  1.5 23.3 %slice-start = ((f32[66,16]{1,0:T(8,128)}), f32[2,16]{1,0:T(2,128)S(1)}, s32[]{:S(2)}) async-start(f32[66,16]{1,0:T(8,128)} %select_select_fusion.1.table_ref), calls=%async_computation.2 | async-start | bytes 2048 | tf_op jit(solution)/shard_map/slice | solution.py:591
  1.5 24.9 %slice-start.1 = ((f32[66,16]{1,0:T(8,128)}), f32[32,16]{1,0:T(8,128)S(1)}, s32[]{:S(2)}) async-start(f32[66,16]{1,0:T(8,128)} %select_select_fusion.1.table_ref), calls=%async_computation.3 | async-start | bytes 32768 | tf_op jit(solution)/shard_map/slice | solution.py:590
  14.0 22.8 %all-to-all-start = ((f32[128,8,128]{2,1,0:T(8,128)}), f32[128,8,128]{2,1,0:T(8,128)S(1)}, u32[]{:S(2)}, u32[]{:S(2)}) async-start(f32[128,8,128]{2,1,0:T(8,128)} %bitcast.28), calls=%async_computation | async-start | bytes 1048576 | tf_op jit(solution)/shard_map/all_to_all | solution.py:566
  36.8 0.8 copy-start.1
  42.7 15.2 %all-to-all-start.1 = ((bf16[128,4,128]{2,1,0:T(4,128)(2,1)}), bf16[128,4,128]{2,1,0:T(4,128)(2,1)S(1)}, u32[]{:S(2)}, u32[]{:S(2)}) async-start(bf16[128,4,128]{2,1,0:T(4,128)(2,1)} %bitcast.30), calls=%async_computation.1 | async-start | bytes 262144 | tf_op jit(solution)/shard_map/all_to_all | solution.py:586
  57.9 0.7 copy-start.2
  71.3 5.3 %collective-permute-start = (f32[4,16,128]{2,1,0:T(8,128)}, f32[4,16,128]{2,1,0:T(8,128)S(1)}, u32[]{:S(2)}, u32[]{:S(2)}) collective-permute-start(f32[4,16,128]{2,1,0:T(8,128)} %get-tuple-element.8), channel_id=1, source_target_pairs={{0,1},{1,2},{2,3},{3,4},{4,5},{5,6},{6,7},{8,9},{9,10},{10,11},{11... | collective-permute-start | bytes 98312 | tf_op jit(solution)/shard_map/ppermute | solution.py:615
  73.8 5.4 %collective-permute-start.1 = (f32[4,16,128]{2,1,0:T(8,128)}, f32[4,16,128]{2,1,0:T(8,128)S(1)}, u32[]{:S(2)}, u32[]{:S(2)}) collective-permute-start(f32[4,16,128]{2,1,0:T(8,128)} %get-tuple-element.9), channel_id=1, source_target_pairs={{1,0},{2,1},{3,2},{4,3},{5,4},{6,5},{7,6},{9,8},{10,9},{11,10},{12... | collective-permute-start | bytes 98312 | tf_op jit(solution)/shard_map/ppermute | solution.py:616
  76.6 11.5 %copy-start.3 = (f32[4,16,128]{2,1,0:T(8,128)}, f32[4,16,128]{2,1,0:T(8,128)S(1)}, u32[]{:S(2)}) copy-start(f32[4,16,128]{2,1,0:T(8,128)S(1)} %collective-permute-done.before_ref) | copy-start | bytes 98308
  79.2 8.9 %copy-start.4 = (f32[4,16,128]{2,1,0:T(8,128)}, f32[4,16,128]{2,1,0:T(8,128)S(1)}, u32[]{:S(2)}) copy-start(f32[4,16,128]{2,1,0:T(8,128)S(1)} %collective-permute-done.1.after_ref) | copy-start | bytes 98308
  79.2 8.0 %collective-permute-start.2 = (f32[5,16,256]{2,1,0:T(8,128)S(1)}, f32[5,16,256]{2,1,0:T(8,128)S(1)}, u32[]{:S(2)}, u32[]{:S(2)}) collective-permute-start(f32[5,16,256]{2,1,0:T(8,128)S(1)} %pad_maximum_fusion), channel_id=1, source_target_pairs={{0,8},{8,16},{16,24},{24,32},{32,40},{40,48},{48,56},{56,64},{64,7... | collective-permute-start | bytes 245768 | tf_op jit(solution)/shard_map/ppermute | solution.py:621
  81.4 6.7 %collective-permute-start.3 = (f32[5,16,256]{2,1,0:T(8,128)S(1)}, f32[5,16,256]{2,1,0:T(8,128)S(1)}, u32[]{:S(2)}, u32[]{:S(2)}) collective-permute-start(f32[5,16,256]{2,1,0:T(8,128)S(1)} %pad_maximum_fusion.1), channel_id=1, source_target_pairs={{8,0},{16,8},{24,16},{32,24},{40,32},{48,40},{56,48},{64,56},{72,6... | collective-permute-start | bytes 245768 | tf_op jit(solution)/shard_map/ppermute | solution.py:622
  87.2 0.9 copy-start.5
  88.1 0.6 copy-start.6

commit v4 on v3

v4 whole, which is shorter than its diff:
```python
import functools
import math

import jax
import jax.numpy as jnp
from jax import lax
from jax.experimental import pallas as pl
from jax.experimental.pallas import tpu as pltpu
from jax.sharding import PartitionSpec as P

TILE = 128
ANGLES = 16
ALL_ANGLES = 256
TV_STEPS = 4
SIDE = 16
PATCHES = TILE // SIDE
PIX = SIDE * SIDE
BINS = 24
ROWS = 32
BAND = ANGLES * BINS
PAIRS = PATCHES * PATCHES // 2
MESSAGE = 8

inverse_root = 0.7071067811865476
smoothing = 0.25
descent_step = 0.05

VMEM = pltpu.VMEM
F32 = jnp.float32
BF16 = jnp.bfloat16


def geometry(angle_ids):
    radians = angle_ids.astype(F32) * (math.pi / ALL_ANGLES)
    cosine = jnp.cos(radians)[None] * inverse_root
    sine = jnp.sin(radians)[None] * inverse_root
    row = lax.broadcasted_iota(jnp.int32, (2 * PAIRS + 2, ANGLES), 0)
    patch = row % PAIRS
    down = (patch // PATCHES).astype(F32) * SIDE - (TILE - 1) / 2.0
    across = (patch % PATCHES).astype(F32) * SIDE - (TILE - 1) / 2.0
    corner = TILE / 2.0 + down * cosine + across * sine
    low = corner + (SIDE - 1) * (jnp.minimum(cosine, 0.0) + jnp.minimum(sine, 0.0))
    base = jnp.clip(jnp.floor((jnp.floor(low - 1.5) + 1.0) / 8.0) * 8.0, 0.0, TILE - BINS)
    delta = corner - base - 0.5
    ends = jnp.where(row == 2 * PAIRS, cosine, sine)
    return jnp.where(row < PAIRS, base, jnp.where(row < 2 * PAIRS, delta, ends))


def reversal():
    there = lax.broadcasted_iota(jnp.int32, (TILE, TILE), 0)
    here = lax.broadcasted_iota(jnp.int32, (TILE, TILE), 1)
    return jnp.where(there + here == TILE - 1, 1.0, 0.0).astype(BF16)


def reverse_lanes(value):
    high = value.astype(BF16)
    low = (value - high.astype(F32)).astype(BF16)
    both = jnp.concatenate([high, low], axis=1)
    turn = reversal()
    return jnp.dot(both, jnp.concatenate([turn, turn], axis=0), preferred_element_type=F32)


def pipeline(build, use, bands):
    def pair(i, action, slots):
        half = i // PATCHES
        col = i % PATCHES
        for own in range(2):
            patch = (2 * half + own) * PATCHES + col
            if action is build:
                build(patch, bands.at[slots + own])
            else:
                use(patch, bands.at[slots + own], half, col, own)

    pair(0, build, 0)

    def step(i, carry):
        pair(2 * i + 1, build, 2)
        pair(2 * i, use, 0)
        pair(jnp.minimum(2 * i + 2, 2 * PATCHES - 1), build, 0)
        pair(2 * i + 1, use, 2)
        return carry

    lax.fori_loop(0, PATCHES, step, 0)


def blocks_at(half):
    return 2 * half, PATCHES - 1 - 2 * half, 2 * half + 1, PATCHES - 2 - 2 * half


def reflected(ref, i):
    other = (i // SIDE) * SIDE + SIDE - 1 - i % SIDE
    back = 7 - lax.broadcasted_iota(jnp.int32, (8, TILE), 0)
    mirrored = lax.broadcasted_iota(jnp.int32, (8, TILE), 1) & ROWS != 0
    parts = []
    for g in range(TILE // 8):
        far = ref[other, TILE - 8 * (g + 1) : TILE - 8 * g, :]
        far = jnp.take_along_axis(far, back, axis=0)
        parts.append(jnp.where(mirrored, far, ref[i, 8 * g : 8 * (g + 1), :]))
    return jnp.concatenate(parts, axis=0)


def halves_of(image, targets, sems):
    return [
        pltpu.make_async_copy(image.at[:, pl.ds(t * TILE, TILE)], target, sems.at[t])
        for t, target in enumerate(targets)
    ]


def forward_kernel(
    table_ref, own_ref, measured_ref, weight_ref, image_ref,
    out_ref, turned_ref, xt, rel, bands, tails, message, image0_ref, image1_ref, flat, sems,
    *sums,
):
    coming = halves_of(image_ref, (image0_ref, image1_ref), sems)
    for copy in coming:
        copy.start()
    slices = ROWS // 2
    lane = lax.broadcasted_iota(jnp.int32, (BINS, PIX), 1)
    bin_at = lax.broadcasted_iota(jnp.int32, (BINS, PIX), 0).astype(F32)
    down = (lane // SIDE).astype(F32)
    across = (lane % SIDE).astype(F32)
    for a in range(ANGLES):
        rel[a * BINS : (a + 1) * BINS, :] = (
            down * table_ref[2 * PAIRS, a] + across * table_ref[2 * PAIRS + 1, a] - bin_at
        )
    for ref in sums:
        ref[...] = jnp.zeros_like(ref)
    for copy in coming:
        copy.wait()

    def rows_of(u):
        return [ref[pl.ds(u, slices, stride=TILE), :] for ref in (image0_ref, image1_ref)]

    def flip(i, carry):
        rows = []
        for block in blocks_at(i // SIDE):
            rows += rows_of(block * SIDE + i % SIDE)
        flat[i] = jnp.concatenate(rows, axis=0).T
        return carry

    lax.fori_loop(0, 2 * SIDE, flip, 0, unroll=4)
    going = pltpu.make_async_copy(flat, turned_ref, sems.at[2])
    going.start()

    def reflect(i, carry):
        value = reflected(flat, i)
        xt[pl.ds(pl.multiple_of(i * TILE, TILE), TILE), :] = value.astype(BF16)
        return carry

    lax.fori_loop(0, 2 * SIDE, reflect, 0, unroll=2)

    def build(patch, band):
        for a in range(0, ANGLES, 2):
            pair = []
            for b in (a, a + 1):
                away = jnp.abs(rel[b * BINS : (b + 1) * BINS, :] + table_ref[PAIRS + patch, b])
                pair.append(jnp.maximum(0.0, 1.0 - away))
            band[a * BINS : (a + 2) * BINS, :] = jnp.concatenate(pair, axis=0).astype(BF16)

    first_half = lax.broadcasted_iota(jnp.int32, (PIX, TILE), 1) < TILE // 2

    def project(patch, band, half, col, own):
        pieces = []
        for u in range(SIDE):
            start = pl.multiple_of((half * SIDE + u) * TILE + col * SIDE, SIDE)
            pieces.append(xt[pl.ds(start, SIDE), :])
        pixels = jnp.concatenate(pieces, axis=0)
        nothing = jnp.zeros_like(pixels)
        pixels = jnp.where(first_half, *((nothing, pixels) if own else (pixels, nothing)))
        got = jnp.dot(band[...], pixels, preferred_element_type=F32)
        for a in range(ANGLES):
            start = pl.multiple_of(table_ref[patch, a].astype(jnp.int32), 8)
            sums[a][pl.ds(start, BINS), :] += got[a * BINS : (a + 1) * BINS, :]

    pipeline(build, project, bands)
    stride = MESSAGE * ANGLES // 2
    for a in range(ANGLES):
        tails[a * TILE : (a + 1) * TILE, :] = sums[a][...].T * 0.03125
    mirrored = [
        tails[a * TILE + ROWS : a * TILE + 2 * ROWS, :]
        + tails[a * TILE + 3 * ROWS : (a + 1) * TILE, :]
        for a in range(ANGLES)
    ]
    mirrored = reverse_lanes(jnp.concatenate(mirrored, axis=0))
    for a in range(ANGLES):
        total = tails[a * TILE : a * TILE + ROWS, :] + tails[a * TILE + 2 * ROWS : a * TILE + 3 * ROWS, :]
        total = total + mirrored[a * ROWS : (a + 1) * ROWS, :]
        for t in range(2):
            row = (a // 2) * MESSAGE + t * 2 + a % 2
            message[pl.ds(row, slices, stride=stride), :] = total[t * slices : (t + 1) * slices, :]
    row = own_ref[0] * MESSAGE + 4
    for h in range(2):
        message[pl.ds(row + h, slices, stride=stride), :] = measured_ref[h]
        weight = jnp.broadcast_to(weight_ref[h : h + 1, :], (slices, TILE))
        message[pl.ds(row + 2 + h, slices, stride=stride), :] = weight
    out_ref[...] = message[...].astype(BF16)
    going.wait()


def owner_kernel(
    starts_ref, own_ref, sent_ref, out_ref, wide, filt, staged, ramp_ref, got_ref, came, sem, *sums
):
    coming = pltpu.make_async_copy(sent_ref, came, sem)
    coming.start()
    low, high = sums[:8], sums[8:]
    blocks = 16
    per = 8
    groups = staged.shape[0] // (8 * per)
    for ref in sums:
        ref[...] = jnp.zeros_like(ref)
    lane = lax.broadcasted_iota(jnp.int32, (8, TILE), 1)
    sub = lax.broadcasted_iota(jnp.int32, (8, TILE), 0)

    offset = (
        lax.broadcasted_iota(jnp.int32, (3 * TILE, TILE), 1)
        + TILE
        - lax.broadcasted_iota(jnp.int32, (3 * TILE, TILE), 0)
    )
    nonzero = jnp.where(offset == 0, 1, offset).astype(F32)
    ramp = jnp.where((offset & 1) == 1, -1.0 / (math.pi * math.pi * nonzero * nonzero), 0.0)
    ramp = jnp.where(offset == 0, 0.25, ramp)
    ramp = jnp.where(jnp.abs(offset) < TILE, ramp, 0.0)
    ramp_ref[...] = ramp
    coming.wait()
    got_ref[...] = came[...].astype(F32)

    def add(g, carry):
        turned = []
        for i in range(2 * per):
            source = g * 2 * per + i
            rows = got_ref[pl.ds(pl.multiple_of(source * MESSAGE, MESSAGE), MESSAGE), :]
            for k in range(4):
                start = starts_ref[source * 4 + k]
                turned.append((start >> 7, start & (TILE - 1), rows, i % 2 * 4 + k, k))
        turned = [
            (block, shift, pltpu.roll(rows, shift, 1), slot) for block, shift, rows, slot, k in turned
        ]
        for block, shift, value, slot in turned:
            tail = jnp.where(lane >= shift, value, 0.0)
            low[slot][block] += tail
            high[slot][block] += value - tail
        return carry

    lax.fori_loop(0, groups, add, 0)
    wide[...] = jnp.zeros_like(wide)
    for b in range(blocks):
        total = jnp.zeros((8, TILE), F32)
        for slot in range(8):
            here = low[slot][b]
            if b:
                here = here + high[slot][b - 1]
            total = total + jnp.where(sub == slot % 4, here, 0.0)
        home = pl.multiple_of((b * 8 + own_ref[0]) * MESSAGE, MESSAGE)
        given = got_ref[pl.ds(home, MESSAGE), :]
        for h in range(2):
            row = total[h : h + 1, :] + total[2 + h : 3 + h, :]
            wide[h * blocks + b : h * blocks + b + 1, TILE : 2 * TILE] = given[6 + h : 7 + h, :] * (
                given[4 + h : 5 + h, :] - row
            )
    centre = wide[:, TILE : 2 * TILE]
    at = lax.broadcasted_iota(jnp.int32, (2 * blocks, TILE), 0) % blocks
    wide[:, :TILE] = jnp.where(at == 0, 0.0, pltpu.roll(centre, 1, 0))
    wide[:, 2 * TILE :] = jnp.where(at == blocks - 1, 0.0, pltpu.roll(centre, 2 * blocks - 1, 0))
    done = jnp.dot(wide[...], ramp_ref[...], precision=lax.Precision.HIGHEST, preferred_element_type=F32)
    wide[:, :TILE] = done.astype(BF16).astype(F32)
    filt[...] = jnp.zeros_like(filt)
    for h in range(2):
        for b in range(blocks):
            row = wide[h * blocks + b : h * blocks + b + 1, :TILE]
            filt[h, b] = jnp.broadcast_to(row, (8, TILE))

    def take(g, carry):
        mixed = []
        for i in range(per):
            for k in range(8):
                start = starts_ref[(g * per + i) * 8 + k]
                block, shift = start >> 7, start & (TILE - 1)
                value = jnp.where(lane >= shift, filt[k % 2, block], filt[k % 2, block + 1])
                mixed.append((value, (TILE - shift) & (TILE - 1)))
        turned = [pltpu.roll(value, shift, 1) for value, shift in mixed]
        for i in range(per):
            rows = turned[i * 8]
            for k in range(1, 8):
                rows = jnp.where(sub == k, turned[i * 8 + k], rows)
            staged[pl.ds(pl.multiple_of((g * per + i) * 8, 8), 8), :] = rows
        return carry

    lax.fori_loop(0, groups, take, 0)
    out_ref[...] = staged[...].astype(BF16)


def backward_kernel(
    table_ref, delta_ref, lanes_ref, image_ref, sent_ref,
    final_ref, left_ref, right_ref, top_ref, bottom_ref,
    rel, bands, shadows, staged, mirror, update, image, got_ref, sems,
):
    slices = ROWS // 2
    arriving = pltpu.make_async_copy(sent_ref, got_ref, sems.at[1])
    arriving.start()
    coming = pltpu.make_async_copy(image_ref, image, sems.at[0])
    coming.start()
    pixel = lax.broadcasted_iota(jnp.int32, (PIX, BAND), 0)
    rel[...] = (
        (pixel // SIDE).astype(F32) * lanes_ref[0:1, :]
        + (pixel % SIDE).astype(F32) * lanes_ref[1:2, :]
    )
    arriving.wait()
    staged[...] = got_ref[...].astype(F32)
    mirror[...] = jnp.dot(got_ref[...], reversal(), preferred_element_type=F32)
    for a in range(ANGLES):
        parts = []
        for ref in (staged, mirror):
            for t in range(2):
                row = (a // 2) * 4 + t * 2 + a % 2
                parts.append(ref[pl.ds(row, slices, stride=ROWS), :])
        shadows[a] = jnp.concatenate(parts + parts, axis=0).T

    def build(patch, band):
        shift = delta_ref[pl.ds(patch, 1), :]
        for r in range(0, PIX, 16):
            away = jnp.abs(rel[r : r + 16, :] + shift)
            band[r : r + 16, :] = jnp.maximum(0.0, 1.0 - away).astype(BF16)

    def spread(patch, band, half, col, own):
        pieces = []
        for a in range(ANGLES):
            start = pl.multiple_of(table_ref[patch, a].astype(jnp.int32), 8)
            pieces.append(shadows[a, pl.ds(start, BINS), :])
        seen = jnp.concatenate(pieces, axis=0).astype(BF16)
        got = jnp.dot(band[...], seen, preferred_element_type=F32)
        for u in range(SIDE):
            spot = pl.ds(pl.multiple_of(col * SIDE, SIDE), SIDE)
            piece = got[u * SIDE : (u + 1) * SIDE, :]
            if own:
                update[half * SIDE + u, spot, TILE // 2 :] = piece[:, TILE // 2 :]
            else:
                update[half * SIDE + u, spot, :] = piece

    pipeline(build, spread, bands)

    coming.wait()

    def finish(i, carry):
        image[i] = image[i] + 0.25 * reflected(update, i)
        return carry

    lax.fori_loop(0, SIDE, finish, 0, unroll=2)
    going = [
        pltpu.make_async_copy(
            image.at[pl.ds(h * SIDE, SIDE)], final_ref.at[pl.ds(h * SIDE, SIDE)], sems.at[h]
        )
        for h in range(2)
    ]
    going[0].start()
    lax.fori_loop(SIDE, 2 * SIDE, finish, 0, unroll=2)
    going[1].start()
    lane = lax.broadcasted_iota(jnp.int32, (8, TILE), 1)
    sub = lax.broadcasted_iota(jnp.int32, (8, TILE), 0)
    second = lane & slices != 0

    def column(u, start, far):
        value = [image[h * SIDE + u, start : start + 8, :] for h in range(2)]
        value[far] = pltpu.roll(value[far], 4, 0)
        return jnp.where(sub < 4, value[0], value[1])

    for u in range(8):
        here, there = column(u, 0, 1), column(u + 8, 0, 1)
        left_ref[u] = jnp.where(second, pltpu.roll(there, slices, 1), here)
        here, there = column(u, TILE - 8, 0), column(u + 8, TILE - 8, 0)
        right_ref[u] = jnp.where(second, here, pltpu.roll(there, TILE - slices, 1))
    lanes = lax.broadcasted_iota(jnp.int32, (TILE, TILE), 1) // ROWS
    for ref, row, shift in ((top_ref, 0, 0), (bottom_ref, SIDE - TV_STEPS, TILE - ROWS)):
        packed = jnp.zeros((TILE, TILE), F32)
        for k in range(TV_STEPS):
            turned = pltpu.roll(image[row + k], (k * ROWS + shift) % TILE, 1)
            packed = jnp.where(lanes == k, turned, packed)
        ref[...] = packed.reshape(TILE // 8, 8, TILE)
    for copy in going:
        copy.wait()


def smooth_kernel(half, place_ref, before_ref, after_ref, *refs):
    if half == 0:
        above_ref, below_ref, x_ref, unused, out_ref = refs[:5]
    else:
        x_ref, out_ref = refs[:2]
    first, second, other, flow, out0, out1, sems = refs[-7:]
    slices = ROWS // 2
    own = pl.ds(16, TILE)
    wide = TILE + 16
    last_rows = SIDE - TV_STEPS
    coming = [
        pltpu.make_async_copy(
            x_ref.at[pl.ds(start, count)], ref.at[pl.ds(row, count), own, :], sems.at[i]
        )
        for i, (start, count, ref, row) in enumerate(
            (
                (half * SIDE, SIDE, first, TV_STEPS),
                ((1 - half) * SIDE, TV_STEPS, other, 0),
                ((1 - half) * SIDE + last_rows, TV_STEPS, other, TV_STEPS),
            )
        )
    ]
    for copy in coming:
        copy.start()
    lane = lax.broadcasted_iota(jnp.int32, (8, TILE), 1)
    later = lane & slices != 0
    has_above, has_below, has_before, has_after = (place_ref[i] for i in range(4))

    def roll(value, shift):
        return pltpu.roll(value, shift % TILE, 1)

    def sink(value):
        return pltpu.roll(value, 4, 0)

    if half == 0:
        for ref, row, shift, left, right in (
            (above_ref, 0, 0, -ROWS, -ROWS),
            (below_ref, SIDE + TV_STEPS, ROWS, slices, ROWS + slices),
        ):
            for k in range(TV_STEPS):
                back = shift - k * ROWS
                lead = jnp.where(
                    later,
                    roll(ref[TILE // 8 - 1], back + slices),
                    sink(roll(ref[TILE // 8 + k], left)),
                )
                trail = jnp.where(
                    later,
                    roll(ref[TILE // 8 + TV_STEPS + k], right),
                    roll(ref[0], back - slices),
                )
                first[row + k, 8:16, :] = lead
                for g in range(TILE // 8):
                    first[row + k, 16 + 8 * g : 24 + 8 * g, :] = roll(ref[g], back)
                first[row + k, 16 + TILE : 24 + TILE, :] = trail
    for copy in coming:
        copy.wait()
    sides = [(first, u + TV_STEPS, u, half) for u in range(SIDE)]
    sides += [(other, k, k, 1 - half) for k in range(TV_STEPS)]
    sides += [(other, TV_STEPS + k, last_rows + k, 1 - half) for k in range(TV_STEPS)]
    for ref, row, u, h in sides:
        before = before_ref[u % 8]
        after = after_ref[u % 8]
        if u < 8:
            before, after = roll(before, -slices), roll(after, slices)
        if h:
            after = sink(after)
        else:
            before = sink(before)
        lead = jnp.where(later, roll(ref[row, 8 + TILE : 16 + TILE, :], slices), before)
        trail = jnp.where(later, after, roll(ref[row, 16:24, :], -slices))
        ref[row, 8:16, :] = lead
        ref[row, 16 + TILE : 24 + TILE, :] = trail

    group = lax.broadcasted_iota(jnp.int32, (wide, TILE), 1) // ROWS
    span = pl.ds(8, wide)
    for k in range(TV_STEPS):
        for mine, others, target, low in (
            (SIDE + k, TV_STEPS + k, k, True),
            (TV_STEPS + k, k, SIDE + TV_STEPS + k, False),
        ):
            mine = first[mine, span, :]
            others = roll(other[others, span, :], 2 * ROWS)
            swapped = roll(mine, 2 * ROWS)
            if half == 0:
                value = jnp.where(group == (3 if low else 2), others, swapped)
                outer = group == (0 if low else 1)
                value = jnp.where(outer, first[target, span, :], value)
            else:
                step = roll(mine, ROWS if low else -ROWS)
                value = jnp.where(group == (3 if low else 2), step, swapped)
                value = jnp.where(group == (0 if low else 1), others, value)
            first[target, span, :] = value

    keep_lead = later | (has_before == 1)
    keep_trail = jnp.logical_not(later) | (has_after == 1)

    def flows(source, r):
        here = source[r, span, :]
        down = source[r + 1, span, :] - here
        right = source[r, pl.ds(9, wide), :] - here
        inverse = lax.rsqrt(smoothing * smoothing + down * down + right * right)
        return here, down * inverse, right * inverse

    for k in range(TV_STEPS):
        source, target = (first, second) if k % 2 == 0 else (second, first)
        last = k == TV_STEPS - 1

        def row(r, came, slot, inside=None, source=source, target=target, last=last):
            here, down, right = flows(source, r)
            flow[slot, span, :] = right
            left = flow[slot, pl.ds(7, wide), :]
            fresh = here - descent_step * (came - down + left - right)
            if last:
                turned = fresh[8 : 8 + TILE, :].T
                for g, block in enumerate(blocks_at(half)):
                    spot = pl.ds(block * SIDE + r - TV_STEPS, slices, stride=TILE)
                    for t, ref in enumerate((out0, out1)):
                        start = g * ROWS + t * slices
                        ref[spot, :] = turned[start : start + slices, :]
                return down
            if inside is not None:
                fresh = jnp.where(inside, fresh, 0.0)
            target[r, 8:16, :] = jnp.where(keep_lead, fresh[:8, :], 0.0)
            target[r, own, :] = fresh[8 : 8 + TILE, :]
            target[r, 16 + TILE : 24 + TILE, :] = jnp.where(keep_trail, fresh[wide - 8 :, :], 0.0)
            return down

        unused, came, unused = flows(source, k)
        for r in range(k + 1, TV_STEPS):
            came = row(r, came, r % 2, None if half else (group != 0) | (has_above == 1))

        def pair(i, came, row=row):
            came = row(TV_STEPS + 2 * i, came, 0)
            return row(TV_STEPS + 2 * i + 1, came, 1)

        came = lax.fori_loop(0, SIDE // 2, pair, came)
        for r in range(SIDE + TV_STEPS, SIDE + 2 * TV_STEPS - 1 - k):
            came = row(r, came, r % 2, None if half else (group != 1) | (has_below == 1))
    spans = ((2 * SIDE, 4 * SIDE),) if half else ((0, 2 * SIDE), (TILE - 2 * SIDE, 2 * SIDE))
    going = [
        pltpu.make_async_copy(
            ref.reshape(slices, TILE, TILE).at[:, pl.ds(start, count), :],
            out_ref.at[:, pl.ds(start, count), pl.ds(t * TILE, TILE)],
            sems.at[2 * i + t],
        )
        for i, (start, count) in enumerate(spans)
        for t, ref in enumerate((out0, out1))
    ]
    for copy in going:
        copy.start()
    for copy in going:
        copy.wait()


def call(kernel, scalars, arrays, left, outs, scratch, flops, aliases=None):
    vmem = pl.BlockSpec(memory_space=VMEM)
    stays = pl.BlockSpec(memory_space=pl.ANY)
    smem = pl.BlockSpec(memory_space=pltpu.SMEM)
    operands = (*scalars, *arrays, *left)
    moved = sum(x.size * x.dtype.itemsize for x in operands)
    big = 1 << 20
    inside = [x for x in (*arrays, *jax.tree.leaves(outs)) if x.size * 4 <= big]
    held = sum(x.size * 4 for x in inside)
    held += sum(math.prod(x.shape) * 4 for x in scratch if hasattr(x, "shape"))
    return pl.pallas_call(
        kernel,
        out_shape=outs,
        in_specs=[smem] * len(scalars) + [vmem] * len(arrays) + [stays] * len(left),
        out_specs=jax.tree.map(lambda x: stays if x.size * 4 > big else vmem, outs),
        scratch_shapes=scratch,
        input_output_aliases=aliases or {},
        compiler_params=pltpu.CompilerParams(vmem_limit_bytes=held + (6 << 20)),
        cost_estimate=pl.CostEstimate(flops=flops, bytes_accessed=moved, transcendentals=0),
    )(*operands)


def local(current_image, measured, ray_weight, angle_ids, shadow_start):
    row_index = lax.axis_index("row")
    col_index = lax.axis_index("col")
    rows = lax.axis_size("row")
    cols = lax.axis_size("col")
    slices = current_image.shape[0]
    both = ("row", "col")
    image = current_image.reshape(slices * TILE, 2 * TILE)
    table = geometry(angle_ids)
    half = VMEM((slices * TILE, TILE), F32)

    turned = jax.ShapeDtypeStruct((2 * SIDE, TILE, TILE), F32)
    sent, image = call(
        forward_kernel,
        (table, col_index.reshape(1)),
        (measured[:, 0], ray_weight[:, 0]),
        (image,),
        (jax.ShapeDtypeStruct((rows * cols * MESSAGE, TILE), BF16), turned),
        [
            VMEM((2 * SIDE * TILE, TILE), BF16),
            VMEM((BAND, PIX), F32),
            VMEM((4, BAND, PIX), BF16),
            VMEM((ANGLES * TILE, TILE), F32),
            VMEM((rows * cols * MESSAGE, TILE), F32),
            half,
            half,
            VMEM(turned.shape, F32),
            pltpu.SemaphoreType.DMA((3,)),
        ]
        + [VMEM((TILE, TILE), F32)] * ANGLES,
        30_000_000_000,
    )
    got = lax.all_to_all(
        sent.reshape(rows * cols, MESSAGE, TILE), both, split_axis=0, concat_axis=0, tiled=True
    )
    blocks = rows
    starts = shadow_start.reshape(-1, ANGLES)
    starts = lax.dynamic_slice_in_dim(starts, col_index * 2, 2, 1).reshape(-1)
    out = call(
        owner_kernel,
        (starts, col_index.reshape(1)),
        (),
        (got.reshape(-1, TILE),),
        jax.ShapeDtypeStruct((rows * cols * 4, TILE), BF16),
        [
            VMEM((2 * blocks, 3 * TILE), F32),
            VMEM((2, blocks + 1, 8, TILE), F32),
            VMEM((rows * cols * 4, TILE), F32),
            VMEM((3 * TILE, TILE), F32),
            VMEM((rows * cols * MESSAGE, TILE), F32),
            VMEM((rows * cols * MESSAGE, TILE), BF16),
            pltpu.SemaphoreType.DMA,
        ]
        + [VMEM((blocks, 8, TILE), F32)] * 16,
        10_000_000_000,
    )
    shadows = lax.all_to_all(
        out.reshape(rows * cols, 4, TILE), both, split_axis=0, concat_axis=0, tiled=True
    )
    bins = jnp.arange(BINS, dtype=F32)
    delta_lanes = (table[PAIRS : 2 * PAIRS, :, None] - bins).reshape(-1, BAND)
    angle_lanes = jnp.repeat(table[2 * PAIRS :], BINS, axis=1)
    side = jax.ShapeDtypeStruct((8, 8, TILE), F32)
    edge = jax.ShapeDtypeStruct((TILE // 8, 8, TILE), F32)
    x, left, right, top, bottom = call(
        backward_kernel,
        (table,),
        (delta_lanes, angle_lanes),
        (image, shadows.reshape(-1, TILE)),
        (turned, side, side, edge, edge),
        [
            VMEM((PIX, BAND), F32),
            VMEM((4, PIX, BAND), BF16),
            VMEM((ANGLES, TILE, TILE), F32),
            VMEM((rows * cols * 4, TILE), F32),
            VMEM((rows * cols * 4, TILE), F32),
            VMEM(turned.shape, F32),
            VMEM(turned.shape, F32),
            VMEM((rows * cols * 4, TILE), BF16),
            pltpu.SemaphoreType.DMA((2,)),
        ],
        30_000_000_000,
    )
    before = lax.ppermute(right, "col", [(i, i + 1) for i in range(cols - 1)])
    after = lax.ppermute(left, "col", [(i + 1, i) for i in range(cols - 1)])
    upward = jnp.concatenate([top, before[:TV_STEPS], after[:TV_STEPS]], axis=0)
    downward = jnp.concatenate([bottom, before[TV_STEPS:], after[TV_STEPS:]], axis=0)
    above = lax.ppermute(downward, "row", [(i, i + 1) for i in range(rows - 1)])
    below = lax.ppermute(upward, "row", [(i + 1, i) for i in range(rows - 1)])
    place = jnp.stack(
        [row_index > 0, row_index < rows - 1, col_index > 0, col_index < cols - 1]
    ).astype(jnp.int32)
    wide = VMEM((SIDE + 2 * TV_STEPS, TILE + 32, TILE), F32)
    few = VMEM((2 * TV_STEPS, TILE + 32, TILE), F32)
    scratch = [wide, wide, few, VMEM((2, TILE + 32, TILE), F32), half, half]
    scratch.append(pltpu.SemaphoreType.DMA((4,)))
    final = jax.ShapeDtypeStruct(current_image.shape, F32)
    smooth = call(
        functools.partial(smooth_kernel, 1),
        (place,),
        (before, after),
        (x,),
        final,
        scratch,
        10_000_000_000,
    )
    return call(
        functools.partial(smooth_kernel, 0),
        (place,),
        (before, after, above, below),
        (x, smooth),
        final,
        scratch,
        10_000_000_000,
        {6: 0},
    )


def solution(mesh):
    return jax.shard_map(
        local,
        mesh=mesh,
        in_specs=(
            P(None, "row", "col"),
            P("col", "row", None, None),
            P("col", "row", None),
            P(),
            P(),
        ),
        out_specs=P(None, "row", "col"),
        check_vma=False,
    )
```

time: 106 us -> 90.2 us (0.85)
  Pallas kernels: 46.2 us -> 35.4 us
  other arithmetic: 2.74 us -> 1.01 us
  local copies, waits for them, and re-layouts: 4.93 us -> 3.77 us
    pallas_call x4 -> x5, Pallas kernels: 46.2 us -> 35.4 us  [call(): pl.pallas_call(kernel, out_shape=outs, in_specs=[smem] * len(scalars) + [...]
    unnamed x14 -> x8, local copies, waits for them, and re-layouts: 2.09 us -> 2.99 us
  transfers between devices with their start and end apart: 6 -> 6, of which waited for: 4 -> 3; matrix products, arithmetic and copies ran while one was open for 4% -> 1% of each run, Pallas kernels for 0% -> 8%
where the time goes in v4:
time: 90.2 us; the launch traced here: 89.8 us
  Pallas kernels  35.4 us (39%)
  starting transfers between devices  28 us (31%)
  waiting for transfers between devices  21.4 us (24%)
  local copies, waits for them, and re-layouts  3.77 us (4%)
  other arithmetic  1.01 us (1%)
    pallas_call x5, Pallas kernels, call(): pl.pallas_call(kernel, out_shape=outs, in_specs=[smem] * len(scalars) + [...  35.4 us
    all_to_all x1, starting transfers between devices, local(): lax.all_to_all(sent.reshape(rows * cols, MESSAGE, TILE), both, split_axis...  10.7 us
    all_to_all x1, waiting for transfers between devices, local(): lax.all_to_all(sent.reshape(rows * cols, MESSAGE, TILE), both, split_axis...  9.16 us
    all_to_all x1, waiting for transfers between devices, local(): lax.all_to_all(out.reshape(rows * cols, 4, TILE), both, split_axis=0, con...  8.96 us
    all_to_all x1, starting transfers between devices, local(): lax.all_to_all(out.reshape(rows * cols, 4, TILE), both, split_axis=0, con...  5.48 us
    ppermute x1, starting transfers between devices, local(): below = lax.ppermute(upward, 'row', [(i + 1, i) for i in range(rows - 1)])  5.27 us
    ppermute x1, waiting for transfers between devices, local(): after = lax.ppermute(left, 'col', [(i + 1, i) for i in range(cols - 1)])  3.28 us
    unnamed x8, local copies, waits for them, and re-layouts  2.99 us
  transfers between devices with their start and end apart: 6, of which 3 were waited for; matrix products, arithmetic and copies ran while one was open for 1% of the time, Pallas kernels for 8%

profile of v4, /device:TPU:9, one launch (start us, length us, event | category | flops | bytes accessed | tf_op | source)
XLA Modules:
  0.0 89.8 jit_solution(15956129316794972404)
XLA Ops:
  0.0 0.0 copy-start
  0.0 0.7 cosine_multiply_fusion
  0.8 0.2 select_select_fusion.1.table_ref
  0.9 0.0 copy-start.1
  0.9 1.6 %copy-done.1 = f32[16,128,256]{2,1,0:T(8,128)S(1)} copy-done((f32[16,128,256]{2,1,0:T(8,128)S(1)}, f32[16,128,256]{2,1,0:T(8,128)}, u32[]{:S(2)}) %copy-start.1) | copy-done | bytes 2097176
  2.5 0.0 copy-start.2
  2.5 0.7 copy-done.2
  3.2 0.0 copy-start.3
  3.2 0.7 copy-done.3
  3.9 9.7 %shard_map.55 = (bf16[1024,128]{1,0:T(8,128)(2,1)}, f32[32,128,128]{2,1,0:T(8,128)S(1)}) custom-call(f32[66,16]{1,0:T(8,128)S(1)} %select_select_fusion.1.table_ref, s32[1]{0:T(128)} %bitcast.4.own_ref, f32[2,16,128]{2,1,0:T(8,128)S(1)} %bitcast.17, f32[2,128]{1,0:T(2,128)S(1)} %bitcast.18, f32[2048,256]{1,0:T(8,128)S(1)} %bitcast.16), custom_call_target="tpu_custom_call" | custom-call | flops 30000001024 | bytes 2118788 | tf_op jit(solution)/shard_map/pallas_call | solution.py:547
  13.7 10.7 %all-to-all-start = ((bf16[128,8,128]{2,1,0:T(8,128)(2,1)}), bf16[128,8,128]{2,1,0:T(8,128)(2,1)S(1)}, u32[]{:S(2)}, u32[]{:S(2)}) async-start(bf16[128,8,128]{2,1,0:T(8,128)(2,1)} %bitcast.9), calls=%async_computation | async-start | bytes 524288 | tf_op jit(solution)/shard_map/all_to_all | solution.py:591
  24.4 0.1 sub.52
  24.5 0.1 broadcast_in_dim.14
  24.6 0.1 reshape.41.lanes_ref
  24.7 0.0 copy-done
  24.7 0.1 constant_dynamic-slice_fusion
  24.8 0.1 reshape.45.starts_ref
  25.0 0.1 sub.49
  25.1 0.2 sub.50
  25.3 9.2 %all-to-all-done = bf16[128,8,128]{2,1,0:T(8,128)(2,1)S(1)} async-done(((bf16[128,8,128]{2,1,0:T(8,128)(2,1)}), bf16[128,8,128]{2,1,0:T(8,128)(2,1)S(1)}, u32[]{:S(2)}, u32[]{:S(2)}) %all-to-all-start) | async-done | bytes 262176 | tf_op jit(solution)/shard_map/all_to_all | solution.py:591
  34.4 4.7 %shard_map.56 = bf16[512,128]{1,0:T(8,128)(2,1)} custom-call(s32[512]{0:T(512)S(1)} %reshape.45.starts_ref, s32[1]{0:T(128)} %bitcast.4.own_ref, bf16[1024,128]{1,0:T(8,128)(2,1)S(1)} %bitcast.14), custom_call_target="tpu_custom_call" | custom-call | flops 10000000000 | bytes 264196 | tf_op jit(solution)/shard_map/pallas_call | solution.py:547
  39.1 5.5 %all-to-all-start.1 = ((bf16[128,4,128]{2,1,0:T(4,128)(2,1)}), bf16[128,4,128]{2,1,0:T(4,128)(2,1)S(1)}, u32[]{:S(2)}, u32[]{:S(2)}) async-start(bf16[128,4,128]{2,1,0:T(4,128)(2,1)} %bitcast.11), calls=%async_computation.1 | async-start | bytes 262144 | tf_op jit(solution)/shard_map/all_to_all | solution.py:615
  44.6 9.0 %all-to-all-done.1 = bf16[128,4,128]{2,1,0:T(4,128)(2,1)S(1)} async-done(((bf16[128,4,128]{2,1,0:T(4,128)(2,1)}), bf16[128,4,128]{2,1,0:T(4,128)(2,1)S(1)}, u32[]{:S(2)}, u32[]{:S(2)}) %all-to-all-start.1) | async-done | bytes 131104 | tf_op jit(solution)/shard_map/all_to_all | solution.py:615
  53.6 6.9 %shard_map.57 = (f32[32,128,128]{2,1,0:T(8,128)S(1)}, f32[8,8,128]{2,1,0:T(8,128)S(1)}, f32[8,8,128]{2,1,0:T(8,128)S(1)}, f32[16,8,128]{2,1,0:T(8,128)S(1)}, f32[16,8,128]{2,1,0:T(8,128)S(1)}) custom-call(f32[66,16]{1,0:T(8,128)S(1)} %select_select_fusion.1.table_ref, f32[32,384]{1,0:T(8,128)S(1)} %broadcast_subtract_fusion.delta_ref, ...), custom_call_target="tpu_custom_call" | custom-call | flops 30000001024 | bytes 2284672 | tf_op jit(solution)/shard_map/pallas_call | solution.py:547
  60.5 2.5 %collective-permute-start = (f32[8,8,128]{2,1,0:T(8,128)S(1)}, f32[8,8,128]{2,1,0:T(8,128)S(1)}, u32[]{:S(2)}, u32[]{:S(2)}) collective-permute-start(f32[8,8,128]{2,1,0:T(8,128)S(1)} %get-tuple-element.14), channel_id=1, source_target_pairs={{0,1},{1,2},{2,3},{3,4},{4,5},{5,6},{6,7},{8,9},{9,10},{10,11},{11... | collective-permute-start | bytes 98312 | tf_op jit(solution)/shard_map/ppermute | solution.py:642
  63.0 0.1 add_convert_fusion.place_ref
  63.1 1.9 %collective-permute-start.1 = (f32[8,8,128]{2,1,0:T(8,128)S(1)}, f32[8,8,128]{2,1,0:T(8,128)S(1)}, u32[]{:S(2)}, u32[]{:S(2)}) collective-permute-start(f32[8,8,128]{2,1,0:T(8,128)S(1)} %get-tuple-element.15), channel_id=1, source_target_pairs={{1,0},{2,1},{3,2},{4,3},{5,4},{6,5},{7,6},{9,8},{10,9},{11,10},{12... | collective-permute-start | bytes 98312 | tf_op jit(solution)/shard_map/ppermute | solution.py:643
  65.0 0.0 collective-permute-done.before_ref
  65.0 3.3 %collective-permute-done.1.after_ref = f32[8,8,128]{2,1,0:T(8,128)S(1)} collective-permute-done((f32[8,8,128]{2,1,0:T(8,128)S(1)}, f32[8,8,128]{2,1,0:T(8,128)S(1)}, u32[]{:S(2)}, u32[]{:S(2)}) %collective-permute-start.1) | collective-permute-done | bytes 32800 | tf_op jit(solution)/shard_map/ppermute | solution.py:643
  68.3 2.1 %collective-permute-start.2 = (f32[24,8,128]{2,1,0:T(8,128)S(1)}, f32[24,8,128]{2,1,0:T(8,128)S(1)}, u32[]{:S(2)}, u32[]{:S(2)}) collective-permute-start(f32[24,8,128]{2,1,0:T(8,128)S(1)} %pad_maximum_fusion), channel_id=1, source_target_pairs={{0,8},{8,16},{16,24},{24,32},{32,40},{40,48},{48,56},{56,64},{64,7... | collective-permute-start | bytes 294920 | tf_op jit(solution)/shard_map/ppermute | solution.py:646
  70.5 5.3 %collective-permute-start.3 = (f32[24,8,128]{2,1,0:T(8,128)S(1)}, f32[24,8,128]{2,1,0:T(8,128)S(1)}, u32[]{:S(2)}, u32[]{:S(2)}) collective-permute-start(f32[24,8,128]{2,1,0:T(8,128)S(1)} %pad_maximum_fusion.1), channel_id=1, source_target_pairs={{8,0},{16,8},{24,16},{32,24},{40,32},{48,40},{56,48},{64,56},{72,6... | collective-permute-start | bytes 294920 | tf_op jit(solution)/shard_map/ppermute | solution.py:647
  75.7 7.0 %shard_map.58.refs_3_ = f32[16,128,256]{2,1,0:T(8,128)} custom-call(s32[4]{0:T(128)S(1)} %add_convert_fusion.place_ref, f32[8,8,128]{2,1,0:T(8,128)S(1)} %collective-permute-done.before_ref, f32[8,8,128]{2,1,0:T(8,128)S(1)} %collective-permute-done.1.after_ref, f32[32,128,128]{2,1,0:T(8,128)S(1)} %get-tuple-element.18.refs_0_.refs_2_), custom_call_target="tpu_custom_call" | custom-call | flops 10000000000 | bytes 2162704 | tf_op jit(solution)/shard_map/pallas_call | solution.py:547
  82.8 0.0 collective-permute-done.2.refs_0_
  82.8 0.0 collective-permute-done.3.refs_1_
  82.8 7.0 %shard_map.59 = f32[16,128,256]{2,1,0:T(8,128)} custom-call(s32[4]{0:T(128)S(1)} %add_convert_fusion.place_ref, f32[8,8,128]{2,1,0:T(8,128)S(1)} %collective-permute-done.before_ref, f32[8,8,128]{2,1,0:T(8,128)S(1)} %collective-permute-done.1.after_ref, f32[24,8,128]{2,1,0:T(8,128)S(1)} %collective-permute-done.2.refs_0_, ...), custom_call_target="tpu_custom_call", output_to_operand_aliasing={{}: (6, {})} | custom-call | flops 10000000000 | bytes 4456464 | tf_op jit(solution)/shard_map/pallas_call | solution.py:547
  (11 shorter events, 0.1 us)
Async XLA Ops:
  0.0 24.7 %copy-start = (s32[16,16,16]{2,1,0:T(8,128)S(1)}, s32[16,16,16]{2,1,0:T(8,128)}, u32[]{:S(2)}) copy-start(s32[16,16,16]{2,1,0:T(8,128)} %param.9) | copy-start | bytes 49156
  0.9 1.6 %copy-start.1 = (f32[16,128,256]{2,1,0:T(8,128)S(1)}, f32[16,128,256]{2,1,0:T(8,128)}, u32[]{:S(2)}) copy-start(f32[16,128,256]{2,1,0:T(8,128)} %param.5) | copy-start | bytes 6291460
  2.5 0.7 copy-start.2
  3.2 0.7 copy-start.3
  13.7 20.8 %all-to-all-start = ((bf16[128,8,128]{2,1,0:T(8,128)(2,1)}), bf16[128,8,128]{2,1,0:T(8,128)(2,1)S(1)}, u32[]{:S(2)}, u32[]{:S(2)}) async-start(bf16[128,8,128]{2,1,0:T(8,128)(2,1)} %bitcast.9), calls=%async_computation | async-start | bytes 524288 | tf_op jit(solution)/shard_map/all_to_all | solution.py:591
  39.1 14.5 %all-to-all-start.1 = ((bf16[128,4,128]{2,1,0:T(4,128)(2,1)}), bf16[128,4,128]{2,1,0:T(4,128)(2,1)S(1)}, u32[]{:S(2)}, u32[]{:S(2)}) async-start(bf16[128,4,128]{2,1,0:T(4,128)(2,1)} %bitcast.11), calls=%async_computation.1 | async-start | bytes 262144 | tf_op jit(solution)/shard_map/all_to_all | solution.py:615
  60.5 4.5 %collective-permute-start = (f32[8,8,128]{2,1,0:T(8,128)S(1)}, f32[8,8,128]{2,1,0:T(8,128)S(1)}, u32[]{:S(2)}, u32[]{:S(2)}) collective-permute-start(f32[8,8,128]{2,1,0:T(8,128)S(1)} %get-tuple-element.14), channel_id=1, source_target_pairs={{0,1},{1,2},{2,3},{3,4},{4,5},{5,6},{6,7},{8,9},{9,10},{10,11},{11... | collective-permute-start | bytes 98312 | tf_op jit(solution)/shard_map/ppermute | solution.py:642
  63.1 5.2 %collective-permute-start.1 = (f32[8,8,128]{2,1,0:T(8,128)S(1)}, f32[8,8,128]{2,1,0:T(8,128)S(1)}, u32[]{:S(2)}, u32[]{:S(2)}) collective-permute-start(f32[8,8,128]{2,1,0:T(8,128)S(1)} %get-tuple-element.15), channel_id=1, source_target_pairs={{1,0},{2,1},{3,2},{4,3},{5,4},{6,5},{7,6},{9,8},{10,9},{11,10},{12... | collective-permute-start | bytes 98312 | tf_op jit(solution)/shard_map/ppermute | solution.py:643
  68.3 14.5 %collective-permute-start.2 = (f32[24,8,128]{2,1,0:T(8,128)S(1)}, f32[24,8,128]{2,1,0:T(8,128)S(1)}, u32[]{:S(2)}, u32[]{:S(2)}) collective-permute-start(f32[24,8,128]{2,1,0:T(8,128)S(1)} %pad_maximum_fusion), channel_id=1, source_target_pairs={{0,8},{8,16},{16,24},{24,32},{32,40},{40,48},{48,56},{56,64},{64,7... | collective-permute-start | bytes 294920 | tf_op jit(solution)/shard_map/ppermute | solution.py:646
  70.5 12.3 %collective-permute-start.3 = (f32[24,8,128]{2,1,0:T(8,128)S(1)}, f32[24,8,128]{2,1,0:T(8,128)S(1)}, u32[]{:S(2)}, u32[]{:S(2)}) collective-permute-start(f32[24,8,128]{2,1,0:T(8,128)S(1)} %pad_maximum_fusion.1), channel_id=1, source_target_pairs={{8,0},{16,8},{24,16},{32,24},{40,32},{48,40},{56,48},{64,56},{72,6... | collective-permute-start | bytes 294920 | tf_op jit(solution)/shard_map/ppermute | solution.py:647

commit v5 on v4

--- a/solution.py
+++ b/solution.py
@@ -19,6 +19,8 @@
 ROWS = 32
 BAND = ANGLES * BINS
 PAIRS = PATCHES * PATCHES // 2
+PHASE = 4
+STRIDE = 4
 MESSAGE = 8
 
 inverse_root = 0.7071067811865476
@@ -35,9 +37,9 @@
     cosine = jnp.cos(radians)[None] * inverse_root
     sine = jnp.sin(radians)[None] * inverse_root
     row = lax.broadcasted_iota(jnp.int32, (2 * PAIRS + 2, ANGLES), 0)
-    patch = row % PAIRS
-    down = (patch // PATCHES).astype(F32) * SIDE - (TILE - 1) / 2.0
-    across = (patch % PATCHES).astype(F32) * SIDE - (TILE - 1) / 2.0
+    patch = row & (PAIRS - 1)
+    down = (patch >> 3).astype(F32) * SIDE - (TILE - 1) / 2.0
+    across = (patch & (PATCHES - 1)).astype(F32) * SIDE - (TILE - 1) / 2.0
     corner = TILE / 2.0 + down * cosine + across * sine
     low = corner + (SIDE - 1) * (jnp.minimum(cosine, 0.0) + jnp.minimum(sine, 0.0))
     base = jnp.clip(jnp.floor((jnp.floor(low - 1.5) + 1.0) / 8.0) * 8.0, 0.0, TILE - BINS)
@@ -61,26 +63,30 @@
 
 
 def pipeline(build, use, bands):
-    def pair(i, action, slots):
-        half = i // PATCHES
-        col = i % PATCHES
-        for own in range(2):
-            patch = (2 * half + own) * PATCHES + col
-            if action is build:
-                build(patch, bands.at[slots + own])
-            else:
-                use(patch, bands.at[slots + own], half, col, own)
-
-    pair(0, build, 0)
+    def phase(i, action, slot):
+        for j in range(PHASE):
+            at = i * PHASE + j
+            half = at // PATCHES
+            col = at % PATCHES
+            for own in range(2):
+                patch = (2 * half + own) * PATCHES + col
+                band = bands.at[(slot * PHASE + j) * 2 + own]
+                if action is build:
+                    build(patch, band)
+                else:
+                    use(patch, band, half, col, own)
+
+    phase(0, build, 0)
+    phases = 2 * PATCHES // PHASE
 
     def step(i, carry):
-        pair(2 * i + 1, build, 2)
-        pair(2 * i, use, 0)
-        pair(jnp.minimum(2 * i + 2, 2 * PATCHES - 1), build, 0)
-        pair(2 * i + 1, use, 2)
+        phase(2 * i + 1, build, 1)
+        phase(2 * i, use, 0)
+        phase(jnp.minimum(2 * i + 2, phases - 1), build, 0)
+        phase(2 * i + 1, use, 1)
         return carry
 
-    lax.fori_loop(0, PATCHES, step, 0)
+    lax.fori_loop(0, phases // 2, step, 0)
 
 
 def blocks_at(half):
@@ -99,22 +105,29 @@
     return jnp.concatenate(parts, axis=0)
 
 
-def halves_of(image, targets, sems):
-    return [
-        pltpu.make_async_copy(image.at[:, pl.ds(t * TILE, TILE)], target, sems.at[t])
-        for t, target in enumerate(targets)
+def forward_kernel(
+    table_ref, own_ref, image_ref, given_ref, given_weight_ref,
+    out_ref, turned_ref, xt, rel, bands, tails, message, image0_ref, image1_ref, flat,
+    measured_ref, weight_ref, sems, *sums,
+):
+    slices = ROWS // 2
+    coming = [[], []]
+    for part, start in ((0, 0), (0, 6), (1, 2), (1, 4)):
+        spot = pl.ds(start * SIDE, 2 * SIDE)
+        for t, ref in enumerate((image0_ref, image1_ref)):
+            coming[part].append(
+                pltpu.make_async_copy(
+                    image_ref.at[:, spot, pl.ds(t * TILE, TILE)],
+                    ref.reshape(slices, TILE, TILE).at[:, spot, :],
+                    sems.at[2 + start + t],
+                )
+            )
+    small = [
+        pltpu.make_async_copy(given_ref, measured_ref, sems.at[0]),
+        pltpu.make_async_copy(given_weight_ref, weight_ref, sems.at[1]),
     ]
-
-
-def forward_kernel(
-    table_ref, own_ref, measured_ref, weight_ref, image_ref,
-    out_ref, turned_ref, xt, rel, bands, tails, message, image0_ref, image1_ref, flat, sems,
-    *sums,
-):
-    coming = halves_of(image_ref, (image0_ref, image1_ref), sems)
-    for copy in coming:
+    for copy in (*coming[0], *coming[1], *small):
         copy.start()
-    slices = ROWS // 2
     lane = lax.broadcasted_iota(jnp.int32, (BINS, PIX), 1)
     bin_at = lax.broadcasted_iota(jnp.int32, (BINS, PIX), 0).astype(F32)
     down = (lane // SIDE).astype(F32)
@@ -125,9 +138,6 @@
         )
     for ref in sums:
         ref[...] = jnp.zeros_like(ref)
-    for copy in coming:
-        copy.wait()
-
     def rows_of(u):
         return [ref[pl.ds(u, slices, stride=TILE), :] for ref in (image0_ref, image1_ref)]
 
@@ -138,8 +148,13 @@
         flat[i] = jnp.concatenate(rows, axis=0).T
         return carry
 
-    lax.fori_loop(0, 2 * SIDE, flip, 0, unroll=4)
-    going = pltpu.make_async_copy(flat, turned_ref, sems.at[2])
+    for part in range(2):
+        for copy in coming[part]:
+            copy.wait()
+        lax.fori_loop(part * SIDE, (part + 1) * SIDE, flip, 0, unroll=4)
+    for copy in small:
+        copy.wait()
+    going = pltpu.make_async_copy(flat, turned_ref, sems.at[0])
     going.start()
 
     def reflect(i, carry):
@@ -154,8 +169,9 @@
             pair = []
             for b in (a, a + 1):
                 away = jnp.abs(rel[b * BINS : (b + 1) * BINS, :] + table_ref[PAIRS + patch, b])
-                pair.append(jnp.maximum(0.0, 1.0 - away))
-            band[a * BINS : (a + 2) * BINS, :] = jnp.concatenate(pair, axis=0).astype(BF16)
+                pair.append(1.0 - away)
+            rounded = jnp.concatenate(pair, axis=0).astype(BF16)
+            band[a * BINS : (a + 2) * BINS, :] = jnp.maximum(rounded, jnp.zeros_like(rounded))
 
     first_half = lax.broadcasted_iota(jnp.int32, (PIX, TILE), 1) < TILE // 2
 
@@ -319,7 +335,8 @@
         shift = delta_ref[pl.ds(patch, 1), :]
         for r in range(0, PIX, 16):
             away = jnp.abs(rel[r : r + 16, :] + shift)
-            band[r : r + 16, :] = jnp.maximum(0.0, 1.0 - away).astype(BF16)
+            rounded = (1.0 - away).astype(BF16)
+            band[r : r + 16, :] = jnp.maximum(rounded, jnp.zeros_like(rounded))
 
     def spread(patch, band, half, col, own):
         pieces = []
@@ -511,48 +528,61 @@
         for r in range(k + 1, TV_STEPS):
             came = row(r, came, r % 2, None if half else (group != 0) | (has_above == 1))
 
-        def pair(i, came, row=row):
-            came = row(TV_STEPS + 2 * i, came, 0)
-            return row(TV_STEPS + 2 * i + 1, came, 1)
-
-        came = lax.fori_loop(0, SIDE // 2, pair, came)
+        def some(i, came, row=row):
+            for j in range(STRIDE):
+                came = row(TV_STEPS + STRIDE * i + j, came, j % 2)
+            return came
+
+        if not last:
+            came = lax.fori_loop(0, SIDE // STRIDE, some, came)
         for r in range(SIDE + TV_STEPS, SIDE + 2 * TV_STEPS - 1 - k):
             came = row(r, came, r % 2, None if half else (group != 1) | (has_below == 1))
-    spans = ((2 * SIDE, 4 * SIDE),) if half else ((0, 2 * SIDE), (TILE - 2 * SIDE, 2 * SIDE))
-    going = [
-        pltpu.make_async_copy(
-            ref.reshape(slices, TILE, TILE).at[:, pl.ds(start, count), :],
-            out_ref.at[:, pl.ds(start, count), pl.ds(t * TILE, TILE)],
-            sems.at[2 * i + t],
+    going = []
+    for part in range(2):
+        came = lax.fori_loop(
+            part * SIDE // 2 // STRIDE, (part + 1) * SIDE // 2 // STRIDE, some, came
         )
-        for i, (start, count) in enumerate(spans)
-        for t, ref in enumerate((out0, out1))
-    ]
-    for copy in going:
-        copy.start()
+        for block in blocks_at(half):
+            spot = pl.ds(block * SIDE + part * 8, 8)
+            for t, ref in enumerate((out0, out1)):
+                going.append(
+                    pltpu.make_async_copy(
+                        ref.reshape(slices, TILE, TILE).at[:, spot, :],
+                        out_ref.at[:, spot, pl.ds(t * TILE, TILE)],
+                        sems.at[len(going)],
+                    )
+                )
+                going[-1].start()
     for copy in going:
         copy.wait()
 
 
-def call(kernel, scalars, arrays, left, outs, scratch, flops, aliases=None):
+def call(
+    kernel, scalars, arrays, left, outs, scratch, flops, aliases=None, tight=True
+):
     vmem = pl.BlockSpec(memory_space=VMEM)
-    stays = pl.BlockSpec(memory_space=pl.ANY)
     smem = pl.BlockSpec(memory_space=pltpu.SMEM)
     operands = (*scalars, *arrays, *left)
-    moved = sum(x.size * x.dtype.itemsize for x in operands)
-    big = 1 << 20
-    inside = [x for x in (*arrays, *jax.tree.leaves(outs)) if x.size * 4 <= big]
-    held = sum(x.size * 4 for x in inside)
-    held += sum(math.prod(x.shape) * 4 for x in scratch if hasattr(x, "shape"))
+    bytes_of = lambda x: math.prod(x.shape) * x.dtype.itemsize
+    stays = lambda x: bytes_of(x) > 1 << 20
+    held = sum(bytes_of(x) for x in arrays)
+    held += sum(bytes_of(x) for x in jax.tree.leaves(outs) if not stays(x))
+    held += sum(bytes_of(x) for x in scratch if getattr(x, "memory_space", None) == VMEM)
     return pl.pallas_call(
         kernel,
         out_shape=outs,
-        in_specs=[smem] * len(scalars) + [vmem] * len(arrays) + [stays] * len(left),
-        out_specs=jax.tree.map(lambda x: stays if x.size * 4 > big else vmem, outs),
+        in_specs=[smem] * len(scalars)
+        + [vmem] * len(arrays)
+        + [pl.BlockSpec(memory_space=pl.ANY)] * len(left),
+        out_specs=jax.tree.map(
+            lambda x: pl.BlockSpec(memory_space=pl.ANY) if stays(x) else vmem, outs
+        ),
         scratch_shapes=scratch,
         input_output_aliases=aliases or {},
-        compiler_params=pltpu.CompilerParams(vmem_limit_bytes=held + (6 << 20)),
-        cost_estimate=pl.CostEstimate(flops=flops, bytes_accessed=moved, transcendentals=0),
+        compiler_params=pltpu.CompilerParams(vmem_limit_bytes=held + (6 << 20) if tight else None),
+        cost_estimate=pl.CostEstimate(
+            flops=flops, bytes_accessed=sum(map(bytes_of, operands)), transcendentals=0
+        ),
     )(*operands)
 
 
@@ -563,7 +593,6 @@
     cols = lax.axis_size("col")
     slices = current_image.shape[0]
     both = ("row", "col")
-    image = current_image.reshape(slices * TILE, 2 * TILE)
     table = geometry(angle_ids)
     half = VMEM((slices * TILE, TILE), F32)
 
@@ -571,22 +600,25 @@
     sent, image = call(
         forward_kernel,
         (table, col_index.reshape(1)),
-        (measured[:, 0], ray_weight[:, 0]),
-        (image,),
+        (),
+        (current_image, measured[:, 0], ray_weight[:, 0]),
         (jax.ShapeDtypeStruct((rows * cols * MESSAGE, TILE), BF16), turned),
         [
             VMEM((2 * SIDE * TILE, TILE), BF16),
             VMEM((BAND, PIX), F32),
-            VMEM((4, BAND, PIX), BF16),
+            VMEM((4 * PHASE, BAND, PIX), BF16),
             VMEM((ANGLES * TILE, TILE), F32),
             VMEM((rows * cols * MESSAGE, TILE), F32),
             half,
             half,
             VMEM(turned.shape, F32),
-            pltpu.SemaphoreType.DMA((3,)),
+            VMEM(measured[:, 0].shape, F32),
+            VMEM(ray_weight[:, 0].shape, F32),
+            pltpu.SemaphoreType.DMA((10,)),
         ]
         + [VMEM((TILE, TILE), F32)] * ANGLES,
         30_000_000_000,
+        tight=False,
     )
     got = lax.all_to_all(
         sent.reshape(rows * cols, MESSAGE, TILE), both, split_axis=0, concat_axis=0, tiled=True
@@ -628,7 +660,7 @@
         (turned, side, side, edge, edge),
         [
             VMEM((PIX, BAND), F32),
-            VMEM((4, PIX, BAND), BF16),
+            VMEM((4 * PHASE, PIX, BAND), BF16),
             VMEM((ANGLES, TILE, TILE), F32),
             VMEM((rows * cols * 4, TILE), F32),
             VMEM((rows * cols * 4, TILE), F32),
@@ -651,7 +683,7 @@
     wide = VMEM((SIDE + 2 * TV_STEPS, TILE + 32, TILE), F32)
     few = VMEM((2 * TV_STEPS, TILE + 32, TILE), F32)
     scratch = [wide, wide, few, VMEM((2, TILE + 32, TILE), F32), half, half]
-    scratch.append(pltpu.SemaphoreType.DMA((4,)))
+    scratch.append(pltpu.SemaphoreType.DMA((16,)))
     final = jax.ShapeDtypeStruct(current_image.shape, F32)
     smooth = call(
         functools.partial(smooth_kernel, 1),

time: 90.2 us -> 87.5 us (0.970)
  local copies, waits for them, and re-layouts: 3.77 us -> 0.79 us
    unnamed x8 -> x6, local copies, waits for them, and re-layouts: 2.99 us -> 0.01 us
where the time goes in v5:
time: 87.5 us; the launch traced here: 87.1 us
  Pallas kernels  34.8 us (40%)
  starting transfers between devices  28.1 us (32%)
  waiting for transfers between devices  21.4 us (24%)
  other arithmetic  1.58 us (2%)
    pallas_call x5, Pallas kernels, call(): pl.pallas_call(kernel, out_shape=outs, in_specs=[smem] * len(scalars) + [...  34.8 us
    all_to_all x1, starting transfers between devices, local(): lax.all_to_all(sent.reshape(rows * cols, MESSAGE, TILE), both, split_axis...  10.7 us
    all_to_all x1, waiting for transfers between devices, local(): lax.all_to_all(sent.reshape(rows * cols, MESSAGE, TILE), both, split_axis...  9.17 us
    all_to_all x1, waiting for transfers between devices, local(): lax.all_to_all(out.reshape(rows * cols, 4, TILE), both, split_axis=0, con...  8.96 us
    all_to_all x1, starting transfers between devices, local(): lax.all_to_all(out.reshape(rows * cols, 4, TILE), both, split_axis=0, con...  5.48 us
    ppermute x1, starting transfers between devices, local(): below = lax.ppermute(upward, 'row', [(i + 1, i) for i in range(rows - 1)])  5.45 us
    ppermute x1, waiting for transfers between devices, local(): after = lax.ppermute(left, 'col', [(i + 1, i) for i in range(cols - 1)])  3.28 us
    ppermute x1, starting transfers between devices, local(): before = lax.ppermute(right, 'col', [(i, i + 1) for i in range(cols - 1)])  2.45 us
  transfers between devices with their start and end apart: 6, of which 3 were waited for; matrix products, arithmetic and copies ran while one was open for 1% of the time, Pallas kernels for 8%

profile of v5, /device:TPU:9, one launch (start us, length us, event | category | flops | bytes accessed | tf_op | source)
XLA Modules:
  0.0 87.1 jit_solution(18305600502384859663)
XLA Ops:
  0.0 0.0 copy-start
  0.0 0.7 cosine_multiply_fusion
  0.8 0.7 select_select_fusion.table_ref
  1.5 0.0 slice-start
  1.5 0.0 slice-start.1
  1.5 10.4 %shard_map.55 = (bf16[1024,128]{1,0:T(8,128)(2,1)}, f32[32,128,128]{2,1,0:T(8,128)}) custom-call(f32[66,16]{1,0:T(8,128)} %select_select_fusion.table_ref, s32[1]{0:T(128)} %bitcast.4.own_ref, f32[16,128,256]{2,1,0:T(8,128)} %image_ref.1, f32[2,16,128]{2,1,0:T(8,128)} %bitcast.16, f32[2,128]{1,0:T(2,128)} %bitcast.17), custom_call_target="tpu_custom_call" | custom-call | flops 30000001024 | bytes 2118788 | tf_op jit(solution)/shard_map/pallas_call | solution.py:571
  11.9 10.7 %all-to-all-start = ((bf16[128,8,128]{2,1,0:T(8,128)(2,1)}), bf16[128,8,128]{2,1,0:T(8,128)(2,1)S(1)}, u32[]{:S(2)}, u32[]{:S(2)}) async-start(bf16[128,8,128]{2,1,0:T(8,128)(2,1)} %bitcast.15), calls=%async_computation | async-start | bytes 524288 | tf_op jit(solution)/shard_map/all_to_all | solution.py:623
  22.7 0.1 sub.45
  22.8 0.0 slice-done
  22.8 0.1 broadcast_in_dim.14
  22.9 0.1 reshape.38.lanes_ref
  23.0 0.0 copy-done
  23.0 0.1 constant_dynamic-slice_fusion
  23.1 0.1 reshape.41.starts_ref
  23.2 0.0 slice-done.1
  23.2 0.1 sub.42
  23.4 0.2 sub.43
  23.5 9.2 %all-to-all-done = bf16[128,8,128]{2,1,0:T(8,128)(2,1)S(1)} async-done(((bf16[128,8,128]{2,1,0:T(8,128)(2,1)}), bf16[128,8,128]{2,1,0:T(8,128)(2,1)S(1)}, u32[]{:S(2)}, u32[]{:S(2)}) %all-to-all-start) | async-done | bytes 262176 | tf_op jit(solution)/shard_map/all_to_all | solution.py:623
  32.7 0.0 copy-start.1
  32.7 0.0 copy-start.2
  32.7 4.7 %shard_map.56 = bf16[512,128]{1,0:T(8,128)(2,1)} custom-call(s32[512]{0:T(512)S(1)} %reshape.41.starts_ref, s32[1]{0:T(128)} %bitcast.4.own_ref, bf16[1024,128]{1,0:T(8,128)(2,1)S(1)} %bitcast.13), custom_call_target="tpu_custom_call" | custom-call | flops 10000000000 | bytes 264196 | tf_op jit(solution)/shard_map/pallas_call | solution.py:571
  37.4 5.5 %all-to-all-start.1 = ((bf16[128,4,128]{2,1,0:T(4,128)(2,1)}), bf16[128,4,128]{2,1,0:T(4,128)(2,1)S(1)}, u32[]{:S(2)}, u32[]{:S(2)}) async-start(bf16[128,4,128]{2,1,0:T(4,128)(2,1)} %bitcast.10), calls=%async_computation.1 | async-start | bytes 262144 | tf_op jit(solution)/shard_map/all_to_all | solution.py:647
  42.9 9.0 %all-to-all-done.1 = bf16[128,4,128]{2,1,0:T(4,128)(2,1)S(1)} async-done(((bf16[128,4,128]{2,1,0:T(4,128)(2,1)}), bf16[128,4,128]{2,1,0:T(4,128)(2,1)S(1)}, u32[]{:S(2)}, u32[]{:S(2)}) %all-to-all-start.1) | async-done | bytes 131104 | tf_op jit(solution)/shard_map/all_to_all | solution.py:647
  51.9 0.0 copy-done.1
  51.9 0.0 copy-done.2
  51.9 6.5 %shard_map.57 = (f32[32,128,128]{2,1,0:T(8,128)S(1)}, f32[8,8,128]{2,1,0:T(8,128)S(1)}, f32[8,8,128]{2,1,0:T(8,128)S(1)}, f32[16,8,128]{2,1,0:T(8,128)S(1)}, f32[16,8,128]{2,1,0:T(8,128)S(1)}) custom-call(f32[66,16]{1,0:T(8,128)S(1)} %copy-done.1, f32[32,384]{1,0:T(8,128)S(1)} %broadcast_subtract_fusion.delta_ref, f32[2,384]{1,0:T(2,128)S(1)} %reshape.38.lanes_ref, ...), custom_call_target="tpu_custom_call" | custom-call | flops 30000001024 | bytes 2284672 | tf_op jit(solution)/shard_map/pallas_call | solution.py:571
  58.3 2.5 %collective-permute-start = (f32[8,8,128]{2,1,0:T(8,128)S(1)}, f32[8,8,128]{2,1,0:T(8,128)S(1)}, u32[]{:S(2)}, u32[]{:S(2)}) collective-permute-start(f32[8,8,128]{2,1,0:T(8,128)S(1)} %get-tuple-element.14), channel_id=1, source_target_pairs={{0,1},{1,2},{2,3},{3,4},{4,5},{5,6},{6,7},{8,9},{9,10},{10,11},{11... | collective-permute-start | bytes 98312 | tf_op jit(solution)/shard_map/ppermute | solution.py:674
  60.8 0.1 add_convert_fusion.place_ref
  60.9 1.9 %collective-permute-start.1 = (f32[8,8,128]{2,1,0:T(8,128)S(1)}, f32[8,8,128]{2,1,0:T(8,128)S(1)}, u32[]{:S(2)}, u32[]{:S(2)}) collective-permute-start(f32[8,8,128]{2,1,0:T(8,128)S(1)} %get-tuple-element.15), channel_id=1, source_target_pairs={{1,0},{2,1},{3,2},{4,3},{5,4},{6,5},{7,6},{9,8},{10,9},{11,10},{12... | collective-permute-start | bytes 98312 | tf_op jit(solution)/shard_map/ppermute | solution.py:675
  62.8 0.0 collective-permute-done.before_ref
  62.8 3.3 %collective-permute-done.1.after_ref = f32[8,8,128]{2,1,0:T(8,128)S(1)} collective-permute-done((f32[8,8,128]{2,1,0:T(8,128)S(1)}, f32[8,8,128]{2,1,0:T(8,128)S(1)}, u32[]{:S(2)}, u32[]{:S(2)}) %collective-permute-start.1) | collective-permute-done | bytes 32800 | tf_op jit(solution)/shard_map/ppermute | solution.py:675
  66.1 2.1 %collective-permute-start.2 = (f32[24,8,128]{2,1,0:T(8,128)S(1)}, f32[24,8,128]{2,1,0:T(8,128)S(1)}, u32[]{:S(2)}, u32[]{:S(2)}) collective-permute-start(f32[24,8,128]{2,1,0:T(8,128)S(1)} %pad_maximum_fusion), channel_id=1, source_target_pairs={{0,8},{8,16},{16,24},{24,32},{32,40},{40,48},{48,56},{56,64},{64,7... | collective-permute-start | bytes 294920 | tf_op jit(solution)/shard_map/ppermute | solution.py:678
  68.3 5.5 %collective-permute-start.3 = (f32[24,8,128]{2,1,0:T(8,128)S(1)}, f32[24,8,128]{2,1,0:T(8,128)S(1)}, u32[]{:S(2)}, u32[]{:S(2)}) collective-permute-start(f32[24,8,128]{2,1,0:T(8,128)S(1)} %pad_maximum_fusion.1), channel_id=1, source_target_pairs={{8,0},{16,8},{24,16},{32,24},{40,32},{48,40},{56,48},{64,56},{72,6... | collective-permute-start | bytes 294920 | tf_op jit(solution)/shard_map/ppermute | solution.py:679
  73.7 6.6 %shard_map.58.refs_3_ = f32[16,128,256]{2,1,0:T(8,128)} custom-call(s32[4]{0:T(128)S(1)} %add_convert_fusion.place_ref, f32[8,8,128]{2,1,0:T(8,128)S(1)} %collective-permute-done.before_ref, f32[8,8,128]{2,1,0:T(8,128)S(1)} %collective-permute-done.1.after_ref, f32[32,128,128]{2,1,0:T(8,128)S(1)} %get-tuple-element.18.refs_0_.refs_2_), custom_call_target="tpu_custom_call" | custom-call | flops 10000000000 | bytes 2162704 | tf_op jit(solution)/shard_map/pallas_call | solution.py:571
  80.3 0.0 collective-permute-done.2.refs_0_
  80.3 0.0 collective-permute-done.3.refs_1_
  80.3 6.6 %shard_map.59 = f32[16,128,256]{2,1,0:T(8,128)} custom-call(s32[4]{0:T(128)S(1)} %add_convert_fusion.place_ref, f32[8,8,128]{2,1,0:T(8,128)S(1)} %collective-permute-done.before_ref, f32[8,8,128]{2,1,0:T(8,128)S(1)} %collective-permute-done.1.after_ref, f32[24,8,128]{2,1,0:T(8,128)S(1)} %collective-permute-done.2.refs_0_, ...), custom_call_target="tpu_custom_call", output_to_operand_aliasing={{}: (6, {})} | custom-call | flops 10000000000 | bytes 4456464 | tf_op jit(solution)/shard_map/pallas_call | solution.py:571
  (9 shorter events, 0.1 us)
Async XLA Ops:
  0.0 23.0 %copy-start = (s32[16,16,16]{2,1,0:T(8,128)S(1)}, s32[16,16,16]{2,1,0:T(8,128)}, u32[]{:S(2)}) copy-start(s32[16,16,16]{2,1,0:T(8,128)} %param.9) | copy-start | bytes 49156
  1.5 21.3 %slice-start = ((f32[66,16]{1,0:T(8,128)}), f32[2,16]{1,0:T(2,128)S(1)}, s32[]{:S(2)}) async-start(f32[66,16]{1,0:T(8,128)} %select_select_fusion.table_ref), calls=%async_computation.2 | async-start | bytes 2048 | tf_op jit(solution)/shard_map/slice | solution.py:652
  1.5 21.7 %slice-start.1 = ((f32[66,16]{1,0:T(8,128)}), f32[32,16]{1,0:T(8,128)S(1)}, s32[]{:S(2)}) async-start(f32[66,16]{1,0:T(8,128)} %select_select_fusion.table_ref), calls=%async_computation.3 | async-start | bytes 32768 | tf_op jit(solution)/shard_map/slice | solution.py:651
  11.9 20.8 %all-to-all-start = ((bf16[128,8,128]{2,1,0:T(8,128)(2,1)}), bf16[128,8,128]{2,1,0:T(8,128)(2,1)S(1)}, u32[]{:S(2)}, u32[]{:S(2)}) async-start(bf16[128,8,128]{2,1,0:T(8,128)(2,1)} %bitcast.15), calls=%async_computation | async-start | bytes 524288 | tf_op jit(solution)/shard_map/all_to_all | solution.py:623
  32.7 19.2 %copy-start.1 = (f32[66,16]{1,0:T(8,128)S(1)}, f32[66,16]{1,0:T(8,128)}, u32[]{:S(2)}) copy-start(f32[66,16]{1,0:T(8,128)} %select_select_fusion.table_ref) | copy-start | bytes 12676
  32.7 19.2 %copy-start.2 = (f32[32,128,128]{2,1,0:T(8,128)S(1)}, f32[32,128,128]{2,1,0:T(8,128)}, u32[]{:S(2)}) copy-start(f32[32,128,128]{2,1,0:T(8,128)} %get-tuple-element.12.image_ref) | copy-start | bytes 6291460
  37.4 14.5 %all-to-all-start.1 = ((bf16[128,4,128]{2,1,0:T(4,128)(2,1)}), bf16[128,4,128]{2,1,0:T(4,128)(2,1)S(1)}, u32[]{:S(2)}, u32[]{:S(2)}) async-start(bf16[128,4,128]{2,1,0:T(4,128)(2,1)} %bitcast.10), calls=%async_computation.1 | async-start | bytes 262144 | tf_op jit(solution)/shard_map/all_to_all | solution.py:647
  58.3 4.5 %collective-permute-start = (f32[8,8,128]{2,1,0:T(8,128)S(1)}, f32[8,8,128]{2,1,0:T(8,128)S(1)}, u32[]{:S(2)}, u32[]{:S(2)}) collective-permute-start(f32[8,8,128]{2,1,0:T(8,128)S(1)} %get-tuple-element.14), channel_id=1, source_target_pairs={{0,1},{1,2},{2,3},{3,4},{4,5},{5,6},{6,7},{8,9},{9,10},{10,11},{11... | collective-permute-start | bytes 98312 | tf_op jit(solution)/shard_map/ppermute | solution.py:674
  60.9 5.2 %collective-permute-start.1 = (f32[8,8,128]{2,1,0:T(8,128)S(1)}, f32[8,8,128]{2,1,0:T(8,128)S(1)}, u32[]{:S(2)}, u32[]{:S(2)}) collective-permute-start(f32[8,8,128]{2,1,0:T(8,128)S(1)} %get-tuple-element.15), channel_id=1, source_target_pairs={{1,0},{2,1},{3,2},{4,3},{5,4},{6,5},{7,6},{9,8},{10,9},{11,10},{12... | collective-permute-start | bytes 98312 | tf_op jit(solution)/shard_map/ppermute | solution.py:675
  66.1 14.2 %collective-permute-start.2 = (f32[24,8,128]{2,1,0:T(8,128)S(1)}, f32[24,8,128]{2,1,0:T(8,128)S(1)}, u32[]{:S(2)}, u32[]{:S(2)}) collective-permute-start(f32[24,8,128]{2,1,0:T(8,128)S(1)} %pad_maximum_fusion), channel_id=1, source_target_pairs={{0,8},{8,16},{16,24},{24,32},{32,40},{40,48},{48,56},{56,64},{64,7... | collective-permute-start | bytes 294920 | tf_op jit(solution)/shard_map/ppermute | solution.py:678
  68.3 12.0 %collective-permute-start.3 = (f32[24,8,128]{2,1,0:T(8,128)S(1)}, f32[24,8,128]{2,1,0:T(8,128)S(1)}, u32[]{:S(2)}, u32[]{:S(2)}) collective-permute-start(f32[24,8,128]{2,1,0:T(8,128)S(1)} %pad_maximum_fusion.1), channel_id=1, source_target_pairs={{8,0},{16,8},{24,16},{32,24},{40,32},{48,40},{56,48},{64,56},{72,6... | collective-permute-start | bytes 294920 | tf_op jit(solution)/shard_map/ppermute | solution.py:679

commit v6 on v5

--- a/solution.py
+++ b/solution.py
@@ -21,6 +21,7 @@
 PAIRS = PATCHES * PATCHES // 2
 PHASE = 4
 STRIDE = 4
+TABLE = 2 * PAIRS + 8
 MESSAGE = 8
 
 inverse_root = 0.7071067811865476
@@ -34,9 +35,9 @@
 
 def geometry(angle_ids):
     radians = angle_ids.astype(F32) * (math.pi / ALL_ANGLES)
-    cosine = jnp.cos(radians)[None] * inverse_root
-    sine = jnp.sin(radians)[None] * inverse_root
-    row = lax.broadcasted_iota(jnp.int32, (2 * PAIRS + 2, ANGLES), 0)
+    cosine = jnp.cos(radians) * inverse_root
+    sine = jnp.sin(radians) * inverse_root
+    row = lax.broadcasted_iota(jnp.int32, (TABLE, TILE), 0)
     patch = row & (PAIRS - 1)
     down = (patch >> 3).astype(F32) * SIDE - (TILE - 1) / 2.0
     across = (patch & (PATCHES - 1)).astype(F32) * SIDE - (TILE - 1) / 2.0
@@ -106,8 +107,9 @@
 
 
 def forward_kernel(
-    table_ref, own_ref, image_ref, given_ref, given_weight_ref,
-    out_ref, turned_ref, xt, rel, bands, tails, message, image0_ref, image1_ref, flat,
+    own_ref, angles_ref, image_ref, given_ref, given_weight_ref,
+    out_ref, turned_ref, geometry_ref, table_ref, xt, rel, bands, tails, message, image0_ref,
+    image1_ref, flat,
     measured_ref, weight_ref, sems, *sums,
 ):
     slices = ROWS // 2
@@ -128,6 +130,42 @@
     ]
     for copy in (*coming[0], *coming[1], *small):
         copy.start()
+    place = lax.broadcasted_iota(jnp.int32, (1, TILE), 1)
+    angles = jnp.zeros((1, TILE), jnp.int32)
+    for a in range(ANGLES):
+        angles = jnp.where(place == a, angles_ref[a], angles)
+    geometry_ref[...] = geometry(angles)
+    table = pltpu.make_async_copy(geometry_ref, table_ref, sems.at[10])
+    table.start()
+    for ref in sums:
+        ref[...] = jnp.zeros_like(ref)
+    def rows_of(u):
+        return [ref[pl.ds(u, slices, stride=TILE), :] for ref in (image0_ref, image1_ref)]
+
+    def flip(i, carry):
+        rows = []
+        for block in blocks_at(i // SIDE):
+            rows += rows_of(block * SIDE + i % SIDE)
+        flat[i] = jnp.concatenate(rows, axis=0).T
+        return carry
+
+    for part in range(2):
+        for copy in coming[part]:
+            copy.wait()
+        lax.fori_loop(part * SIDE, (part + 1) * SIDE, flip, 0, unroll=4)
+    for copy in small:
+        copy.wait()
+    going = pltpu.make_async_copy(flat, turned_ref, sems.at[0])
+    going.start()
+
+    def reflect(i, carry):
+        value = reflected(flat, i)
+        xt[pl.ds(pl.multiple_of(i * TILE, TILE), TILE), :] = value.astype(BF16)
+        return carry
+
+    lax.fori_loop(0, 2 * SIDE, reflect, 0, unroll=2)
+
+    table.wait()
     lane = lax.broadcasted_iota(jnp.int32, (BINS, PIX), 1)
     bin_at = lax.broadcasted_iota(jnp.int32, (BINS, PIX), 0).astype(F32)
     down = (lane // SIDE).astype(F32)
@@ -136,33 +174,6 @@
         rel[a * BINS : (a + 1) * BINS, :] = (
             down * table_ref[2 * PAIRS, a] + across * table_ref[2 * PAIRS + 1, a] - bin_at
         )
-    for ref in sums:
-        ref[...] = jnp.zeros_like(ref)
-    def rows_of(u):
-        return [ref[pl.ds(u, slices, stride=TILE), :] for ref in (image0_ref, image1_ref)]
-
-    def flip(i, carry):
-        rows = []
-        for block in blocks_at(i // SIDE):
-            rows += rows_of(block * SIDE + i % SIDE)
-        flat[i] = jnp.concatenate(rows, axis=0).T
-        return carry
-
-    for part in range(2):
-        for copy in coming[part]:
-            copy.wait()
-        lax.fori_loop(part * SIDE, (part + 1) * SIDE, flip, 0, unroll=4)
-    for copy in small:
-        copy.wait()
-    going = pltpu.make_async_copy(flat, turned_ref, sems.at[0])
-    going.start()
-
-    def reflect(i, carry):
-        value = reflected(flat, i)
-        xt[pl.ds(pl.multiple_of(i * TILE, TILE), TILE), :] = value.astype(BF16)
-        return carry
-
-    lax.fori_loop(0, 2 * SIDE, reflect, 0, unroll=2)
 
     def build(patch, band):
         for a in range(0, ANGLES, 2):
@@ -218,7 +229,6 @@
 ):
     coming = pltpu.make_async_copy(sent_ref, came, sem)
     coming.start()
-    low, high = sums[:8], sums[8:]
     blocks = 16
     per = 8
     groups = staged.shape[0] // (8 * per)
@@ -253,8 +263,8 @@
         ]
         for block, shift, value, slot in turned:
             tail = jnp.where(lane >= shift, value, 0.0)
-            low[slot][block] += tail
-            high[slot][block] += value - tail
+            sums[slot][block, 0] += tail
+            sums[slot][block, 1] += value - tail
         return carry
 
     lax.fori_loop(0, groups, add, 0)
@@ -262,9 +272,9 @@
     for b in range(blocks):
         total = jnp.zeros((8, TILE), F32)
         for slot in range(8):
-            here = low[slot][b]
+            here = sums[slot][b, 0]
             if b:
-                here = here + high[slot][b - 1]
+                here = here + sums[slot][b - 1, 1]
             total = total + jnp.where(sub == slot % 4, here, 0.0)
         home = pl.multiple_of((b * 8 + own_ref[0]) * MESSAGE, MESSAGE)
         given = got_ref[pl.ds(home, MESSAGE), :]
@@ -478,16 +488,15 @@
             (TV_STEPS + k, k, SIDE + TV_STEPS + k, False),
         ):
             mine = first[mine, span, :]
-            others = roll(other[others, span, :], 2 * ROWS)
-            swapped = roll(mine, 2 * ROWS)
+            others = other[others, span, :]
             if half == 0:
-                value = jnp.where(group == (3 if low else 2), others, swapped)
+                value = roll(jnp.where(group == (1 if low else 0), others, mine), 2 * ROWS)
                 outer = group == (0 if low else 1)
                 value = jnp.where(outer, first[target, span, :], value)
             else:
+                value = roll(jnp.where(group == (2 if low else 3), others, mine), 2 * ROWS)
                 step = roll(mine, ROWS if low else -ROWS)
-                value = jnp.where(group == (3 if low else 2), step, swapped)
-                value = jnp.where(group == (0 if low else 1), others, value)
+                value = jnp.where(group == (3 if low else 2), step, value)
             first[target, span, :] = value
 
     keep_lead = later | (has_before == 1)
@@ -593,17 +602,17 @@
     cols = lax.axis_size("col")
     slices = current_image.shape[0]
     both = ("row", "col")
-    table = geometry(angle_ids)
     half = VMEM((slices * TILE, TILE), F32)
 
     turned = jax.ShapeDtypeStruct((2 * SIDE, TILE, TILE), F32)
-    sent, image = call(
+    sent, image, table = call(
         forward_kernel,
-        (table, col_index.reshape(1)),
+        (col_index.reshape(1), angle_ids),
         (),
         (current_image, measured[:, 0], ray_weight[:, 0]),
-        (jax.ShapeDtypeStruct((rows * cols * MESSAGE, TILE), BF16), turned),
+        (jax.ShapeDtypeStruct((rows * cols * MESSAGE, TILE), BF16), turned, jax.ShapeDtypeStruct((TABLE, TILE), F32)),
         [
+            pltpu.SMEM((TABLE, TILE), F32),
             VMEM((2 * SIDE * TILE, TILE), BF16),
             VMEM((BAND, PIX), F32),
             VMEM((4 * PHASE, BAND, PIX), BF16),
@@ -614,7 +623,7 @@
             VMEM(turned.shape, F32),
             VMEM(measured[:, 0].shape, F32),
             VMEM(ray_weight[:, 0].shape, F32),
-            pltpu.SemaphoreType.DMA((10,)),
+            pltpu.SemaphoreType.DMA((11,)),
         ]
         + [VMEM((TILE, TILE), F32)] * ANGLES,
         30_000_000_000,
@@ -641,12 +650,13 @@
             VMEM((rows * cols * MESSAGE, TILE), BF16),
             pltpu.SemaphoreType.DMA,
         ]
-        + [VMEM((blocks, 8, TILE), F32)] * 16,
+        + [VMEM((blocks, 2, 8, TILE), F32)] * 8,
         10_000_000_000,
     )
     shadows = lax.all_to_all(
         out.reshape(rows * cols, 4, TILE), both, split_axis=0, concat_axis=0, tiled=True
     )
+    table = table[: 2 * PAIRS + 2, :ANGLES]
     bins = jnp.arange(BINS, dtype=F32)
     delta_lanes = (table[PAIRS : 2 * PAIRS, :, None] - bins).reshape(-1, BAND)
     angle_lanes = jnp.repeat(table[2 * PAIRS :], BINS, axis=1)
@@ -654,7 +664,7 @@
     edge = jax.ShapeDtypeStruct((TILE // 8, 8, TILE), F32)
     x, left, right, top, bottom = call(
         backward_kernel,
-        (table,),
+        (table[:PAIRS],),
         (delta_lanes, angle_lanes),
         (image, shadows.reshape(-1, TILE)),
         (turned, side, side, edge, edge),

time: 87.5 us -> 84.8 us (0.969)
  other arithmetic: 1.58 us -> 0.1 us
  local copies, waits for them, and re-layouts: 0.79 us -> 2.19 us
  waiting for transfers between devices: 21.4 us -> 20 us
  Pallas kernels: 34.8 us -> 33.5 us
    all_to_all x1, waiting for transfers between devices: 9.17 us -> 7.77 us  [local(): lax.all_to_all(sent.reshape(rows * cols, MESSAGE, TILE), both, split_axis...]
    pallas_call x5, Pallas kernels: 34.8 us -> 33.5 us  [call(): pl.pallas_call(kernel, out_shape=outs, in_specs=[smem] * len(scalars) + [...]
  transfers between devices with their start and end apart: 6 -> 6, of which waited for: 3 -> 3; matrix products, arithmetic and copies ran while one was open for 1% -> 3% of each run, Pallas kernels for 8% -> 8%
where the time goes in v6:
time: 84.8 us; the launch traced here: 84.3 us
  Pallas kernels  33.5 us (40%)
  starting transfers between devices  28.1 us (33%)
  waiting for transfers between devices  20 us (24%)
  local copies, waits for them, and re-layouts  2.19 us (3%)
    pallas_call x5, Pallas kernels, call(): pl.pallas_call(kernel, out_shape=outs, in_specs=[smem] * len(scalars) + [...  33.5 us
    all_to_all x1, starting transfers between devices, local(): lax.all_to_all(sent.reshape(rows * cols, MESSAGE, TILE), both, split_axis...  10.7 us
    all_to_all x1, waiting for transfers between devices, local(): lax.all_to_all(out.reshape(rows * cols, 4, TILE), both, split_axis=0, con...  8.96 us
    all_to_all x1, waiting for transfers between devices, local(): lax.all_to_all(sent.reshape(rows * cols, MESSAGE, TILE), both, split_axis...  7.77 us
    all_to_all x1, starting transfers between devices, local(): lax.all_to_all(out.reshape(rows * cols, 4, TILE), both, split_axis=0, con...  5.48 us
    ppermute x1, starting transfers between devices, local(): below = lax.ppermute(upward, 'row', [(i + 1, i) for i in range(rows - 1)])  5.45 us
    ppermute x1, waiting for transfers between devices, local(): after = lax.ppermute(left, 'col', [(i + 1, i) for i in range(cols - 1)])  3.28 us
    ppermute x1, starting transfers between devices, local(): before = lax.ppermute(right, 'col', [(i, i + 1) for i in range(cols - 1)])  2.45 us
  transfers between devices with their start and end apart: 6, of which 3 were waited for; matrix products, arithmetic and copies ran while one was open for 3% of the time, Pallas kernels for 8%

profile of v6, /device:TPU:9, one launch (start us, length us, event | category | flops | bytes accessed | tf_op | source)
XLA Modules:
  0.0 84.3 jit_solution(10697714478550686047)
XLA Ops:
  0.0 0.0 copy-start
  0.0 9.9 %shard_map.55 = (bf16[1024,128]{1,0:T(8,128)(2,1)}, f32[32,128,128]{2,1,0:T(8,128)}, f32[72,128]{1,0:T(8,128)}) custom-call(s32[1]{0:T(128)} %bitcast.4.own_ref, s32[16]{0:T(128)} %angles_ref.1, f32[16,128,256]{2,1,0:T(8,128)} %image_ref.1, f32[2,16,128]{2,1,0:T(8,128)} %bitcast.16, f32[2,128]{1,0:T(2,128)} %bitcast.17), custom_call_target="tpu_custom_call" | custom-call | flops 30000001024 | bytes 2114628 | tf_op jit(solution)/shard_map/pallas_call | solution.py:580
  9.9 10.7 %all-to-all-start = ((bf16[128,8,128]{2,1,0:T(8,128)(2,1)}), bf16[128,8,128]{2,1,0:T(8,128)(2,1)S(1)}, u32[]{:S(2)}, u32[]{:S(2)}) async-start(bf16[128,8,128]{2,1,0:T(8,128)(2,1)} %bitcast.15), calls=%async_computation | async-start | bytes 524288 | tf_op jit(solution)/shard_map/all_to_all | solution.py:632
  20.6 0.0 copy-done
  20.6 0.1 constant_dynamic-slice_fusion
  20.7 0.1 sub.23
  20.8 0.1 reshape.32.starts_ref
  21.0 0.7 slice.27
  21.6 0.1 broadcast_in_dim.2
  21.7 0.1 reshape.30.lanes_ref
  21.8 0.7 fusion
  22.6 0.1 sub.20
  22.7 0.2 sub.21
  22.8 7.8 %all-to-all-done = bf16[128,8,128]{2,1,0:T(8,128)(2,1)S(1)} async-done(((bf16[128,8,128]{2,1,0:T(8,128)(2,1)}), bf16[128,8,128]{2,1,0:T(8,128)(2,1)S(1)}, u32[]{:S(2)}, u32[]{:S(2)}) %all-to-all-start) | async-done | bytes 262176 | tf_op jit(solution)/shard_map/all_to_all | solution.py:632
  30.6 0.0 copy-start.1
  30.6 4.7 %shard_map.56 = bf16[512,128]{1,0:T(8,128)(2,1)} custom-call(s32[512]{0:T(512)S(1)} %reshape.32.starts_ref, s32[1]{0:T(128)} %bitcast.4.own_ref, bf16[1024,128]{1,0:T(8,128)(2,1)S(1)} %bitcast.13), custom_call_target="tpu_custom_call" | custom-call | flops 10000000000 | bytes 264196 | tf_op jit(solution)/shard_map/pallas_call | solution.py:580
  35.3 5.5 %all-to-all-start.1 = ((bf16[128,4,128]{2,1,0:T(4,128)(2,1)}), bf16[128,4,128]{2,1,0:T(4,128)(2,1)S(1)}, u32[]{:S(2)}, u32[]{:S(2)}) async-start(bf16[128,4,128]{2,1,0:T(4,128)(2,1)} %bitcast.10), calls=%async_computation.1 | async-start | bytes 262144 | tf_op jit(solution)/shard_map/all_to_all | solution.py:656
  40.8 9.0 %all-to-all-done.1 = bf16[128,4,128]{2,1,0:T(4,128)(2,1)S(1)} async-done(((bf16[128,4,128]{2,1,0:T(4,128)(2,1)}), bf16[128,4,128]{2,1,0:T(4,128)(2,1)S(1)}, u32[]{:S(2)}, u32[]{:S(2)}) %all-to-all-start.1) | async-done | bytes 131104 | tf_op jit(solution)/shard_map/all_to_all | solution.py:656
  49.7 0.0 copy-done.1
  49.7 6.1 %shard_map.57 = (f32[32,128,128]{2,1,0:T(8,128)S(1)}, f32[8,8,128]{2,1,0:T(8,128)S(1)}, f32[8,8,128]{2,1,0:T(8,128)S(1)}, f32[16,8,128]{2,1,0:T(8,128)S(1)}, f32[16,8,128]{2,1,0:T(8,128)S(1)}) custom-call(f32[32,16]{1,0:T(8,128)S(1)} %get-tuple-element.22.table_ref, f32[32,384]{1,0:T(8,128)S(1)} %broadcast_subtract_fusion.delta_ref, ...), custom_call_target="tpu_custom_call" | custom-call | flops 30000001024 | bytes 2282496 | tf_op jit(solution)/shard_map/pallas_call | solution.py:580
  55.9 2.5 %collective-permute-start = (f32[8,8,128]{2,1,0:T(8,128)S(1)}, f32[8,8,128]{2,1,0:T(8,128)S(1)}, u32[]{:S(2)}, u32[]{:S(2)}) collective-permute-start(f32[8,8,128]{2,1,0:T(8,128)S(1)} %get-tuple-element.16), channel_id=1, source_target_pairs={{0,1},{1,2},{2,3},{3,4},{4,5},{5,6},{6,7},{8,9},{9,10},{10,11},{11... | collective-permute-start | bytes 98312 | tf_op jit(solution)/shard_map/ppermute | solution.py:684
  58.3 0.1 add_convert_fusion.place_ref
  58.4 1.9 %collective-permute-start.1 = (f32[8,8,128]{2,1,0:T(8,128)S(1)}, f32[8,8,128]{2,1,0:T(8,128)S(1)}, u32[]{:S(2)}, u32[]{:S(2)}) collective-permute-start(f32[8,8,128]{2,1,0:T(8,128)S(1)} %get-tuple-element.17), channel_id=1, source_target_pairs={{1,0},{2,1},{3,2},{4,3},{5,4},{6,5},{7,6},{9,8},{10,9},{11,10},{12... | collective-permute-start | bytes 98312 | tf_op jit(solution)/shard_map/ppermute | solution.py:685
  60.3 0.0 collective-permute-done.before_ref
  60.3 3.3 %collective-permute-done.1.after_ref = f32[8,8,128]{2,1,0:T(8,128)S(1)} collective-permute-done((f32[8,8,128]{2,1,0:T(8,128)S(1)}, f32[8,8,128]{2,1,0:T(8,128)S(1)}, u32[]{:S(2)}, u32[]{:S(2)}) %collective-permute-start.1) | collective-permute-done | bytes 32800 | tf_op jit(solution)/shard_map/ppermute | solution.py:685
  63.6 2.1 %collective-permute-start.2 = (f32[24,8,128]{2,1,0:T(8,128)S(1)}, f32[24,8,128]{2,1,0:T(8,128)S(1)}, u32[]{:S(2)}, u32[]{:S(2)}) collective-permute-start(f32[24,8,128]{2,1,0:T(8,128)S(1)} %pad_maximum_fusion), channel_id=1, source_target_pairs={{0,8},{8,16},{16,24},{24,32},{32,40},{40,48},{48,56},{56,64},{64,7... | collective-permute-start | bytes 294920 | tf_op jit(solution)/shard_map/ppermute | solution.py:688
  65.8 5.5 %collective-permute-start.3 = (f32[24,8,128]{2,1,0:T(8,128)S(1)}, f32[24,8,128]{2,1,0:T(8,128)S(1)}, u32[]{:S(2)}, u32[]{:S(2)}) collective-permute-start(f32[24,8,128]{2,1,0:T(8,128)S(1)} %pad_maximum_fusion.1), channel_id=1, source_target_pairs={{8,0},{16,8},{24,16},{32,24},{40,32},{48,40},{56,48},{64,56},{72,6... | collective-permute-start | bytes 294920 | tf_op jit(solution)/shard_map/ppermute | solution.py:689
  71.2 6.4 %shard_map.58.refs_3_ = f32[16,128,256]{2,1,0:T(8,128)} custom-call(s32[4]{0:T(128)S(1)} %add_convert_fusion.place_ref, f32[8,8,128]{2,1,0:T(8,128)S(1)} %collective-permute-done.before_ref, f32[8,8,128]{2,1,0:T(8,128)S(1)} %collective-permute-done.1.after_ref, f32[32,128,128]{2,1,0:T(8,128)S(1)} %get-tuple-element.20.refs_0_.refs_2_), custom_call_target="tpu_custom_call" | custom-call | flops 10000000000 | bytes 2162704 | tf_op jit(solution)/shard_map/pallas_call | solution.py:580
  77.7 0.0 collective-permute-done.2.refs_0_
  77.7 0.0 collective-permute-done.3.refs_1_
  77.7 6.5 %shard_map.59 = f32[16,128,256]{2,1,0:T(8,128)} custom-call(s32[4]{0:T(128)S(1)} %add_convert_fusion.place_ref, f32[8,8,128]{2,1,0:T(8,128)S(1)} %collective-permute-done.before_ref, f32[8,8,128]{2,1,0:T(8,128)S(1)} %collective-permute-done.1.after_ref, f32[24,8,128]{2,1,0:T(8,128)S(1)} %collective-permute-done.2.refs_0_, ...), custom_call_target="tpu_custom_call", output_to_operand_aliasing={{}: (6, {})} | custom-call | flops 10000000000 | bytes 4456464 | tf_op jit(solution)/shard_map/pallas_call | solution.py:580
  (6 shorter events, 0.0 us)
Async XLA Ops:
  0.0 20.6 %copy-start = (s32[16,16,16]{2,1,0:T(8,128)S(1)}, s32[16,16,16]{2,1,0:T(8,128)}, u32[]{:S(2)}) copy-start(s32[16,16,16]{2,1,0:T(8,128)} %param.9) | copy-start | bytes 49156
  9.9 20.7 %all-to-all-start = ((bf16[128,8,128]{2,1,0:T(8,128)(2,1)}), bf16[128,8,128]{2,1,0:T(8,128)(2,1)S(1)}, u32[]{:S(2)}, u32[]{:S(2)}) async-start(bf16[128,8,128]{2,1,0:T(8,128)(2,1)} %bitcast.15), calls=%async_computation | async-start | bytes 524288 | tf_op jit(solution)/shard_map/all_to_all | solution.py:632
  30.6 19.1 %copy-start.1 = (f32[32,128,128]{2,1,0:T(8,128)S(1)}, f32[32,128,128]{2,1,0:T(8,128)}, u32[]{:S(2)}) copy-start(f32[32,128,128]{2,1,0:T(8,128)} %get-tuple-element.14.image_ref) | copy-start | bytes 6291460
  35.3 14.5 %all-to-all-start.1 = ((bf16[128,4,128]{2,1,0:T(4,128)(2,1)}), bf16[128,4,128]{2,1,0:T(4,128)(2,1)S(1)}, u32[]{:S(2)}, u32[]{:S(2)}) async-start(bf16[128,4,128]{2,1,0:T(4,128)(2,1)} %bitcast.10), calls=%async_computation.1 | async-start | bytes 262144 | tf_op jit(solution)/shard_map/all_to_all | solution.py:656
  55.9 4.5 %collective-permute-start = (f32[8,8,128]{2,1,0:T(8,128)S(1)}, f32[8,8,128]{2,1,0:T(8,128)S(1)}, u32[]{:S(2)}, u32[]{:S(2)}) collective-permute-start(f32[8,8,128]{2,1,0:T(8,128)S(1)} %get-tuple-element.16), channel_id=1, source_target_pairs={{0,1},{1,2},{2,3},{3,4},{4,5},{5,6},{6,7},{8,9},{9,10},{10,11},{11... | collective-permute-start | bytes 98312 | tf_op jit(solution)/shard_map/ppermute | solution.py:684
  58.4 5.2 %collective-permute-start.1 = (f32[8,8,128]{2,1,0:T(8,128)S(1)}, f32[8,8,128]{2,1,0:T(8,128)S(1)}, u32[]{:S(2)}, u32[]{:S(2)}) collective-permute-start(f32[8,8,128]{2,1,0:T(8,128)S(1)} %get-tuple-element.17), channel_id=1, source_target_pairs={{1,0},{2,1},{3,2},{4,3},{5,4},{6,5},{7,6},{9,8},{10,9},{11,10},{12... | collective-permute-start | bytes 98312 | tf_op jit(solution)/shard_map/ppermute | solution.py:685
  63.6 14.0 %collective-permute-start.2 = (f32[24,8,128]{2,1,0:T(8,128)S(1)}, f32[24,8,128]{2,1,0:T(8,128)S(1)}, u32[]{:S(2)}, u32[]{:S(2)}) collective-permute-start(f32[24,8,128]{2,1,0:T(8,128)S(1)} %pad_maximum_fusion), channel_id=1, source_target_pairs={{0,8},{8,16},{16,24},{24,32},{32,40},{40,48},{48,56},{56,64},{64,7... | collective-permute-start | bytes 294920 | tf_op jit(solution)/shard_map/ppermute | solution.py:688
  65.8 11.9 %collective-permute-start.3 = (f32[24,8,128]{2,1,0:T(8,128)S(1)}, f32[24,8,128]{2,1,0:T(8,128)S(1)}, u32[]{:S(2)}, u32[]{:S(2)}) collective-permute-start(f32[24,8,128]{2,1,0:T(8,128)S(1)} %pad_maximum_fusion.1), channel_id=1, source_target_pairs={{8,0},{16,8},{24,16},{32,24},{40,32},{48,40},{56,48},{64,56},{72,6... | collective-permute-start | bytes 294920 | tf_op jit(solution)/shard_map/ppermute | solution.py:689

commit v7 on v6

--- a/solution.py
+++ b/solution.py
@@ -152,7 +152,7 @@
     for part in range(2):
         for copy in coming[part]:
             copy.wait()
-        lax.fori_loop(part * SIDE, (part + 1) * SIDE, flip, 0, unroll=4)
+        lax.fori_loop(part * SIDE, (part + 1) * SIDE, flip, 0, unroll=8)
     for copy in small:
         copy.wait()
     going = pltpu.make_async_copy(flat, turned_ref, sems.at[0])
@@ -225,10 +225,8 @@
 
 
 def owner_kernel(
-    starts_ref, own_ref, sent_ref, out_ref, wide, filt, staged, ramp_ref, got_ref, came, sem, *sums
+    starts_ref, own_ref, sent_ref, out_ref, wide, filt, staged, ramp_ref, got_ref, *sums
 ):
-    coming = pltpu.make_async_copy(sent_ref, came, sem)
-    coming.start()
     blocks = 16
     per = 8
     groups = staged.shape[0] // (8 * per)
@@ -247,8 +245,7 @@
     ramp = jnp.where(offset == 0, 0.25, ramp)
     ramp = jnp.where(jnp.abs(offset) < TILE, ramp, 0.0)
     ramp_ref[...] = ramp
-    coming.wait()
-    got_ref[...] = came[...].astype(F32)
+    got_ref[...] = sent_ref[...].astype(F32)
 
     def add(g, carry):
         turned = []
@@ -316,13 +313,11 @@
 
 
 def backward_kernel(
-    table_ref, delta_ref, lanes_ref, image_ref, sent_ref,
+    table_ref, delta_ref, lanes_ref, got_ref, image_ref,
     final_ref, left_ref, right_ref, top_ref, bottom_ref,
-    rel, bands, shadows, staged, mirror, update, image, got_ref, sems,
+    rel, bands, shadows, staged, mirror, update, image, sems,
 ):
     slices = ROWS // 2
-    arriving = pltpu.make_async_copy(sent_ref, got_ref, sems.at[1])
-    arriving.start()
     coming = pltpu.make_async_copy(image_ref, image, sems.at[0])
     coming.start()
     pixel = lax.broadcasted_iota(jnp.int32, (PIX, BAND), 0)
@@ -330,7 +325,6 @@
         (pixel // SIDE).astype(F32) * lanes_ref[0:1, :]
         + (pixel % SIDE).astype(F32) * lanes_ref[1:2, :]
     )
-    arriving.wait()
     staged[...] = got_ref[...].astype(F32)
     mirror[...] = jnp.dot(got_ref[...], reversal(), preferred_element_type=F32)
     for a in range(ANGLES):
@@ -638,8 +632,8 @@
     out = call(
         owner_kernel,
         (starts, col_index.reshape(1)),
+        (got.reshape(-1, TILE),),
         (),
-        (got.reshape(-1, TILE),),
         jax.ShapeDtypeStruct((rows * cols * 4, TILE), BF16),
         [
             VMEM((2 * blocks, 3 * TILE), F32),
@@ -647,8 +641,6 @@
             VMEM((rows * cols * 4, TILE), F32),
             VMEM((3 * TILE, TILE), F32),
             VMEM((rows * cols * MESSAGE, TILE), F32),
-            VMEM((rows * cols * MESSAGE, TILE), BF16),
-            pltpu.SemaphoreType.DMA,
         ]
         + [VMEM((blocks, 2, 8, TILE), F32)] * 8,
         10_000_000_000,
@@ -665,8 +657,8 @@
     x, left, right, top, bottom = call(
         backward_kernel,
         (table[:PAIRS],),
-        (delta_lanes, angle_lanes),
-        (image, shadows.reshape(-1, TILE)),
+        (delta_lanes, angle_lanes, shadows.reshape(-1, TILE)),
+        (image,),
         (turned, side, side, edge, edge),
         [
             VMEM((PIX, BAND), F32),
@@ -676,7 +668,6 @@
             VMEM((rows * cols * 4, TILE), F32),
             VMEM(turned.shape, F32),
             VMEM(turned.shape, F32),
-            VMEM((rows * cols * 4, TILE), BF16),
             pltpu.SemaphoreType.DMA((2,)),
         ],
         30_000_000_000,

time: 84.8 us -> 84.4 us (level)
  no operation moved by 1% of the time
where the time goes in v7:
time: 84.4 us; the launch traced here: 83.9 us
  Pallas kernels  33.1 us (39%)
  starting transfers between devices  28.1 us (33%)
  waiting for transfers between devices  20 us (24%)
  local copies, waits for them, and re-layouts  2.19 us (3%)
    pallas_call x5, Pallas kernels, call(): pl.pallas_call(kernel, out_shape=outs, in_specs=[smem] * len(scalars) + [...  33.1 us
    all_to_all x1, starting transfers between devices, local(): lax.all_to_all(sent.reshape(rows * cols, MESSAGE, TILE), both, split_axis...  10.7 us
    all_to_all x1, waiting for transfers between devices, local(): lax.all_to_all(out.reshape(rows * cols, 4, TILE), both, split_axis=0, con...  8.96 us
    all_to_all x1, waiting for transfers between devices, local(): lax.all_to_all(sent.reshape(rows * cols, MESSAGE, TILE), both, split_axis...  7.77 us
    all_to_all x1, starting transfers between devices, local(): lax.all_to_all(out.reshape(rows * cols, 4, TILE), both, split_axis=0, con...  5.47 us
    ppermute x1, starting transfers between devices, local(): below = lax.ppermute(upward, 'row', [(i + 1, i) for i in range(rows - 1)])  5.45 us
    ppermute x1, waiting for transfers between devices, local(): after = lax.ppermute(left, 'col', [(i + 1, i) for i in range(cols - 1)])  3.28 us
    ppermute x1, starting transfers between devices, local(): before = lax.ppermute(right, 'col', [(i, i + 1) for i in range(cols - 1)])  2.45 us
  transfers between devices with their start and end apart: 6, of which 3 were waited for; matrix products, arithmetic and copies ran while one was open for 3% of the time, Pallas kernels for 8%

profile of v7, /device:TPU:9, one launch (start us, length us, event | category | flops | bytes accessed | tf_op | source)
XLA Modules:
  0.0 83.9 jit_solution(181365594906261736)
XLA Ops:
  0.0 0.0 copy-start
  0.0 9.6 %shard_map.55 = (bf16[1024,128]{1,0:T(8,128)(2,1)}, f32[32,128,128]{2,1,0:T(8,128)}, f32[72,128]{1,0:T(8,128)}) custom-call(s32[1]{0:T(128)} %bitcast.4.own_ref, s32[16]{0:T(128)} %angles_ref.1, f32[16,128,256]{2,1,0:T(8,128)} %image_ref.1, f32[2,16,128]{2,1,0:T(8,128)} %bitcast.16, f32[2,128]{1,0:T(2,128)} %bitcast.17), custom_call_target="tpu_custom_call" | custom-call | flops 30000001024 | bytes 2114628 | tf_op jit(solution)/shard_map/pallas_call | solution.py:574
  9.6 10.7 %all-to-all-start = ((bf16[128,8,128]{2,1,0:T(8,128)(2,1)}), bf16[128,8,128]{2,1,0:T(8,128)(2,1)S(1)}, u32[]{:S(2)}, u32[]{:S(2)}) async-start(bf16[128,8,128]{2,1,0:T(8,128)(2,1)} %bitcast.15), calls=%async_computation | async-start | bytes 524288 | tf_op jit(solution)/shard_map/all_to_all | solution.py:626
  20.3 0.0 copy-done
  20.3 0.1 constant_dynamic-slice_fusion
  20.5 0.1 sub.23
  20.6 0.1 reshape.32.starts_ref
  20.7 0.7 slice.27
  21.4 0.1 broadcast_in_dim.2
  21.4 0.1 reshape.30.lanes_ref
  21.5 0.7 fusion
  22.3 0.1 sub.20
  22.4 0.2 sub.21
  22.6 7.8 %all-to-all-done = bf16[128,8,128]{2,1,0:T(8,128)(2,1)S(1)} async-done(((bf16[128,8,128]{2,1,0:T(8,128)(2,1)}), bf16[128,8,128]{2,1,0:T(8,128)(2,1)S(1)}, u32[]{:S(2)}, u32[]{:S(2)}) %all-to-all-start) | async-done | bytes 262176 | tf_op jit(solution)/shard_map/all_to_all | solution.py:626
  30.3 0.0 copy-start.1
  30.3 4.6 %shard_map.56 = bf16[512,128]{1,0:T(8,128)(2,1)} custom-call(s32[512]{0:T(512)S(1)} %reshape.32.starts_ref, s32[1]{0:T(128)} %bitcast.4.own_ref, bf16[1024,128]{1,0:T(8,128)(2,1)S(1)} %bitcast.13), custom_call_target="tpu_custom_call" | custom-call | flops 10000000000 | bytes 264196 | tf_op jit(solution)/shard_map/pallas_call | solution.py:574
  35.0 5.5 %all-to-all-start.1 = ((bf16[128,4,128]{2,1,0:T(4,128)(2,1)}), bf16[128,4,128]{2,1,0:T(4,128)(2,1)S(1)}, u32[]{:S(2)}, u32[]{:S(2)}) async-start(bf16[128,4,128]{2,1,0:T(4,128)(2,1)} %bitcast.10), calls=%async_computation.1 | async-start | bytes 262144 | tf_op jit(solution)/shard_map/all_to_all | solution.py:648
  40.5 9.0 %all-to-all-done.1 = bf16[128,4,128]{2,1,0:T(4,128)(2,1)S(1)} async-done(((bf16[128,4,128]{2,1,0:T(4,128)(2,1)}), bf16[128,4,128]{2,1,0:T(4,128)(2,1)S(1)}, u32[]{:S(2)}, u32[]{:S(2)}) %all-to-all-start.1) | async-done | bytes 131104 | tf_op jit(solution)/shard_map/all_to_all | solution.py:648
  49.4 0.0 copy-done.1
  49.4 6.1 %shard_map.57 = (f32[32,128,128]{2,1,0:T(8,128)S(1)}, f32[8,8,128]{2,1,0:T(8,128)S(1)}, f32[8,8,128]{2,1,0:T(8,128)S(1)}, f32[16,8,128]{2,1,0:T(8,128)S(1)}, f32[16,8,128]{2,1,0:T(8,128)S(1)}) custom-call(f32[32,16]{1,0:T(8,128)S(1)} %get-tuple-element.22.table_ref, f32[32,384]{1,0:T(8,128)S(1)} %broadcast_subtract_fusion.delta_ref, ...), custom_call_target="tpu_custom_call" | custom-call | flops 30000001024 | bytes 2282496 | tf_op jit(solution)/shard_map/pallas_call | solution.py:574
  55.5 2.4 %collective-permute-start = (f32[8,8,128]{2,1,0:T(8,128)S(1)}, f32[8,8,128]{2,1,0:T(8,128)S(1)}, u32[]{:S(2)}, u32[]{:S(2)}) collective-permute-start(f32[8,8,128]{2,1,0:T(8,128)S(1)} %get-tuple-element.16), channel_id=1, source_target_pairs={{0,1},{1,2},{2,3},{3,4},{4,5},{5,6},{6,7},{8,9},{9,10},{10,11},{11... | collective-permute-start | bytes 98312 | tf_op jit(solution)/shard_map/ppermute | solution.py:675
  57.9 0.1 add_convert_fusion.place_ref
  58.0 1.9 %collective-permute-start.1 = (f32[8,8,128]{2,1,0:T(8,128)S(1)}, f32[8,8,128]{2,1,0:T(8,128)S(1)}, u32[]{:S(2)}, u32[]{:S(2)}) collective-permute-start(f32[8,8,128]{2,1,0:T(8,128)S(1)} %get-tuple-element.17), channel_id=1, source_target_pairs={{1,0},{2,1},{3,2},{4,3},{5,4},{6,5},{7,6},{9,8},{10,9},{11,10},{12... | collective-permute-start | bytes 98312 | tf_op jit(solution)/shard_map/ppermute | solution.py:676
  59.9 0.0 collective-permute-done.before_ref
  60.0 3.3 %collective-permute-done.1.after_ref = f32[8,8,128]{2,1,0:T(8,128)S(1)} collective-permute-done((f32[8,8,128]{2,1,0:T(8,128)S(1)}, f32[8,8,128]{2,1,0:T(8,128)S(1)}, u32[]{:S(2)}, u32[]{:S(2)}) %collective-permute-start.1) | collective-permute-done | bytes 32800 | tf_op jit(solution)/shard_map/ppermute | solution.py:676
  63.2 2.1 %collective-permute-start.2 = (f32[24,8,128]{2,1,0:T(8,128)S(1)}, f32[24,8,128]{2,1,0:T(8,128)S(1)}, u32[]{:S(2)}, u32[]{:S(2)}) collective-permute-start(f32[24,8,128]{2,1,0:T(8,128)S(1)} %pad_maximum_fusion), channel_id=1, source_target_pairs={{0,8},{8,16},{16,24},{24,32},{32,40},{40,48},{48,56},{56,64},{64,7... | collective-permute-start | bytes 294920 | tf_op jit(solution)/shard_map/ppermute | solution.py:679
  65.4 5.5 %collective-permute-start.3 = (f32[24,8,128]{2,1,0:T(8,128)S(1)}, f32[24,8,128]{2,1,0:T(8,128)S(1)}, u32[]{:S(2)}, u32[]{:S(2)}) collective-permute-start(f32[24,8,128]{2,1,0:T(8,128)S(1)} %pad_maximum_fusion.1), channel_id=1, source_target_pairs={{8,0},{16,8},{24,16},{32,24},{40,32},{48,40},{56,48},{64,56},{72,6... | collective-permute-start | bytes 294920 | tf_op jit(solution)/shard_map/ppermute | solution.py:680
  70.9 6.4 %shard_map.58.refs_3_ = f32[16,128,256]{2,1,0:T(8,128)} custom-call(s32[4]{0:T(128)S(1)} %add_convert_fusion.place_ref, f32[8,8,128]{2,1,0:T(8,128)S(1)} %collective-permute-done.before_ref, f32[8,8,128]{2,1,0:T(8,128)S(1)} %collective-permute-done.1.after_ref, f32[32,128,128]{2,1,0:T(8,128)S(1)} %get-tuple-element.20.refs_0_.refs_2_), custom_call_target="tpu_custom_call" | custom-call | flops 10000000000 | bytes 2162704 | tf_op jit(solution)/shard_map/pallas_call | solution.py:574
  77.3 0.0 collective-permute-done.2.refs_0_
  77.3 0.0 collective-permute-done.3.refs_1_
  77.3 6.5 %shard_map.59 = f32[16,128,256]{2,1,0:T(8,128)} custom-call(s32[4]{0:T(128)S(1)} %add_convert_fusion.place_ref, f32[8,8,128]{2,1,0:T(8,128)S(1)} %collective-permute-done.before_ref, f32[8,8,128]{2,1,0:T(8,128)S(1)} %collective-permute-done.1.after_ref, f32[24,8,128]{2,1,0:T(8,128)S(1)} %collective-permute-done.2.refs_0_, ...), custom_call_target="tpu_custom_call", output_to_operand_aliasing={{}: (6, {})} | custom-call | flops 10000000000 | bytes 4456464 | tf_op jit(solution)/shard_map/pallas_call | solution.py:574
  (6 shorter events, 0.0 us)
Async XLA Ops:
  0.0 20.3 %copy-start = (s32[16,16,16]{2,1,0:T(8,128)S(1)}, s32[16,16,16]{2,1,0:T(8,128)}, u32[]{:S(2)}) copy-start(s32[16,16,16]{2,1,0:T(8,128)} %param.9) | copy-start | bytes 49156
  9.6 20.8 %all-to-all-start = ((bf16[128,8,128]{2,1,0:T(8,128)(2,1)}), bf16[128,8,128]{2,1,0:T(8,128)(2,1)S(1)}, u32[]{:S(2)}, u32[]{:S(2)}) async-start(bf16[128,8,128]{2,1,0:T(8,128)(2,1)} %bitcast.15), calls=%async_computation | async-start | bytes 524288 | tf_op jit(solution)/shard_map/all_to_all | solution.py:626
  30.3 19.1 %copy-start.1 = (f32[32,128,128]{2,1,0:T(8,128)S(1)}, f32[32,128,128]{2,1,0:T(8,128)}, u32[]{:S(2)}) copy-start(f32[32,128,128]{2,1,0:T(8,128)} %get-tuple-element.15.image_ref) | copy-start | bytes 6291460
  35.0 14.5 %all-to-all-start.1 = ((bf16[128,4,128]{2,1,0:T(4,128)(2,1)}), bf16[128,4,128]{2,1,0:T(4,128)(2,1)S(1)}, u32[]{:S(2)}, u32[]{:S(2)}) async-start(bf16[128,4,128]{2,1,0:T(4,128)(2,1)} %bitcast.10), calls=%async_computation.1 | async-start | bytes 262144 | tf_op jit(solution)/shard_map/all_to_all | solution.py:648
  55.5 4.5 %collective-permute-start = (f32[8,8,128]{2,1,0:T(8,128)S(1)}, f32[8,8,128]{2,1,0:T(8,128)S(1)}, u32[]{:S(2)}, u32[]{:S(2)}) collective-permute-start(f32[8,8,128]{2,1,0:T(8,128)S(1)} %get-tuple-element.16), channel_id=1, source_target_pairs={{0,1},{1,2},{2,3},{3,4},{4,5},{5,6},{6,7},{8,9},{9,10},{10,11},{11... | collective-permute-start | bytes 98312 | tf_op jit(solution)/shard_map/ppermute | solution.py:675
  58.0 5.2 %collective-permute-start.1 = (f32[8,8,128]{2,1,0:T(8,128)S(1)}, f32[8,8,128]{2,1,0:T(8,128)S(1)}, u32[]{:S(2)}, u32[]{:S(2)}) collective-permute-start(f32[8,8,128]{2,1,0:T(8,128)S(1)} %get-tuple-element.17), channel_id=1, source_target_pairs={{1,0},{2,1},{3,2},{4,3},{5,4},{6,5},{7,6},{9,8},{10,9},{11,10},{12... | collective-permute-start | bytes 98312 | tf_op jit(solution)/shard_map/ppermute | solution.py:676
  63.2 14.0 %collective-permute-start.2 = (f32[24,8,128]{2,1,0:T(8,128)S(1)}, f32[24,8,128]{2,1,0:T(8,128)S(1)}, u32[]{:S(2)}, u32[]{:S(2)}) collective-permute-start(f32[24,8,128]{2,1,0:T(8,128)S(1)} %pad_maximum_fusion), channel_id=1, source_target_pairs={{0,8},{8,16},{16,24},{24,32},{32,40},{40,48},{48,56},{56,64},{64,7... | collective-permute-start | bytes 294920 | tf_op jit(solution)/shard_map/ppermute | solution.py:679
  65.4 11.9 %collective-permute-start.3 = (f32[24,8,128]{2,1,0:T(8,128)S(1)}, f32[24,8,128]{2,1,0:T(8,128)S(1)}, u32[]{:S(2)}, u32[]{:S(2)}) collective-permute-start(f32[24,8,128]{2,1,0:T(8,128)S(1)} %pad_maximum_fusion.1), channel_id=1, source_target_pairs={{8,0},{16,8},{24,16},{32,24},{40,32},{48,40},{56,48},{64,56},{72,6... | collective-permute-start | bytes 294920 | tf_op jit(solution)/shard_map/ppermute | solution.py:680

commit v8 on v7

--- a/solution.py
+++ b/solution.py
@@ -20,7 +20,7 @@
 BAND = ANGLES * BINS
 PAIRS = PATCHES * PATCHES // 2
 PHASE = 4
-STRIDE = 4
+STRIDE = 8
 TABLE = 2 * PAIRS + 8
 MESSAGE = 8
 
@@ -152,7 +152,7 @@
     for part in range(2):
         for copy in coming[part]:
             copy.wait()
-        lax.fori_loop(part * SIDE, (part + 1) * SIDE, flip, 0, unroll=8)
+        lax.fori_loop(part * SIDE, (part + 1) * SIDE, flip, 0, unroll=16)
     for copy in small:
         copy.wait()
     going = pltpu.make_async_copy(flat, turned_ref, sems.at[0])

time: 84.4 us -> 82.9 us (0.982)
  Pallas kernels: 33.1 us -> 31.7 us
    pallas_call x5, Pallas kernels: 33.1 us -> 31.7 us  [call(): pl.pallas_call(kernel, out_shape=outs, in_specs=[smem] * len(scalars) + [...]
  transfers between devices with their start and end apart: 6 -> 6, of which waited for: 3 -> 3; matrix products, arithmetic and copies ran while one was open for 3% -> 3% of each run, Pallas kernels for 8% -> 7%
where the time goes in v8:
time: 82.9 us; the launch traced here: 82.5 us
  Pallas kernels  31.7 us (38%)
  starting transfers between devices  28.1 us (34%)
  waiting for transfers between devices  20 us (24%)
  local copies, waits for them, and re-layouts  2.19 us (3%)
    pallas_call x5, Pallas kernels, call(): pl.pallas_call(kernel, out_shape=outs, in_specs=[smem] * len(scalars) + [...  31.7 us
    all_to_all x1, starting transfers between devices, local(): lax.all_to_all(sent.reshape(rows * cols, MESSAGE, TILE), both, split_axis...  10.7 us
    all_to_all x1, waiting for transfers between devices, local(): lax.all_to_all(out.reshape(rows * cols, 4, TILE), both, split_axis=0, con...  8.96 us
    all_to_all x1, waiting for transfers between devices, local(): lax.all_to_all(sent.reshape(rows * cols, MESSAGE, TILE), both, split_axis...  7.77 us
    all_to_all x1, starting transfers between devices, local(): lax.all_to_all(out.reshape(rows * cols, 4, TILE), both, split_axis=0, con...  5.47 us
    ppermute x1, starting transfers between devices, local(): below = lax.ppermute(upward, 'row', [(i + 1, i) for i in range(rows - 1)])  5.45 us
    ppermute x1, waiting for transfers between devices, local(): after = lax.ppermute(left, 'col', [(i + 1, i) for i in range(cols - 1)])  3.28 us
    ppermute x1, starting transfers between devices, local(): before = lax.ppermute(right, 'col', [(i, i + 1) for i in range(cols - 1)])  2.45 us
  transfers between devices with their start and end apart: 6, of which 3 were waited for; matrix products, arithmetic and copies ran while one was open for 3% of the time, Pallas kernels for 7%

profile of v8, /device:TPU:9, one launch (start us, length us, event | category | flops | bytes accessed | tf_op | source)
XLA Modules:
  0.0 82.5 jit_solution(11596981264293454688)
XLA Ops:
  0.0 0.0 copy-start
  0.0 8.7 %shard_map.55 = (bf16[1024,128]{1,0:T(8,128)(2,1)}, f32[32,128,128]{2,1,0:T(8,128)}, f32[72,128]{1,0:T(8,128)}) custom-call(s32[1]{0:T(128)} %bitcast.4.own_ref, s32[16]{0:T(128)} %angles_ref.1, f32[16,128,256]{2,1,0:T(8,128)} %image_ref.1, f32[2,16,128]{2,1,0:T(8,128)} %bitcast.16, f32[2,128]{1,0:T(2,128)} %bitcast.17), custom_call_target="tpu_custom_call" | custom-call | flops 30000001024 | bytes 2114628 | tf_op jit(solution)/shard_map/pallas_call | solution.py:574
  8.7 10.7 %all-to-all-start = ((bf16[128,8,128]{2,1,0:T(8,128)(2,1)}), bf16[128,8,128]{2,1,0:T(8,128)(2,1)S(1)}, u32[]{:S(2)}, u32[]{:S(2)}) async-start(bf16[128,8,128]{2,1,0:T(8,128)(2,1)} %bitcast.15), calls=%async_computation | async-start | bytes 524288 | tf_op jit(solution)/shard_map/all_to_all | solution.py:626
  19.5 0.0 copy-done
  19.5 0.1 constant_dynamic-slice_fusion
  19.6 0.1 sub.23
  19.7 0.1 reshape.32.starts_ref
  19.9 0.7 slice.27
  20.5 0.1 broadcast_in_dim.2
  20.6 0.1 reshape.30.lanes_ref
  20.7 0.7 fusion
  21.4 0.1 sub.20
  21.6 0.2 sub.21
  21.7 7.8 %all-to-all-done = bf16[128,8,128]{2,1,0:T(8,128)(2,1)S(1)} async-done(((bf16[128,8,128]{2,1,0:T(8,128)(2,1)}), bf16[128,8,128]{2,1,0:T(8,128)(2,1)S(1)}, u32[]{:S(2)}, u32[]{:S(2)}) %all-to-all-start) | async-done | bytes 262176 | tf_op jit(solution)/shard_map/all_to_all | solution.py:626
  29.5 0.0 copy-start.1
  29.5 4.6 %shard_map.56 = bf16[512,128]{1,0:T(8,128)(2,1)} custom-call(s32[512]{0:T(512)S(1)} %reshape.32.starts_ref, s32[1]{0:T(128)} %bitcast.4.own_ref, bf16[1024,128]{1,0:T(8,128)(2,1)S(1)} %bitcast.13), custom_call_target="tpu_custom_call" | custom-call | flops 10000000000 | bytes 264196 | tf_op jit(solution)/shard_map/pallas_call | solution.py:574
  34.1 5.5 %all-to-all-start.1 = ((bf16[128,4,128]{2,1,0:T(4,128)(2,1)}), bf16[128,4,128]{2,1,0:T(4,128)(2,1)S(1)}, u32[]{:S(2)}, u32[]{:S(2)}) async-start(bf16[128,4,128]{2,1,0:T(4,128)(2,1)} %bitcast.10), calls=%async_computation.1 | async-start | bytes 262144 | tf_op jit(solution)/shard_map/all_to_all | solution.py:648
  39.6 9.0 %all-to-all-done.1 = bf16[128,4,128]{2,1,0:T(4,128)(2,1)S(1)} async-done(((bf16[128,4,128]{2,1,0:T(4,128)(2,1)}), bf16[128,4,128]{2,1,0:T(4,128)(2,1)S(1)}, u32[]{:S(2)}, u32[]{:S(2)}) %all-to-all-start.1) | async-done | bytes 131104 | tf_op jit(solution)/shard_map/all_to_all | solution.py:648
  48.6 0.0 copy-done.1
  48.6 6.1 %shard_map.57 = (f32[32,128,128]{2,1,0:T(8,128)S(1)}, f32[8,8,128]{2,1,0:T(8,128)S(1)}, f32[8,8,128]{2,1,0:T(8,128)S(1)}, f32[16,8,128]{2,1,0:T(8,128)S(1)}, f32[16,8,128]{2,1,0:T(8,128)S(1)}) custom-call(f32[32,16]{1,0:T(8,128)S(1)} %get-tuple-element.22.table_ref, f32[32,384]{1,0:T(8,128)S(1)} %broadcast_subtract_fusion.delta_ref, ...), custom_call_target="tpu_custom_call" | custom-call | flops 30000001024 | bytes 2282496 | tf_op jit(solution)/shard_map/pallas_call | solution.py:574
  54.6 2.5 %collective-permute-start = (f32[8,8,128]{2,1,0:T(8,128)S(1)}, f32[8,8,128]{2,1,0:T(8,128)S(1)}, u32[]{:S(2)}, u32[]{:S(2)}) collective-permute-start(f32[8,8,128]{2,1,0:T(8,128)S(1)} %get-tuple-element.16), channel_id=1, source_target_pairs={{0,1},{1,2},{2,3},{3,4},{4,5},{5,6},{6,7},{8,9},{9,10},{10,11},{11... | collective-permute-start | bytes 98312 | tf_op jit(solution)/shard_map/ppermute | solution.py:675
  57.1 0.1 add_convert_fusion.place_ref
  57.2 1.9 %collective-permute-start.1 = (f32[8,8,128]{2,1,0:T(8,128)S(1)}, f32[8,8,128]{2,1,0:T(8,128)S(1)}, u32[]{:S(2)}, u32[]{:S(2)}) collective-permute-start(f32[8,8,128]{2,1,0:T(8,128)S(1)} %get-tuple-element.17), channel_id=1, source_target_pairs={{1,0},{2,1},{3,2},{4,3},{5,4},{6,5},{7,6},{9,8},{10,9},{11,10},{12... | collective-permute-start | bytes 98312 | tf_op jit(solution)/shard_map/ppermute | solution.py:676
  59.1 0.0 collective-permute-done.before_ref
  59.1 3.3 %collective-permute-done.1.after_ref = f32[8,8,128]{2,1,0:T(8,128)S(1)} collective-permute-done((f32[8,8,128]{2,1,0:T(8,128)S(1)}, f32[8,8,128]{2,1,0:T(8,128)S(1)}, u32[]{:S(2)}, u32[]{:S(2)}) %collective-permute-start.1) | collective-permute-done | bytes 32800 | tf_op jit(solution)/shard_map/ppermute | solution.py:676
  62.4 2.1 %collective-permute-start.2 = (f32[24,8,128]{2,1,0:T(8,128)S(1)}, f32[24,8,128]{2,1,0:T(8,128)S(1)}, u32[]{:S(2)}, u32[]{:S(2)}) collective-permute-start(f32[24,8,128]{2,1,0:T(8,128)S(1)} %pad_maximum_fusion), channel_id=1, source_target_pairs={{0,8},{8,16},{16,24},{24,32},{32,40},{40,48},{48,56},{56,64},{64,7... | collective-permute-start | bytes 294920 | tf_op jit(solution)/shard_map/ppermute | solution.py:679
  64.6 5.5 %collective-permute-start.3 = (f32[24,8,128]{2,1,0:T(8,128)S(1)}, f32[24,8,128]{2,1,0:T(8,128)S(1)}, u32[]{:S(2)}, u32[]{:S(2)}) collective-permute-start(f32[24,8,128]{2,1,0:T(8,128)S(1)} %pad_maximum_fusion.1), channel_id=1, source_target_pairs={{8,0},{16,8},{24,16},{32,24},{40,32},{48,40},{56,48},{64,56},{72,6... | collective-permute-start | bytes 294920 | tf_op jit(solution)/shard_map/ppermute | solution.py:680
  70.0 6.1 %shard_map.58.refs_3_ = f32[16,128,256]{2,1,0:T(8,128)} custom-call(s32[4]{0:T(128)S(1)} %add_convert_fusion.place_ref, f32[8,8,128]{2,1,0:T(8,128)S(1)} %collective-permute-done.before_ref, f32[8,8,128]{2,1,0:T(8,128)S(1)} %collective-permute-done.1.after_ref, f32[32,128,128]{2,1,0:T(8,128)S(1)} %get-tuple-element.20.refs_0_.refs_2_), custom_call_target="tpu_custom_call" | custom-call | flops 10000000000 | bytes 2162704 | tf_op jit(solution)/shard_map/pallas_call | solution.py:574
  76.1 0.0 collective-permute-done.2.refs_0_
  76.1 0.0 collective-permute-done.3.refs_1_
  76.1 6.2 %shard_map.59 = f32[16,128,256]{2,1,0:T(8,128)} custom-call(s32[4]{0:T(128)S(1)} %add_convert_fusion.place_ref, f32[8,8,128]{2,1,0:T(8,128)S(1)} %collective-permute-done.before_ref, f32[8,8,128]{2,1,0:T(8,128)S(1)} %collective-permute-done.1.after_ref, f32[24,8,128]{2,1,0:T(8,128)S(1)} %collective-permute-done.2.refs_0_, ...), custom_call_target="tpu_custom_call", output_to_operand_aliasing={{}: (6, {})} | custom-call | flops 10000000000 | bytes 4456464 | tf_op jit(solution)/shard_map/pallas_call | solution.py:574
  (6 shorter events, 0.0 us)
Async XLA Ops:
  0.0 19.5 %copy-start = (s32[16,16,16]{2,1,0:T(8,128)S(1)}, s32[16,16,16]{2,1,0:T(8,128)}, u32[]{:S(2)}) copy-start(s32[16,16,16]{2,1,0:T(8,128)} %param.9) | copy-start | bytes 49156
  8.7 20.8 %all-to-all-start = ((bf16[128,8,128]{2,1,0:T(8,128)(2,1)}), bf16[128,8,128]{2,1,0:T(8,128)(2,1)S(1)}, u32[]{:S(2)}, u32[]{:S(2)}) async-start(bf16[128,8,128]{2,1,0:T(8,128)(2,1)} %bitcast.15), calls=%async_computation | async-start | bytes 524288 | tf_op jit(solution)/shard_map/all_to_all | solution.py:626
  29.5 19.1 %copy-start.1 = (f32[32,128,128]{2,1,0:T(8,128)S(1)}, f32[32,128,128]{2,1,0:T(8,128)}, u32[]{:S(2)}) copy-start(f32[32,128,128]{2,1,0:T(8,128)} %get-tuple-element.15.image_ref) | copy-start | bytes 6291460
  34.1 14.5 %all-to-all-start.1 = ((bf16[128,4,128]{2,1,0:T(4,128)(2,1)}), bf16[128,4,128]{2,1,0:T(4,128)(2,1)S(1)}, u32[]{:S(2)}, u32[]{:S(2)}) async-start(bf16[128,4,128]{2,1,0:T(4,128)(2,1)} %bitcast.10), calls=%async_computation.1 | async-start | bytes 262144 | tf_op jit(solution)/shard_map/all_to_all | solution.py:648
  54.6 4.5 %collective-permute-start = (f32[8,8,128]{2,1,0:T(8,128)S(1)}, f32[8,8,128]{2,1,0:T(8,128)S(1)}, u32[]{:S(2)}, u32[]{:S(2)}) collective-permute-start(f32[8,8,128]{2,1,0:T(8,128)S(1)} %get-tuple-element.16), channel_id=1, source_target_pairs={{0,1},{1,2},{2,3},{3,4},{4,5},{5,6},{6,7},{8,9},{9,10},{10,11},{11... | collective-permute-start | bytes 98312 | tf_op jit(solution)/shard_map/ppermute | solution.py:675
  57.2 5.2 %collective-permute-start.1 = (f32[8,8,128]{2,1,0:T(8,128)S(1)}, f32[8,8,128]{2,1,0:T(8,128)S(1)}, u32[]{:S(2)}, u32[]{:S(2)}) collective-permute-start(f32[8,8,128]{2,1,0:T(8,128)S(1)} %get-tuple-element.17), channel_id=1, source_target_pairs={{1,0},{2,1},{3,2},{4,3},{5,4},{6,5},{7,6},{9,8},{10,9},{11,10},{12... | collective-permute-start | bytes 98312 | tf_op jit(solution)/shard_map/ppermute | solution.py:676
  62.4 13.7 %collective-permute-start.2 = (f32[24,8,128]{2,1,0:T(8,128)S(1)}, f32[24,8,128]{2,1,0:T(8,128)S(1)}, u32[]{:S(2)}, u32[]{:S(2)}) collective-permute-start(f32[24,8,128]{2,1,0:T(8,128)S(1)} %pad_maximum_fusion), channel_id=1, source_target_pairs={{0,8},{8,16},{16,24},{24,32},{32,40},{40,48},{48,56},{56,64},{64,7... | collective-permute-start | bytes 294920 | tf_op jit(solution)/shard_map/ppermute | solution.py:679
  64.6 11.5 %collective-permute-start.3 = (f32[24,8,128]{2,1,0:T(8,128)S(1)}, f32[24,8,128]{2,1,0:T(8,128)S(1)}, u32[]{:S(2)}, u32[]{:S(2)}) collective-permute-start(f32[24,8,128]{2,1,0:T(8,128)S(1)} %pad_maximum_fusion.1), channel_id=1, source_target_pairs={{8,0},{16,8},{24,16},{32,24},{40,32},{48,40},{56,48},{64,56},{72,6... | collective-permute-start | bytes 294920 | tf_op jit(solution)/shard_map/ppermute | solution.py:680
